TPU v7x, 128 devices: a whole 4x4x4 slice. The times are simulated.
128 devices in a mesh: fact: 8 (over x, core), dim: 16 (over z, y).
Axes of the slice: x: 4, y: 4, z: 4, core: 2. Of those that a mesh axis runs over, the one named last changes fastest.
Arguments:
- queries: bfloat16 [32768, 1024], P(('fact', 'dim')), may hold values from -6 to 6
- key_rows: bfloat16 [16384, 1024], P('dim'), may hold values from -6 to 6
- value_rows: bfloat16 [16384, 1024], P('dim'), may hold values from -6 to 6
- cotangent: bfloat16 [32768, 1024], P(('fact', 'dim')), may hold values from -6 to 6
- block_lists: int32 [256, 8], P(('fact', 'dim')), may hold values from 0 to 127, as said below
- tile_lengths: int32 [256], P(('fact', 'dim')), may hold values from 1 to 8, as said below
Outputs:
- attended: bfloat16 [32768, 1024], P(('fact', 'dim'))
- query_grad: bfloat16 [32768, 1024], P(('fact', 'dim'))
- key_grad: bfloat16 [16384, 1024], P('dim', 'fact')
- value_grad: bfloat16 [16384, 1024], P('dim', 'fact')
Inputs may be any that keep to these rules, and one draw needn't show every extreme that they name: Rows of block_lists come in aligned groups of 2 rows. The entries of one row lie in different ranges [o * 8, (o + 1) * 8). Within one group, all entries that lie in one such range are the same block. Within each aligned run of 16 groups, the first entries of all rows lie in one common range. Only the first tile_lengths[t] entries of row t of block_lists are used.
All inputs are finite; a program needn't handle non-finite values.
Results may differ from a plain program's by a relative error of at most 0.0056.
Values may be sent and summed in bfloat16 or wider, within the bound.
A program may use at most 192 MiB of HBM per device.

v0:
```python
import jax
import jax.numpy as jnp
from jax import lax
from jax.sharding import PartitionSpec as P

HEADS = 16
HEAD_DIM = 64
TILE = 128


NEG_FILL = -1e30


def attend_group(query_group, grad_group, key_group, value_group, alive_keys):
    scale = HEAD_DIM ** (-0.5)
    scores = (
        jnp.einsum("tqhe,tkhe->thqk", query_group, key_group, preferred_element_type=jnp.float32)
        * scale
    )
    scores = jnp.where(alive_keys[:, None, None, :], scores, NEG_FILL)
    row_max = jnp.max(scores, axis=-1, keepdims=True)
    expo_terms = jnp.exp(scores - row_max)
    weights = expo_terms / jnp.sum(expo_terms, axis=-1, keepdims=True)
    weights_low = weights.astype(jnp.bfloat16)
    attended = jnp.einsum(
        "thqk,tkhe->tqhe", weights_low, value_group, preferred_element_type=jnp.float32
    )
    dweights = jnp.einsum(
        "tqhe,tkhe->thqk", grad_group, value_group, preferred_element_type=jnp.float32
    )
    row_delta = jnp.sum(weights * dweights, axis=-1, keepdims=True)
    dscores = (weights * (dweights - row_delta)).astype(jnp.bfloat16)
    query_grad = (
        jnp.einsum("thqk,tkhe->tqhe", dscores, key_group, preferred_element_type=jnp.float32)
        * scale
    )
    key_grad = (
        jnp.einsum("thqk,tqhe->tkhe", dscores, query_group, preferred_element_type=jnp.float32)
        * scale
    )
    value_grad = jnp.einsum(
        "thqk,tqhe->tkhe", weights_low, grad_group, preferred_element_type=jnp.float32
    )
    return (attended, query_grad, key_grad, value_grad)


def body(queries, key_rows, value_rows, cotangent, block_lists, tile_lengths):
    owners = lax.axis_size("dim")
    tile_count = block_lists.shape[0]
    slot_count = block_lists.shape[1]
    blocks_here = key_rows.shape[0] // TILE
    model_width = key_rows.shape[1]
    head_size = HEAD_DIM
    half_heads = HEADS // 2
    alive_slots = jnp.arange(slot_count, dtype=jnp.int32)[None, :] < tile_lengths[:, None]
    owner_of = block_lists // blocks_here
    local_of = block_lists % blocks_here
    owner_ids = jnp.arange(owners, dtype=jnp.int32)
    matched = (owner_of[:, :, None] == owner_ids[None, None, :]) & alive_slots[:, :, None]
    wanted = jnp.max(jnp.where(matched, local_of[:, :, None], -1), axis=(0, 1))
    requests = lax.all_to_all(
        wanted.reshape(owners, 1), "dim", split_axis=0, concat_axis=0, tiled=True
    )
    block_ids = jnp.arange(blocks_here, dtype=jnp.int32)[None, :]
    slot_selector = (requests == block_ids).astype(jnp.bfloat16)
    gathered_key_blocks = key_rows.reshape(blocks_here, TILE, model_width)
    gathered_value_blocks = value_rows.reshape(blocks_here, TILE, model_width)
    reply_keys = jnp.einsum(
        "nh,hcm->ncm", slot_selector, gathered_key_blocks, preferred_element_type=jnp.float32
    ).astype(jnp.bfloat16)
    reply_values = jnp.einsum(
        "nh,hcm->ncm", slot_selector, gathered_value_blocks, preferred_element_type=jnp.float32
    ).astype(jnp.bfloat16)
    fetched_keys, fetched_values = (
        lax.all_to_all(reply_keys, "dim", split_axis=0, concat_axis=0, tiled=True),
        lax.all_to_all(reply_values, "dim", split_axis=0, concat_axis=0, tiled=True),
    )
    per_step = min(4, tile_count)
    step_count = tile_count // per_step
    query_steps = queries.reshape(step_count, per_step, TILE, model_width)
    grad_steps = cotangent.reshape(step_count, per_step, TILE, model_width)
    owner_steps = owner_of.reshape(step_count, per_step, slot_count)
    alive_steps = alive_slots.reshape(step_count, per_step, slot_count)
    match_steps = matched.astype(jnp.float32).reshape(step_count, per_step, slot_count, owners)
    span = half_heads * head_size

    def one_group(totals, inputs_step):
        key_total, value_total = totals
        query_block, grad_block, owner_step, alive_step, match_step = inputs_step
        key_group = fetched_keys[owner_step]
        value_group = fetched_values[owner_step]
        alive_keys = jnp.repeat(alive_step, TILE, axis=1)
        attended_parts = []
        query_parts = []
        key_parts = []
        value_parts = []
        for portion in range(2):
            start = portion * span
            query_half = query_block[..., start : start + span].reshape(
                per_step, TILE, half_heads, head_size
            )
            grad_half = grad_block[..., start : start + span].reshape(
                per_step, TILE, half_heads, head_size
            )
            key_half = key_group[..., start : start + span].reshape(
                per_step, slot_count * TILE, half_heads, head_size
            )
            value_half = value_group[..., start : start + span].reshape(
                per_step, slot_count * TILE, half_heads, head_size
            )
            attended, query_grad, key_grad, value_grad = attend_group(
                query_half, grad_half, key_half, value_half, alive_keys
            )
            attended_parts.append(attended.reshape(per_step, TILE, span))
            query_parts.append(query_grad.reshape(per_step, TILE, span))
            key_parts.append(key_grad.reshape(per_step, slot_count, TILE, span))
            value_parts.append(value_grad.reshape(per_step, slot_count, TILE, span))
        key_full = jnp.concatenate(key_parts, axis=-1)
        value_full = jnp.concatenate(value_parts, axis=-1)
        key_total = key_total + jnp.einsum(
            "tjo,tjkd->okd", match_step, key_full, precision=lax.Precision.HIGHEST
        )
        value_total = value_total + jnp.einsum(
            "tjo,tjkd->okd", match_step, value_full, precision=lax.Precision.HIGHEST
        )
        attended_block = jnp.concatenate(attended_parts, axis=-1).astype(jnp.bfloat16)
        query_block_grad = jnp.concatenate(query_parts, axis=-1).astype(jnp.bfloat16)
        return ((key_total, value_total), (attended_block, query_block_grad))

    empty_total = jnp.zeros((owners, TILE, model_width), jnp.float32)
    (partial_keys, partial_values), (attended_all, query_grad_all) = lax.scan(
        one_group,
        (empty_total, empty_total),
        (query_steps, grad_steps, owner_steps, alive_steps, match_steps),
    )
    attended_out = attended_all.reshape(tile_count * TILE, model_width)
    query_grad_out = query_grad_all.reshape(tile_count * TILE, model_width)
    incoming_key_rows, incoming_value_rows = (
        lax.all_to_all(partial_keys, "dim", split_axis=0, concat_axis=0, tiled=True),
        lax.all_to_all(partial_values, "dim", split_axis=0, concat_axis=0, tiled=True),
    )
    block_selector = (requests == block_ids).astype(jnp.float32)
    reduced_key_grad = jnp.einsum(
        "ep,ejs->pjs", block_selector, incoming_key_rows, precision=lax.Precision.HIGHEST
    )
    summed_values = jnp.einsum(
        "ep,ejs->pjs", block_selector, incoming_value_rows, precision=lax.Precision.HIGHEST
    )
    key_grad_out, value_grad_out = (
        lax.psum_scatter(
            reduced_key_grad.reshape(blocks_here * TILE, model_width),
            "fact",
            scatter_dimension=1,
            tiled=True,
        ),
        lax.psum_scatter(
            summed_values.reshape(blocks_here * TILE, model_width),
            "fact",
            scatter_dimension=1,
            tiled=True,
        ),
    )
    return (
        attended_out,
        query_grad_out,
        key_grad_out.astype(jnp.bfloat16),
        value_grad_out.astype(jnp.bfloat16),
    )


def solution(mesh):
    in_specs = (
        P(("fact", "dim"), None),
        P("dim", None),
        P("dim", None),
        P(("fact", "dim"), None),
        P(("fact", "dim"), None),
        P(("fact", "dim")),
    )
    out_specs = (
        P(("fact", "dim"), None),
        P(("fact", "dim"), None),
        P("dim", "fact"),
        P("dim", "fact"),
    )
    return jax.shard_map(body, mesh=mesh, in_specs=in_specs, out_specs=out_specs, check_vma=False)
```

profile of v0, /device:TPU:32, one launch (start us, length us, event | category | flops | bytes accessed | tf_op | source)
XLA Modules:
  0.0 493.7 jit_solution(815351899450858913)
XLA Ops:
  8.9 14.0 %all_to_all.29 = s32[16,1,1]{2,1,0:T(1,128)S(1)} all-to-all(s32[16,1,1]{2,1,0:T(1,128)S(1)} %copy.93), channel_id=1, replica_groups=mesh['fact'=8,'dim'=16] {'dim'}, dimensions={0} | all-to-all | bytes 128 | tf_op jit(solution)/shard_map/all_to_all | solution.py:61
  29.3 5.9 %all-to-all-start.2 = ((bf16[16,128,1024]{2,1,0:T(8,128)(2,1)}), bf16[16,128,1024]{2,1,0:T(8,128)(2,1)}, u32[]{:S(2)}, u32[]{:S(2)}) async-start(bf16[16,128,1024]{2,1,0:T(8,128)(2,1)} %copy.98), calls=%async_computation.2 | async-start | bytes 8388608 | tf_op jit(solution)/shard_map/all_to_all | solution.py:75
  43.2 51.1 %all-to-all-done.2 = bf16[16,128,1024]{2,1,0:T(8,128)(2,1)} async-done(((bf16[16,128,1024]{2,1,0:T(8,128)(2,1)}), bf16[16,128,1024]{2,1,0:T(8,128)(2,1)}, u32[]{:S(2)}, u32[]{:S(2)}) %all-to-all-start.2) | async-done | bytes 4194336 | tf_op jit(solution)/shard_map/all_to_all | solution.py:75
  94.3 5.9 %all-to-all-start.1 = ((bf16[16,128,1024]{2,1,0:T(8,128)(2,1)}), bf16[16,128,1024]{2,1,0:T(8,128)(2,1)}, u32[]{:S(2)}, u32[]{:S(2)}) async-start(bf16[16,128,1024]{2,1,0:T(8,128)(2,1)} %copy.95), calls=%async_computation.1 | async-start | bytes 8388608 | tf_op jit(solution)/shard_map/all_to_all | solution.py:76
  123.6 8.1 %fusion.97 = (f32[2,8,128]{2,1,0:T(8,128)S(1)}, f32[2,8,128,1024]{2,3,1,0:T(8,128)}) fusion(pred[2,1024]{1,0:T(4,128)(4,1)S(1)} %bitcast.206, bf16[2,1024,8,64]{1,3,2,0:T(8,128)(2,1)} %reshape.149, bf16[2,128,8,64]{1,3,2,0:T(8,128)(2,1)S(1)} %bitcast.194), kind=kOutput, calls=%fused_computation.114 | convolution fusion | flops 276825088 | bytes 10758144 | tf_op jit(solution)/shard_map/while/body/eval_jaxpr/sub | solution.py:22
  139.7 5.6 %copy.124 = f32[2,8,128,512]{3,1,0,2:T(8,128)} copy(f32[2,8,128,512]{2,1,3,0:T(8,128)} %bitcast.183) | data formatting | bytes 8388608 | tf_op jit(solution)/shard_map/while/body/eval_jaxpr/reshape | solution.py:117
  145.3 5.6 %fusion.98 = (f32[2,8,128]{2,1,0:T(8,128)S(1)}, f32[2,8,128,1024]{2,3,1,0:T(8,128)}) fusion(pred[2,1024]{1,0:T(4,128)(4,1)S(1)} %bitcast.207, bf16[2,1024,8,64]{1,3,2,0:T(8,128)(2,1)S(1)} %reshape.146, bf16[2,128,8,64]{1,3,2,0:T(8,128)(2,1)S(1)} %bitcast.192), kind=kOutput, calls=%fused_computation.115 | convolution fusion | flops 276825088 | bytes 10758144 | tf_op jit(solution)/shard_map/while/body/eval_jaxpr/sub | solution.py:22
  158.8 5.6 %copy.123 = f32[2,8,128,512]{3,1,0,2:T(8,128)} copy(f32[2,8,128,512]{2,1,3,0:T(8,128)} %bitcast.184) | data formatting | bytes 8388608 | tf_op jit(solution)/shard_map/while/body/eval_jaxpr/reshape | solution.py:117
  164.4 7.5 %fusion.34 = f32[16,128,1024]{2,0,1:T(8,128)S(1)} fusion(f32[2,8,128,512]{3,1,0,2:T(8,128)} %copy.124, f32[2,8,128,512]{3,1,0,2:T(8,128)} %copy.123, s32[2,8]{1,0:T(2,128)S(1)} %get-tuple-element.53, pred[2,8]{1,0:T(4,128)(4,1)S(1)} %iota_compare_fusion.2), kind=kOutput, calls=%fused_computation.44 | convolution fusion | flops 404750848 | bytes 16777296 | tf_op jit(solution)/shard_map/while/body/eval_jaxpr/tjo,tjkd->okd/dot_general | solution.py:123
  171.8 8.1 %copy.125 = f32[16,128,1024]{2,1,0:T(8,128)} copy(f32[16,128,1024]{2,0,1:T(8,128)S(1)} %fusion.34) | data formatting | bytes 16777216 | tf_op jit(solution)/shard_map/while/body/eval_jaxpr/tjo,tjkd->okd/dot_general | solution.py:123
  179.9 7.6 %all-to-all-start.4 = ((f32[16,128,1024]{2,1,0:T(8,128)}), f32[16,128,1024]{2,1,0:T(8,128)}, u32[]{:S(2)}, u32[]{:S(2)}) async-start(f32[16,128,1024]{2,1,0:T(8,128)} %copy.125), calls=%async_computation.5 | async-start | bytes 16777216 | tf_op jit(solution)/shard_map/all_to_all | solution.py:140
  208.1 5.9 %fusion.10 = (f32[2,8,128]{2,1,0:T(8,128)S(1)}, f32[2,8,1024,128]{3,2,1,0:T(8,128)S(1)}) fusion(f32[2,8,128,1024]{2,3,1,0:T(8,128)} %get-tuple-element.64, f32[2,8,128]{2,1,0:T(8,128)S(1)} %get-tuple-element.63, bf16[2,1024,8,64]{1,3,2,0:T(8,128)(2,1)} %reshape.148, bf16[2,128,8,64]{1,3,2,0:T(8,128)(2,1)S(1)} %bitcast.205), kind=kOutput, calls=%fused_computation.14 | convolution fusion | flops 274724864 | bytes 19152896 | tf_op jit(solution)/shard_map/while/body/eval_jaxpr/tqhe,tkhe->thqk/dot_general | solution.py:28
  223.0 5.8 %copy.117 = f32[2,8,128,512]{3,1,0,2:T(8,128)} copy(f32[2,8,128,512]{2,1,3,0:T(8,128)} %bitcast.186) | data formatting | bytes 8388608 | tf_op jit(solution)/shard_map/while/body/eval_jaxpr/reshape | solution.py:116
  228.8 5.3 %fusion.13 = (f32[2,8,128]{2,1,0:T(8,128)S(1)}, f32[2,8,1024,128]{3,2,1,0:T(8,128)S(1)}) fusion(f32[2,8,128,1024]{2,3,1,0:T(8,128)} %get-tuple-element.66, f32[2,8,128]{2,1,0:T(8,128)S(1)} %get-tuple-element.65, bf16[2,1024,8,64]{1,3,2,0:T(8,128)(2,1)S(1)} %copy-done.8, bf16[2,128,8,64]{1,3,2,0:T(8,128)(2,1)S(1)} %bitcast.203), kind=kOutput, calls=%fused_computation.19 | convolution fusion | flops 274724864 | bytes 19152896 | tf_op jit(solution)/shard_map/while/body/eval_jaxpr/tqhe,tkhe->thqk/dot_general | solution.py:28
  243.1 5.6 %copy.116 = f32[2,8,128,512]{3,1,0,2:T(8,128)} copy(f32[2,8,128,512]{2,1,3,0:T(8,128)} %bitcast.188) | data formatting | bytes 8388608 | tf_op jit(solution)/shard_map/while/body/eval_jaxpr/reshape | solution.py:116
  248.7 7.2 %fusion.37 = f32[16,128,1024]{2,0,1:T(8,128)S(1)} fusion(f32[2,8,128,512]{3,1,0,2:T(8,128)} %copy.117, f32[2,8,128,512]{3,1,0,2:T(8,128)} %copy.116, s32[2,8]{1,0:T(2,128)S(1)} %get-tuple-element.53, pred[2,8]{1,0:T(4,128)(4,1)S(1)} %iota_compare_fusion.2), kind=kOutput, calls=%fused_computation.45 | convolution fusion | flops 404750848 | bytes 16777296 | tf_op jit(solution)/shard_map/while/body/eval_jaxpr/tjo,tjkd->okd/dot_general | solution.py:120
  255.9 8.1 %copy.118 = f32[16,128,1024]{2,1,0:T(8,128)} copy(f32[16,128,1024]{2,0,1:T(8,128)S(1)} %fusion.37) | data formatting | bytes 16777216 | tf_op jit(solution)/shard_map/while/body/eval_jaxpr/tjo,tjkd->okd/dot_general | solution.py:120
  264.0 41.6 %all-to-all-done.4 = f32[16,128,1024]{2,1,0:T(8,128)} async-done(((f32[16,128,1024]{2,1,0:T(8,128)}), f32[16,128,1024]{2,1,0:T(8,128)}, u32[]{:S(2)}, u32[]{:S(2)}) %all-to-all-start.4) | async-done | bytes 8388640 | tf_op jit(solution)/shard_map/all_to_all | solution.py:140
  305.5 6.3 %all-to-all-start.3 = ((f32[16,128,1024]{2,1,0:T(8,128)}), f32[16,128,1024]{2,1,0:T(8,128)}, u32[]{:S(2)}, u32[]{:S(2)}) async-start(f32[16,128,1024]{2,1,0:T(8,128)} %copy.118), calls=%async_computation.3 | async-start | bytes 16777216 | tf_op jit(solution)/shard_map/all_to_all | solution.py:139
  311.8 14.2 %fusion.20 = f32[8,128,1024]{2,0,1:T(8,128)S(1)} fusion(f32[16,128,1024]{2,1,0:T(8,128)} %all-to-all-done.4, s32[16]{0:T(128)S(1)} %reduce), kind=kOutput, calls=%fused_computation.30 | convolution fusion | flops 201326720 | bytes 12582976 | tf_op jit(solution)/shard_map/ep,ejs->pjs/dot_general | solution.py:146
  330.5 98.4 %all-to-all-done.3 = f32[16,128,1024]{2,1,0:T(8,128)} async-done(((f32[16,128,1024]{2,1,0:T(8,128)}), f32[16,128,1024]{2,1,0:T(8,128)}, u32[]{:S(2)}, u32[]{:S(2)}) %all-to-all-start.3) | async-done | bytes 8388640 | tf_op jit(solution)/shard_map/all_to_all | solution.py:139
  428.8 14.5 %fusion.22 = f32[8,128,1024]{2,0,1:T(8,128)S(1)} fusion(f32[16,128,1024]{2,1,0:T(8,128)} %all-to-all-done.3, s32[16]{0:T(128)S(1)} %reduce), kind=kOutput, calls=%fused_computation.32 | convolution fusion | flops 201326720 | bytes 12582976 | tf_op jit(solution)/shard_map/ep,ejs->pjs/dot_general | solution.py:143
  447.8 5.0 %fusion.58 = bf16[2,128,8,64]{1,3,2,0:T(8,128)(2,1)S(1)} fusion(bf16[2,1024,8,64]{1,3,2,0:T(8,128)(2,1)} %reshape.148, f32[2,8,128,1024]{2,3,1,0:T(8,128)} %get-tuple-element.64, f32[2,8,128]{2,1,0:T(8,128)S(1)} %get-tuple-element.63), kind=kOutput, calls=%fused_computation.66 | convolution fusion | flops 272760832 | bytes 10756096 | tf_op jit(solution)/shard_map/while/body/eval_jaxpr/thqk,tkhe->tqhe/dot_general | solution.py:25
  468.0 16.9 %reduce-scatter.3.cloned.1.call-done = f32[1024,128]{1,0:T(8,128)} async-done(((f32[1024,1024]{1,0:T(8,128)}), f32[1024,128]{1,0:T(8,128)}) %reduce-scatter.3.cloned.1.call-update) | async-done | bytes 524304 | tf_op jit(solution)/shard_map/reduce_scatter | solution.py:150
  (86 shorter events, 119.4 us)
Async XLA Ops:
  7.2 16.2 %copy-start = (bf16[1024,1024]{1,0:T(8,128)(2,1)S(1)}, bf16[1024,1024]{1,0:T(8,128)(2,1)}, u32[]{:S(2)}) copy-start(bf16[1024,1024]{1,0:T(8,128)(2,1)} %param.7) | copy-start | bytes 6291460
  29.3 6.1 %copy-start.10 = (bf16[256,1024]{1,0:T(8,128)(2,1)S(1)}, bf16[256,1024]{1,0:T(8,128)(2,1)}, u32[]{:S(2)}) copy-start(bf16[256,1024]{1,0:T(8,128)(2,1)} %param.6) | copy-start | bytes 1572868
  29.3 65.0 %all-to-all-start.2 = ((bf16[16,128,1024]{2,1,0:T(8,128)(2,1)}), bf16[16,128,1024]{2,1,0:T(8,128)(2,1)}, u32[]{:S(2)}, u32[]{:S(2)}) async-start(bf16[16,128,1024]{2,1,0:T(8,128)(2,1)} %copy.98), calls=%async_computation.2 | async-start | bytes 8388608 | tf_op jit(solution)/shard_map/all_to_all | solution.py:75
  35.2 2.1 copy-start.7
  94.3 85.7 %all-to-all-start.1 = ((bf16[16,128,1024]{2,1,0:T(8,128)(2,1)}), bf16[16,128,1024]{2,1,0:T(8,128)(2,1)}, u32[]{:S(2)}, u32[]{:S(2)}) async-start(bf16[16,128,1024]{2,1,0:T(8,128)(2,1)} %copy.95), calls=%async_computation.1 | async-start | bytes 8388608 | tf_op jit(solution)/shard_map/all_to_all | solution.py:76
  114.6 30.7 %copy-start.5 = (bf16[2,1024,8,64]{1,3,2,0:T(8,128)(2,1)}, bf16[2,1024,8,64]{1,3,2,0:T(8,128)(2,1)S(1)}, u32[]{:S(2)}) copy-start(bf16[2,1024,8,64]{1,3,2,0:T(8,128)(2,1)S(1)} %reshape.146) | copy-start | bytes 6291460
  179.9 125.6 %all-to-all-start.4 = ((f32[16,128,1024]{2,1,0:T(8,128)}), f32[16,128,1024]{2,1,0:T(8,128)}, u32[]{:S(2)}, u32[]{:S(2)}) async-start(f32[16,128,1024]{2,1,0:T(8,128)} %copy.125), calls=%async_computation.5 | async-start | bytes 16777216 | tf_op jit(solution)/shard_map/all_to_all | solution.py:140
  218.1 1.9 copy-start.3
  223.0 5.8 %copy-start.8 = (bf16[2,1024,8,64]{1,3,2,0:T(8,128)(2,1)S(1)}, bf16[2,1024,8,64]{1,3,2,0:T(8,128)(2,1)}, u32[]{:S(2)}) copy-start(bf16[2,1024,8,64]{1,3,2,0:T(8,128)(2,1)} %reshape.144) | copy-start | bytes 6291460
  238.2 1.9 copy-start.2
  305.5 123.3 %all-to-all-start.3 = ((f32[16,128,1024]{2,1,0:T(8,128)}), f32[16,128,1024]{2,1,0:T(8,128)}, u32[]{:S(2)}, u32[]{:S(2)}) async-start(f32[16,128,1024]{2,1,0:T(8,128)} %copy.118), calls=%async_computation.3 | async-start | bytes 16777216 | tf_op jit(solution)/shard_map/all_to_all | solution.py:139
  311.8 154.5 %reduce-scatter.5.cloned.1.call-start = ((), (), s32[]{:S(2)}) async-start(), calls=%async_computation.8 | async-start | bytes 4718592 | tf_op jit(solution)/shard_map/reduce_scatter | solution.py:156
  330.4 154.5 %reduce-scatter.3.cloned.1.call-start = ((), (), s32[]{:S(2)}) async-start(), calls=%async_computation.7 | async-start | bytes 4718592 | tf_op jit(solution)/shard_map/reduce_scatter | solution.py:150
  447.8 5.3 %copy-start.4 = (bf16[2,8,128,1024]{2,3,1,0:T(8,128)(2,1)S(1)}, bf16[2,8,128,1024]{2,3,1,0:T(8,128)(2,1)}, u32[]{:S(2)}) copy-start(bf16[2,8,128,1024]{2,3,1,0:T(8,128)(2,1)} %copy-done.3) | copy-start | bytes 12582916
  447.8 5.9 %copy-start.6 = (bf16[2,1024,8,64]{1,3,2,0:T(8,128)(2,1)S(1)}, bf16[2,1024,8,64]{1,3,2,0:T(8,128)(2,1)}, u32[]{:S(2)}) copy-start(bf16[2,1024,8,64]{1,3,2,0:T(8,128)(2,1)} %reshape.149) | copy-start | bytes 6291460
  452.9 2.0 copy-start.9
  460.9 25.8 %copy-start.1 = (bf16[1024,1024]{1,0:T(8,128)(2,1)S(1)}, bf16[1024,1024]{1,0:T(8,128)(2,1)}, u32[]{:S(2)}) copy-start(bf16[1024,1024]{1,0:T(8,128)(2,1)} %param.7) | copy-start | bytes 6291460
Sparse Core Ops, SparseCore 0:
  330.5 40.1 reduce-scatter.4
  447.9 36.9 reduce-scatter.2
where the time goes:
time: 502 us; the launch traced here: 494 us
  waiting for transfers between devices  208 us (41%)
  local copies, waits for them, and re-layouts  118 us (24%)
  matrix products  99.1 us (20%)
  starting transfers between devices  25.7 us (5%)
  between operations  14.6 us (3%)
  blocking collectives  14 us (3%)
  other arithmetic  13.8 us (3%)
    all_to_all x1, waiting for transfers between devices, body(): lax.all_to_all(partial_keys, 'dim', split_axis=0, concat_axis=0, tiled=True)  98.4 us
    all_to_all x1, waiting for transfers between devices, body(): lax.all_to_all(reply_keys, 'dim', split_axis=0, concat_axis=0, tiled=True)  51.1 us
    all_to_all x1, waiting for transfers between devices, body(): lax.all_to_all(partial_values, 'dim', split_axis=0, concat_axis=0, tiled=...  41.6 us
    unnamed x38, local copies, waits for them, and re-layouts  29.6 us
    reduce_scatter x1, waiting for transfers between devices, body(): lax.psum_scatter(reduced_key_grad.reshape(blocks_here * TILE, model_width...  16.9 us
    dot_general x1, matrix products, body(): jnp.einsum('ep,ejs->pjs', block_selector, incoming_key_rows, precision=la...  14.5 us
    dot_general x1, matrix products, body(): jnp.einsum('ep,ejs->pjs', block_selector, incoming_value_rows, precision=...  14.2 us
    all_to_all x1, blocking collectives, body(): lax.all_to_all(wanted.reshape(owners, 1), 'dim', split_axis=0, concat_axi...  14 us
  transfers between devices with their start and end apart: 6, of which 4 were waited for; matrix products, arithmetic and copies ran while one was open for 45% of the time, Pallas kernels for 0%

commit v1 on v0

--- a/solution.py
+++ b/solution.py
@@ -136,9 +136,11 @@
     attended_out = attended_all.reshape(tile_count * TILE, model_width)
     query_grad_out = query_grad_all.reshape(tile_count * TILE, model_width)
     incoming_key_rows, incoming_value_rows = (
-        lax.all_to_all(partial_keys, "dim", split_axis=0, concat_axis=0, tiled=True),
-        lax.all_to_all(partial_values, "dim", split_axis=0, concat_axis=0, tiled=True),
+        lax.all_to_all(partial_keys.astype(jnp.bfloat16), "dim", split_axis=0, concat_axis=0, tiled=True),
+        lax.all_to_all(partial_values.astype(jnp.bfloat16), "dim", split_axis=0, concat_axis=0, tiled=True),
     )
+    incoming_key_rows = incoming_key_rows.astype(jnp.float32)
+    incoming_value_rows = incoming_value_rows.astype(jnp.float32)
     block_selector = (requests == block_ids).astype(jnp.float32)
     reduced_key_grad = jnp.einsum(
         "ep,ejs->pjs", block_selector, incoming_key_rows, precision=lax.Precision.HIGHEST

time: 502 us -> 417 us (0.83)
  waiting for transfers between devices: 208 us -> 99.4 us
  blocking collectives: 14 us -> 66.9 us
  matrix products: 99.1 us -> 82 us
  local copies, waits for them, and re-layouts: 118 us -> 108 us
  starting transfers between devices: 25.7 us -> 19 us
    all_to_all x2 -> x1, waiting for transfers between devices: 140 us -> 30.9 us  [body(): lax.all_to_all(partial_values.astype(jnp.bfloat16), 'dim', split_axis=0,...]
    all_to_all x0 -> x1, blocking collectives: none -> 52.8 us  [body(): lax.all_to_all(partial_keys.astype(jnp.bfloat16), 'dim', split_axis=0, co...]
    dot_general x2 -> x0, local copies, waits for them, and re-layouts: 16.2 us -> none  [the longest x1 8.08 us: one_group(): jnp.einsum('tjo,tjkd->okd', match_step, value_full, precision=lax.Precisi...]
    dot_general x1, matrix products: 14.5 us -> 2.42 us  [body(): jnp.einsum('ep,ejs->pjs', block_selector, incoming_key_rows, precision=la...]
    dot_general x1, matrix products: 14.2 us -> 4.6 us  [body(): jnp.einsum('ep,ejs->pjs', block_selector, incoming_value_rows, precision=...]
    convert_element_type x0 -> x2, local copies, waits for them, and re-layouts: none -> 6.6 us  [the longest x1 4.28 us: body(): partial_values.astype(jnp.bfloat16)]
    all_to_all x2 -> x1, starting transfers between devices: 13.8 us -> 7.26 us  [body(): lax.all_to_all(partial_values.astype(jnp.bfloat16), 'dim', split_axis=0,...]
    unnamed x38 -> x36, local copies, waits for them, and re-layouts: 29.6 us -> 29.2 us
  transfers between devices with their start and end apart: 6 -> 5, of which waited for: 4 -> 3; matrix products, arithmetic and copies ran while one was open for 45% -> 46% of each run, Pallas kernels for 0% -> 0%
where the time goes in v1:
time: 417 us; the launch traced here: 409 us
  local copies, waits for them, and re-layouts  108 us (26%)
  waiting for transfers between devices  99.4 us (24%)
  matrix products  82 us (20%)
  blocking collectives  66.9 us (16%)
  starting transfers between devices  19 us (5%)
  other arithmetic  18.5 us (4%)
  between operations  14.6 us (4%)
    all_to_all x1, blocking collectives, body(): lax.all_to_all(partial_keys.astype(jnp.bfloat16), 'dim', split_axis=0, co...  52.8 us
    all_to_all x1, waiting for transfers between devices, body(): lax.all_to_all(reply_keys, 'dim', split_axis=0, concat_axis=0, tiled=True)  51.1 us
    all_to_all x1, waiting for transfers between devices, body(): lax.all_to_all(partial_values.astype(jnp.bfloat16), 'dim', split_axis=0,...  30.9 us
    unnamed x36, local copies, waits for them, and re-layouts  29.2 us
    reduce_scatter x1, waiting for transfers between devices, body(): lax.psum_scatter(reduced_key_grad.reshape(blocks_here * TILE, model_width...  17.5 us
    dot_general x2, matrix products, attend_group(): jnp.einsum('tqhe,tkhe->thqk', grad_group, value_group, preferred_element_...  14.4 us
    all_to_all x1, blocking collectives, body(): lax.all_to_all(wanted.reshape(owners, 1), 'dim', split_axis=0, concat_axi...  14 us
    sub x2, matrix products, attend_group(): expo_terms = jnp.exp(scores - row_max)  13.7 us
  transfers between devices with their start and end apart: 5, of which 3 were waited for; matrix products, arithmetic and copies ran while one was open for 46% of the time, Pallas kernels for 0%

profile of v1, /device:TPU:32, one launch (start us, length us, event | category | flops | bytes accessed | tf_op | source)
XLA Modules:
  0.0 408.9 jit_solution(6419694125128672954)
XLA Ops:
  8.9 14.0 %all_to_all.29 = s32[16,1,1]{2,1,0:T(1,128)S(1)} all-to-all(s32[16,1,1]{2,1,0:T(1,128)S(1)} %copy.93), channel_id=1, replica_groups=mesh['fact'=8,'dim'=16] {'dim'}, dimensions={0} | all-to-all | bytes 128 | tf_op jit(solution)/shard_map/all_to_all | solution.py:61
  29.3 5.9 %all-to-all-start.2 = ((bf16[16,128,1024]{2,1,0:T(8,128)(2,1)}), bf16[16,128,1024]{2,1,0:T(8,128)(2,1)}, u32[]{:S(2)}, u32[]{:S(2)}) async-start(bf16[16,128,1024]{2,1,0:T(8,128)(2,1)} %copy.98), calls=%async_computation.2 | async-start | bytes 8388608 | tf_op jit(solution)/shard_map/all_to_all | solution.py:75
  43.2 51.1 %all-to-all-done.2 = bf16[16,128,1024]{2,1,0:T(8,128)(2,1)} async-done(((bf16[16,128,1024]{2,1,0:T(8,128)(2,1)}), bf16[16,128,1024]{2,1,0:T(8,128)(2,1)}, u32[]{:S(2)}, u32[]{:S(2)}) %all-to-all-start.2) | async-done | bytes 4194336 | tf_op jit(solution)/shard_map/all_to_all | solution.py:75
  94.3 5.8 %all-to-all-start.1 = ((bf16[16,128,1024]{2,1,0:T(8,128)(2,1)}), bf16[16,128,1024]{2,1,0:T(8,128)(2,1)}, u32[]{:S(2)}, u32[]{:S(2)}) async-start(bf16[16,128,1024]{2,1,0:T(8,128)(2,1)} %copy.95), calls=%async_computation.1 | async-start | bytes 8388608 | tf_op jit(solution)/shard_map/all_to_all | solution.py:76
  100.1 5.0 %gather_fusion.1 = bf16[16,128,1024]{2,1,0:T(8,128)(2,1)} fusion(bf16[16,128,1024]{2,1,0:T(8,128)(2,1)} %all-to-all-done.2, s32[1024]{0:T(1024)S(1)} %pad_clamp_fusion), kind=kCustom, calls=%fused_computation.1 | custom fusion | bytes 8388672 | tf_op jit(solution)/shard_map/while/body/eval_jaxpr/gather | solution.py:90
  123.3 8.1 %fusion.95 = (f32[2,8,128]{2,1,0:T(8,128)S(1)}, f32[2,8,128,1024]{2,3,1,0:T(8,128)}) fusion(pred[2,1024]{1,0:T(4,128)(4,1)S(1)} %bitcast.206, bf16[2,1024,8,64]{1,3,2,0:T(8,128)(2,1)} %reshape.149, bf16[2,128,8,64]{1,3,2,0:T(8,128)(2,1)S(1)} %bitcast.194), kind=kOutput, calls=%fused_computation.114 | convolution fusion | flops 276825088 | bytes 10758144 | tf_op jit(solution)/shard_map/while/body/eval_jaxpr/sub | solution.py:22
  131.5 5.0 %fusion.40 = f32[2,8,1024,64]{2,3,1,0:T(8,128)S(1)} fusion(bf16[2,128,8,64]{1,3,2,0:T(8,128)(2,1)S(1)} %bitcast.204, f32[2,8,128,1024]{2,3,1,0:T(8,128)} %get-tuple-element.64, f32[2,8,128]{2,1,0:T(8,128)S(1)} %get-tuple-element.63), kind=kOutput, calls=%fused_computation.52 | convolution fusion | flops 272629760 | bytes 12853248 | tf_op jit(solution)/shard_map/while/body/eval_jaxpr/thqk,tqhe->tkhe/dot_general | solution.py:41
  139.4 5.6 %copy.124 = f32[2,8,128,512]{3,1,0,2:T(8,128)} copy(f32[2,8,128,512]{2,1,3,0:T(8,128)} %bitcast.183) | data formatting | bytes 8388608 | tf_op jit(solution)/shard_map/while/body/eval_jaxpr/reshape | solution.py:117
  145.0 5.6 %fusion.96 = (f32[2,8,128]{2,1,0:T(8,128)S(1)}, f32[2,8,128,1024]{2,3,1,0:T(8,128)}) fusion(pred[2,1024]{1,0:T(4,128)(4,1)S(1)} %bitcast.207, bf16[2,1024,8,64]{1,3,2,0:T(8,128)(2,1)S(1)} %reshape.146, bf16[2,128,8,64]{1,3,2,0:T(8,128)(2,1)S(1)} %bitcast.192), kind=kOutput, calls=%fused_computation.115 | convolution fusion | flops 276825088 | bytes 10758144 | tf_op jit(solution)/shard_map/while/body/eval_jaxpr/sub | solution.py:22
  150.5 5.0 %fusion.44 = f32[2,8,1024,64]{2,3,1,0:T(8,128)S(1)} fusion(bf16[2,128,8,64]{1,3,2,0:T(8,128)(2,1)S(1)} %bitcast.202, f32[2,8,128,1024]{2,3,1,0:T(8,128)} %get-tuple-element.66, f32[2,8,128]{2,1,0:T(8,128)S(1)} %get-tuple-element.65), kind=kOutput, calls=%fused_computation.56 | convolution fusion | flops 272629760 | bytes 12853248 | tf_op jit(solution)/shard_map/while/body/eval_jaxpr/thqk,tqhe->tkhe/dot_general | solution.py:41
  158.6 5.6 %copy.123 = f32[2,8,128,512]{3,1,0,2:T(8,128)} copy(f32[2,8,128,512]{2,1,3,0:T(8,128)} %bitcast.184) | data formatting | bytes 8388608 | tf_op jit(solution)/shard_map/while/body/eval_jaxpr/reshape | solution.py:117
  164.2 7.1 %bitcast_convert_fusion = bf16[16,128,1024]{2,0,1:T(8,128)(2,1)S(1)} fusion(f32[2,8,128,512]{3,1,0,2:T(8,128)} %copy.124, f32[2,8,128,512]{3,1,0,2:T(8,128)} %copy.123, s32[2,8]{1,0:T(2,128)S(1)} %get-tuple-element.53, pred[2,8]{1,0:T(4,128)(4,1)S(1)} %iota_compare_fusion.2), kind=kOutput, calls=%fused_computation.12 | convolution fusion | flops 406848000 | bytes 12582992 | tf_op jit(solution)/shard_map/while/body/eval_jaxpr/tjo,tjkd->okd/dot_general | solution.py:123
  175.5 7.3 %all-to-all-start.4 = ((bf16[16,128,1024]{2,1,0:T(8,128)(2,1)}), bf16[16,128,1024]{2,1,0:T(8,128)(2,1)}, u32[]{:S(2)}, u32[]{:S(2)}) async-start(bf16[16,128,1024]{2,1,0:T(8,128)(2,1)} %copy.125), calls=%async_computation.5 | async-start | bytes 8388608 | tf_op jit(solution)/shard_map/all_to_all | solution.py:140
  182.8 5.0 %gather_fusion = bf16[16,128,1024]{2,1,0:T(8,128)(2,1)} fusion(bf16[16,128,1024]{2,1,0:T(8,128)(2,1)} %all-to-all-done.1, s32[1024]{0:T(1024)S(1)} %pad_clamp_fusion), kind=kCustom, calls=%fused_computation | custom fusion | bytes 8388672 | tf_op jit(solution)/shard_map/while/body/eval_jaxpr/gather | solution.py:91
  197.9 8.9 %fusion.10 = (f32[2,8,128]{2,1,0:T(8,128)S(1)}, f32[2,8,1024,128]{3,2,1,0:T(8,128)}) fusion(f32[2,8,128,1024]{2,3,1,0:T(8,128)} %get-tuple-element.64, f32[2,8,128]{2,1,0:T(8,128)S(1)} %get-tuple-element.63, bf16[2,1024,8,64]{1,3,2,0:T(8,128)(2,1)} %reshape.148, bf16[2,128,8,64]{1,3,2,0:T(8,128)(2,1)S(1)} %bitcast.205), kind=kOutput, calls=%fused_computation.16 | convolution fusion | flops 274724864 | bytes 19152896 | tf_op jit(solution)/shard_map/while/body/eval_jaxpr/tqhe,tkhe->thqk/dot_general | solution.py:28
  206.8 30.9 %all-to-all-done.4 = bf16[16,128,1024]{2,1,0:T(8,128)(2,1)} async-done(((bf16[16,128,1024]{2,1,0:T(8,128)(2,1)}), bf16[16,128,1024]{2,1,0:T(8,128)(2,1)}, u32[]{:S(2)}, u32[]{:S(2)}) %all-to-all-start.4) | async-done | bytes 4194336 | tf_op jit(solution)/shard_map/all_to_all | solution.py:140
  246.7 8.7 %fusion.12 = bf16[2,8,128,1024]{2,3,1,0:T(8,128)(2,1)} fusion(f32[2,8,1024,128]{3,2,1,0:T(8,128)} %get-tuple-element.68, f32[2,8,128]{2,1,0:T(8,128)S(1)} %get-tuple-element.67, f32[2,8,128,1024]{2,3,1,0:T(8,128)} %get-tuple-element.64, f32[2,8,128]{2,1,0:T(8,128)S(1)} %get-tuple-element.63), kind=kLoop, calls=%fused_computation.18 | loop fusion | flops 8388608 | bytes 20987904 | tf_op jit(solution)/shard_map/while/body/eval_jaxpr/convert_element_type | solution.py:32
  267.7 5.8 %copy.117 = f32[2,8,128,512]{3,1,0,2:T(8,128)} copy(f32[2,8,128,512]{2,1,3,0:T(8,128)} %bitcast.186) | data formatting | bytes 8388608 | tf_op jit(solution)/shard_map/while/body/eval_jaxpr/reshape | solution.py:116
  273.5 5.5 %fusion.13 = (f32[2,8,128]{2,1,0:T(8,128)S(1)}, f32[2,8,1024,128]{3,2,1,0:T(8,128)S(1)}) fusion(f32[2,8,128,1024]{2,3,1,0:T(8,128)} %get-tuple-element.66, f32[2,8,128]{2,1,0:T(8,128)S(1)} %get-tuple-element.65, bf16[2,1024,8,64]{1,3,2,0:T(8,128)(2,1)S(1)} %copy-done.7, bf16[2,128,8,64]{1,3,2,0:T(8,128)(2,1)S(1)} %bitcast.203), kind=kOutput, calls=%fused_computation.21 | convolution fusion | flops 274724864 | bytes 19152896 | tf_op jit(solution)/shard_map/while/body/eval_jaxpr/tqhe,tkhe->thqk/dot_general | solution.py:28
  288.1 5.6 %copy.116 = f32[2,8,128,512]{3,1,0,2:T(8,128)} copy(f32[2,8,128,512]{2,1,3,0:T(8,128)} %bitcast.188) | data formatting | bytes 8388608 | tf_op jit(solution)/shard_map/while/body/eval_jaxpr/reshape | solution.py:116
  293.7 6.7 %bitcast_convert_fusion.1 = bf16[16,128,1024]{2,0,1:T(8,128)(2,1)S(1)} fusion(f32[2,8,128,512]{3,1,0,2:T(8,128)} %copy.117, f32[2,8,128,512]{3,1,0,2:T(8,128)} %copy.116, s32[2,8]{1,0:T(2,128)S(1)} %get-tuple-element.53, pred[2,8]{1,0:T(4,128)(4,1)S(1)} %iota_compare_fusion.2), kind=kOutput, calls=%fused_computation.13 | convolution fusion | flops 406848000 | bytes 12582992 | tf_op jit(solution)/shard_map/while/body/eval_jaxpr/tjo,tjkd->okd/dot_general | solution.py:120
  302.7 52.8 %all_to_all.30 = bf16[16,128,1024]{2,1,0:T(8,128)(2,1)S(1)} all-to-all(bf16[16,128,1024]{2,1,0:T(8,128)(2,1)S(1)} %copy.118), channel_id=1, replica_groups=mesh['fact'=8,'dim'=16] {'dim'}, dimensions={0} | all-to-all | bytes 8388608 | tf_op jit(solution)/shard_map/all_to_all | solution.py:139
  362.4 5.0 %fusion.56 = bf16[2,128,8,64]{1,3,2,0:T(8,128)(2,1)S(1)} fusion(bf16[2,1024,8,64]{1,3,2,0:T(8,128)(2,1)} %reshape.148, f32[2,8,128,1024]{2,3,1,0:T(8,128)} %get-tuple-element.64, f32[2,8,128]{2,1,0:T(8,128)S(1)} %get-tuple-element.63), kind=kOutput, calls=%fused_computation.66 | convolution fusion | flops 272760832 | bytes 10756096 | tf_op jit(solution)/shard_map/while/body/eval_jaxpr/thqk,tkhe->tqhe/dot_general | solution.py:25
  382.6 17.5 %reduce-scatter.3.cloned.1.call-done = f32[1024,128]{1,0:T(8,128)} async-done(((f32[1024,1024]{1,0:T(8,128)}), f32[1024,128]{1,0:T(8,128)}) %reduce-scatter.3.cloned.1.call-update) | async-done | bytes 524304 | tf_op jit(solution)/shard_map/reduce_scatter | solution.py:152
  (83 shorter events, 111.0 us)
Async XLA Ops:
  7.2 16.2 %copy-start = (bf16[1024,1024]{1,0:T(8,128)(2,1)S(1)}, bf16[1024,1024]{1,0:T(8,128)(2,1)}, u32[]{:S(2)}) copy-start(bf16[1024,1024]{1,0:T(8,128)(2,1)} %param.7) | copy-start | bytes 6291460
  29.3 6.0 %copy-start.9 = (bf16[256,1024]{1,0:T(8,128)(2,1)S(1)}, bf16[256,1024]{1,0:T(8,128)(2,1)}, u32[]{:S(2)}) copy-start(bf16[256,1024]{1,0:T(8,128)(2,1)} %param.6) | copy-start | bytes 1572868
  29.3 65.0 %all-to-all-start.2 = ((bf16[16,128,1024]{2,1,0:T(8,128)(2,1)}), bf16[16,128,1024]{2,1,0:T(8,128)(2,1)}, u32[]{:S(2)}, u32[]{:S(2)}) async-start(bf16[16,128,1024]{2,1,0:T(8,128)(2,1)} %copy.98), calls=%async_computation.2 | async-start | bytes 8388608 | tf_op jit(solution)/shard_map/all_to_all | solution.py:75
  35.2 2.1 copy-start.6
  94.3 81.3 %all-to-all-start.1 = ((bf16[16,128,1024]{2,1,0:T(8,128)(2,1)}), bf16[16,128,1024]{2,1,0:T(8,128)(2,1)}, u32[]{:S(2)}, u32[]{:S(2)}) async-start(bf16[16,128,1024]{2,1,0:T(8,128)(2,1)} %copy.95), calls=%async_computation.1 | async-start | bytes 8388608 | tf_op jit(solution)/shard_map/all_to_all | solution.py:76
  114.5 30.5 %copy-start.4 = (bf16[2,1024,8,64]{1,3,2,0:T(8,128)(2,1)}, bf16[2,1024,8,64]{1,3,2,0:T(8,128)(2,1)S(1)}, u32[]{:S(2)}) copy-start(bf16[2,1024,8,64]{1,3,2,0:T(8,128)(2,1)S(1)} %reshape.146) | copy-start | bytes 6291460
  175.5 62.1 %all-to-all-start.4 = ((bf16[16,128,1024]{2,1,0:T(8,128)(2,1)}), bf16[16,128,1024]{2,1,0:T(8,128)(2,1)}, u32[]{:S(2)}, u32[]{:S(2)}) async-start(bf16[16,128,1024]{2,1,0:T(8,128)(2,1)} %copy.125), calls=%async_computation.5 | async-start | bytes 8388608 | tf_op jit(solution)/shard_map/all_to_all | solution.py:140
  182.8 198.0 %reduce-scatter.5.cloned.1.call-start = ((), (), s32[]{:S(2)}) async-start(), calls=%async_computation.8 | async-start | bytes 4718592 | tf_op jit(solution)/shard_map/reduce_scatter | solution.py:158
  246.7 153.4 %reduce-scatter.3.cloned.1.call-start = ((), (), s32[]{:S(2)}) async-start(), calls=%async_computation.7 | async-start | bytes 4718592 | tf_op jit(solution)/shard_map/reduce_scatter | solution.py:152
  267.7 5.8 %copy-start.7 = (bf16[2,1024,8,64]{1,3,2,0:T(8,128)(2,1)S(1)}, bf16[2,1024,8,64]{1,3,2,0:T(8,128)(2,1)}, u32[]{:S(2)}) copy-start(bf16[2,1024,8,64]{1,3,2,0:T(8,128)(2,1)} %reshape.144) | copy-start | bytes 6291460
  283.2 1.9 copy-start.2
  362.4 5.3 %copy-start.3 = (bf16[2,8,128,1024]{2,3,1,0:T(8,128)(2,1)S(1)}, bf16[2,8,128,1024]{2,3,1,0:T(8,128)(2,1)}, u32[]{:S(2)}) copy-start(bf16[2,8,128,1024]{2,3,1,0:T(8,128)(2,1)} %fusion.12) | copy-start | bytes 12582916
  362.4 5.9 %copy-start.5 = (bf16[2,1024,8,64]{1,3,2,0:T(8,128)(2,1)S(1)}, bf16[2,1024,8,64]{1,3,2,0:T(8,128)(2,1)}, u32[]{:S(2)}) copy-start(bf16[2,1024,8,64]{1,3,2,0:T(8,128)(2,1)} %reshape.149) | copy-start | bytes 6291460
  367.4 2.0 copy-start.8
  375.5 26.4 %copy-start.1 = (bf16[1024,1024]{1,0:T(8,128)(2,1)S(1)}, bf16[1024,1024]{1,0:T(8,128)(2,1)}, u32[]{:S(2)}) copy-start(bf16[1024,1024]{1,0:T(8,128)(2,1)} %param.7) | copy-start | bytes 6291460
Sparse Core Ops, SparseCore 0:
  246.8 36.2 reduce-scatter.4
  362.5 37.5 reduce-scatter.2

commit v2 on v1

v2 whole, which is shorter than its diff:
```python
import functools
import jax
import jax.numpy as jnp
from jax import lax
from jax.experimental import pallas as pl
from jax.experimental.pallas import tpu as pltpu
from jax.sharding import PartitionSpec as P

HEADS = 16
HEAD_DIM = 64
TILE = 128
NEG_FILL = -1e30
PAIR = 2 * HEAD_DIM


def _nt(a, b):
    return lax.dot_general(a, b, (((1,), (1,)), ((), ())), preferred_element_type=jnp.float32)


def _tn(a, b):
    return lax.dot_general(a, b, (((0,), (0,)), ((), ())), preferred_element_type=jnp.float32)


def _nn(a, b):
    return jnp.dot(a, b, preferred_element_type=jnp.float32)


def attention_kernel(owner_ref, length_ref, q_ref, g_ref, k_ref, v_ref,
                     att_ref, qg_ref, dk_ref, dv_ref, kbuf, vbuf):
    tiles = q_ref.shape[0] // TILE
    slots = kbuf.shape[0] // TILE
    scale = HEAD_DIM ** (-0.5)
    dk_ref[...] = jnp.zeros_like(dk_ref)
    dv_ref[...] = jnp.zeros_like(dv_ref)
    lane = lax.broadcasted_iota(jnp.int32, (1, PAIR), 1)
    first = lane < HEAD_DIM
    key_pos = lax.broadcasted_iota(jnp.int32, (1, slots * TILE), 1)
    for t in range(tiles):
        rows = pl.ds(t * TILE, TILE)
        for j in range(slots):
            owner = owner_ref[t, j]
            kbuf[pl.ds(j * TILE, TILE), :] = k_ref[owner]
            vbuf[pl.ds(j * TILE, TILE), :] = v_ref[owner]
        q = q_ref[rows, :]
        g = g_ref[rows, :]
        keys = kbuf[...]
        values = vbuf[...]
        alive = key_pos < length_ref[t] * TILE
        outs = []
        for h in range(2):
            mine = first if h == 0 else jnp.logical_not(first)
            qh = jnp.where(mine, q, jnp.zeros_like(q))
            gh = jnp.where(mine, g, jnp.zeros_like(g))
            scores = _nt(qh, keys) * scale
            scores = jnp.where(alive, scores, NEG_FILL)
            row_max = jnp.max(scores, axis=-1, keepdims=True)
            expo = jnp.exp(scores - row_max)
            weights = expo / jnp.sum(expo, axis=-1, keepdims=True)
            weights_low = weights.astype(jnp.bfloat16)
            attended = _nn(weights_low, values)
            dweights = _nt(gh, values)
            row_delta = jnp.sum(weights * dweights, axis=-1, keepdims=True)
            dscores = (weights * (dweights - row_delta)).astype(jnp.bfloat16)
            query_grad = _nn(dscores, keys)
            key_grad = _tn(dscores, q)
            value_grad = _tn(weights_low, g)
            outs.append((attended, query_grad, key_grad, value_grad))
        pick = lambda i: jnp.where(first, outs[0][i], outs[1][i])
        att_ref[rows, :] = pick(0).astype(att_ref.dtype)
        qg_ref[rows, :] = (pick(1) * scale).astype(qg_ref.dtype)
        key_grad = pick(2) * scale
        value_grad = pick(3)
        for j in range(slots):
            owner = owner_ref[t, j]
            dk_ref[owner] = dk_ref[owner] + key_grad[j * TILE:(j + 1) * TILE]
            dv_ref[owner] = dv_ref[owner] + value_grad[j * TILE:(j + 1) * TILE]


def attend_local(owner_of, tile_lengths, queries, cotangent, fetched_keys, fetched_values):
    owners, _, width = fetched_keys.shape
    rows = queries.shape[0]
    slots = owner_of.shape[1]
    pairs = width // PAIR
    col = lambda hp, own, ln: (0, hp)
    blk = lambda hp, own, ln: (0, 0, hp)
    grid_spec = pltpu.PrefetchScalarGridSpec(
        num_scalar_prefetch=2,
        grid=(pairs,),
        in_specs=[
            pl.BlockSpec((rows, PAIR), col),
            pl.BlockSpec((rows, PAIR), col),
            pl.BlockSpec((owners, TILE, PAIR), blk),
            pl.BlockSpec((owners, TILE, PAIR), blk),
        ],
        out_specs=[
            pl.BlockSpec((rows, PAIR), col),
            pl.BlockSpec((rows, PAIR), col),
            pl.BlockSpec((owners, TILE, PAIR), blk),
            pl.BlockSpec((owners, TILE, PAIR), blk),
        ],
        scratch_shapes=[
            pltpu.VMEM((slots * TILE, PAIR), jnp.bfloat16),
            pltpu.VMEM((slots * TILE, PAIR), jnp.bfloat16),
        ],
    )
    return pl.pallas_call(
        attention_kernel,
        grid_spec=grid_spec,
        out_shape=[
            jax.ShapeDtypeStruct((rows, width), jnp.bfloat16),
            jax.ShapeDtypeStruct((rows, width), jnp.bfloat16),
            jax.ShapeDtypeStruct((owners, TILE, width), jnp.float32),
            jax.ShapeDtypeStruct((owners, TILE, width), jnp.float32),
        ],
        compiler_params=pltpu.CompilerParams(dimension_semantics=("arbitrary",)),
    )(owner_of, tile_lengths, queries, cotangent, fetched_keys, fetched_values)


def body(queries, key_rows, value_rows, cotangent, block_lists, tile_lengths):
    owners = lax.axis_size("dim")
    tile_count = block_lists.shape[0]
    slot_count = block_lists.shape[1]
    blocks_here = key_rows.shape[0] // TILE
    model_width = key_rows.shape[1]
    alive_slots = jnp.arange(slot_count, dtype=jnp.int32)[None, :] < tile_lengths[:, None]
    owner_of = block_lists // blocks_here
    local_of = block_lists % blocks_here
    owner_ids = jnp.arange(owners, dtype=jnp.int32)
    matched = (owner_of[:, :, None] == owner_ids[None, None, :]) & alive_slots[:, :, None]
    wanted = jnp.max(jnp.where(matched, local_of[:, :, None], -1), axis=(0, 1))
    requests = lax.all_to_all(
        wanted.reshape(owners, 1), "dim", split_axis=0, concat_axis=0, tiled=True
    )
    block_ids = jnp.arange(blocks_here, dtype=jnp.int32)[None, :]
    slot_selector = (requests == block_ids).astype(jnp.bfloat16)
    gathered_key_blocks = key_rows.reshape(blocks_here, TILE, model_width)
    gathered_value_blocks = value_rows.reshape(blocks_here, TILE, model_width)
    reply_keys = jnp.einsum(
        "nh,hcm->ncm", slot_selector, gathered_key_blocks, preferred_element_type=jnp.float32
    ).astype(jnp.bfloat16)
    reply_values = jnp.einsum(
        "nh,hcm->ncm", slot_selector, gathered_value_blocks, preferred_element_type=jnp.float32
    ).astype(jnp.bfloat16)
    fetched_keys, fetched_values = (
        lax.all_to_all(reply_keys, "dim", split_axis=0, concat_axis=0, tiled=True),
        lax.all_to_all(reply_values, "dim", split_axis=0, concat_axis=0, tiled=True),
    )
    attended_out, query_grad_out, partial_keys, partial_values = attend_local(
        owner_of, tile_lengths, queries, cotangent, fetched_keys, fetched_values
    )
    incoming_key_rows, incoming_value_rows = (
        lax.all_to_all(partial_keys.astype(jnp.bfloat16), "dim", split_axis=0, concat_axis=0, tiled=True),
        lax.all_to_all(partial_values.astype(jnp.bfloat16), "dim", split_axis=0, concat_axis=0, tiled=True),
    )
    incoming_key_rows = incoming_key_rows.astype(jnp.float32)
    incoming_value_rows = incoming_value_rows.astype(jnp.float32)
    block_selector = (requests == block_ids).astype(jnp.float32)
    reduced_key_grad = jnp.einsum(
        "ep,ejs->pjs", block_selector, incoming_key_rows, precision=lax.Precision.HIGHEST
    )
    summed_values = jnp.einsum(
        "ep,ejs->pjs", block_selector, incoming_value_rows, precision=lax.Precision.HIGHEST
    )
    key_grad_out, value_grad_out = (
        lax.psum_scatter(
            reduced_key_grad.reshape(blocks_here * TILE, model_width),
            "fact",
            scatter_dimension=1,
            tiled=True,
        ),
        lax.psum_scatter(
            summed_values.reshape(blocks_here * TILE, model_width),
            "fact",
            scatter_dimension=1,
            tiled=True,
        ),
    )
    return (
        attended_out,
        query_grad_out,
        key_grad_out.astype(jnp.bfloat16),
        value_grad_out.astype(jnp.bfloat16),
    )


def solution(mesh):
    in_specs = (
        P(("fact", "dim"), None),
        P("dim", None),
        P("dim", None),
        P(("fact", "dim"), None),
        P(("fact", "dim"), None),
        P(("fact", "dim")),
    )
    out_specs = (
        P(("fact", "dim"), None),
        P(("fact", "dim"), None),
        P("dim", "fact"),
        P("dim", "fact"),
    )
    return jax.shard_map(body, mesh=mesh, in_specs=in_specs, out_specs=out_specs, check_vma=False)
```

time: 417 us -> 353 us (0.85); the launches traced: 409 us -> 352 us
  blocking collectives: 66.9 us -> 168 us
  local copies, waits for them, and re-layouts: 108 us -> 17.4 us
  matrix products: 82 us -> 8.13 us
  Pallas kernels: 0 us -> 36 us
  starting transfers between devices: 19 us -> 5.95 us
  waiting for transfers between devices: 99.4 us -> 88.6 us
  other arithmetic: 18.5 us -> 13.7 us
    all_to_all x0 -> x2, blocking collectives: none -> 103 us  [the longest x1 52.4 us: body(): lax.all_to_all(reply_keys, 'dim', split_axis=0, concat_axis=0, tiled=True)]
    all_to_all x2 -> x0, waiting for transfers between devices: 81.9 us -> none  [the longest x1 51.1 us: body(): lax.all_to_all(reply_keys, 'dim', split_axis=0, concat_axis=0, tiled=True)]
    dot_general x12 -> x0, matrix products: 58 us -> none  [the longest x2 14.4 us: attend_group(): jnp.einsum('tqhe,tkhe->thqk', grad_group, value_group, preferred_element_...]
    all_to_all x1, waiting for transfers between devices: 0.01 us -> 53.1 us  [body(): lax.all_to_all(reply_values, 'dim', split_axis=0, concat_axis=0, tiled=True)]
    pallas_call x0 -> x1, Pallas kernels: none -> 36 us  [attend_local(): pl.pallas_call(attention_kernel, grid_spec=grid_spec, out_shape=[jax.Shap...]
    reduce_scatter x1, waiting for transfers between devices: 0.01 us -> 35.4 us  [body(): lax.psum_scatter(summed_values.reshape(blocks_here * TILE, model_width),...]
    reshape x8 -> x0, local copies, waits for them, and re-layouts: 34.2 us -> none  [the longest x2 11.4 us: one_group(): key_parts.append(key_grad.reshape(per_step, slot_count, TILE, span))]
    unnamed x36 -> x8, local copies, waits for them, and re-layouts: 29.2 us -> 0.02 us
  transfers between devices with their start and end apart: 5 -> 3, of which waited for: 3 -> 2; matrix products, arithmetic and copies ran while one was open for 46% -> 5% of each run, Pallas kernels for 0% -> 0%
where the time goes in v2:
time: 353 us; the launch traced here: 352 us
  blocking collectives  168 us (48%)
  waiting for transfers between devices  88.6 us (25%)
  Pallas kernels  36 us (10%)
  local copies, waits for them, and re-layouts  17.4 us (5%)
  between operations  14.1 us (4%)
  other arithmetic  13.7 us (4%)
  matrix products  8.13 us (2%)
  starting transfers between devices  5.95 us (2%)
    all_to_all x1, waiting for transfers between devices, body(): lax.all_to_all(reply_values, 'dim', split_axis=0, concat_axis=0, tiled=True)  53.1 us
    all_to_all x1, blocking collectives, body(): lax.all_to_all(reply_keys, 'dim', split_axis=0, concat_axis=0, tiled=True)  52.4 us
    all_to_all x1, blocking collectives, body(): lax.all_to_all(partial_keys.astype(jnp.bfloat16), 'dim', split_axis=0, co...  51.5 us
    all_to_all x1, blocking collectives, body(): lax.all_to_all(partial_values.astype(jnp.bfloat16), 'dim', split_axis=0,...  50.4 us
    pallas_call x1, Pallas kernels, attend_local(): pl.pallas_call(attention_kernel, grid_spec=grid_spec, out_shape=[jax.Shap...  36 us
    reduce_scatter x1, waiting for transfers between devices, body(): lax.psum_scatter(summed_values.reshape(blocks_here * TILE, model_width),...  35.4 us
    all_to_all x1, blocking collectives, body(): lax.all_to_all(wanted.reshape(owners, 1), 'dim', split_axis=0, concat_axi...  14 us
  transfers between devices with their start and end apart: 3, of which 2 were waited for; matrix products, arithmetic and copies ran while one was open for 5% of the time, Pallas kernels for 0%

profile of v2, /device:TPU:32, one launch (start us, length us, event | category | flops | bytes accessed | tf_op | source)
XLA Modules:
  0.0 352.2 jit_solution(2213395440130952776)
XLA Ops:
  7.2 0.9 iota_compare_fusion.2
  8.1 0.7 and_select_fusion
  8.8 0.1 select_reduce_fusion
  8.9 14.0 %all_to_all.29 = s32[16,1,1]{2,1,0:T(1,128)S(1)} all-to-all(s32[16,1,1]{2,1,0:T(1,128)S(1)} %copy.42), channel_id=1, replica_groups=mesh['fact'=8,'dim'=16] {'dim'}, dimensions={0} | all-to-all | bytes 128 | tf_op jit(solution)/shard_map/all_to_all | solution.py:131
  23.0 0.4 reduce
  23.4 1.6 fusion.4
  25.0 4.3 %copy.61 = bf16[16,128,1024]{2,1,0:T(8,128)(2,1)} copy(bf16[16,128,1024]{2,0,1:T(8,128)(2,1)S(1)} %fusion.4) | data formatting | bytes 8388608 | tf_op jit(solution)/shard_map/nh,hcm->ncm/dot_general | solution.py:141
  29.3 5.9 %all-to-all-start.2 = ((bf16[16,128,1024]{2,1,0:T(8,128)(2,1)}), bf16[16,128,1024]{2,1,0:T(8,128)(2,1)}, u32[]{:S(2)}, u32[]{:S(2)}) async-start(bf16[16,128,1024]{2,1,0:T(8,128)(2,1)} %copy.61), calls=%async_computation.2 | async-start | bytes 8388608 | tf_op jit(solution)/shard_map/all_to_all | solution.py:146
  35.2 1.6 fusion.6
  36.9 4.3 %copy.62 = bf16[16,128,1024]{2,1,0:T(8,128)(2,1)} copy(bf16[16,128,1024]{2,0,1:T(8,128)(2,1)S(1)} %fusion.6) | data formatting | bytes 8388608 | tf_op jit(solution)/shard_map/nh,hcm->ncm/dot_general | solution.py:138
  41.2 53.1 %all-to-all-done.2.v_ref = bf16[16,128,1024]{2,1,0:T(8,128)(2,1)} async-done(((bf16[16,128,1024]{2,1,0:T(8,128)(2,1)}), bf16[16,128,1024]{2,1,0:T(8,128)(2,1)}, u32[]{:S(2)}, u32[]{:S(2)}) %all-to-all-start.2) | async-done | bytes 4194336 | tf_op jit(solution)/shard_map/all_to_all | solution.py:146
  94.3 52.4 %all_to_all.30.k_ref = bf16[16,128,1024]{2,1,0:T(8,128)(2,1)} all-to-all(bf16[16,128,1024]{2,1,0:T(8,128)(2,1)} %copy.62), channel_id=1, replica_groups=mesh['fact'=8,'dim'=16] {'dim'}, dimensions={0} | all-to-all | bytes 8388608 | tf_op jit(solution)/shard_map/all_to_all | solution.py:145
  146.6 36.0 %shard_map.93 = (bf16[256,1024]{1,0:T(8,128)(2,1)}, bf16[256,1024]{1,0:T(8,128)(2,1)}, f32[16,128,1024]{2,1,0:T(8,128)}, f32[16,128,1024]{2,1,0:T(8,128)}) custom-call(s32[2,8]{1,0:T(2,128)} %copy-done.3, s32[2]{0:T(128)} %length_ref.1, bf16[256,1024]{1,0:T(8,128)(2,1)} %q_ref.1, bf16[256,1024]{1,0:T(8,128)(2,1)} %g_ref.1, ...), custom_call_target="tpu_custom_call" | custom-call | tf_op jit(solution)/shard_map/pallas_call | solution.py:106
  182.6 4.0 %convert_element_type.24 = bf16[16,128,1024]{2,1,0:T(8,128)(2,1)S(1)} convert(f32[16,128,1024]{2,1,0:T(8,128)} %get-tuple-element.10) | non-fusion elementwise | flops 2097152 | bytes 12582912 | tf_op jit(solution)/shard_map/convert_element_type | solution.py:152
  186.7 51.5 %all_to_all.31 = bf16[16,128,1024]{2,1,0:T(8,128)(2,1)S(1)} all-to-all(bf16[16,128,1024]{2,1,0:T(8,128)(2,1)S(1)} %convert_element_type.24), channel_id=1, replica_groups=mesh['fact'=8,'dim'=16] {'dim'}, dimensions={0} | all-to-all | bytes 8388608 | tf_op jit(solution)/shard_map/all_to_all | solution.py:152
  238.2 2.4 fusion.2
  240.6 4.4 %copy.48 = f32[8,128,1024]{2,1,0:T(8,128)} copy(f32[8,128,1024]{2,0,1:T(8,128)S(1)} %fusion.2) | data formatting | bytes 8388608 | tf_op jit(solution)/shard_map/ep,ejs->pjs/dot_general | solution.py:158
  245.0 4.0 %convert_element_type.26 = bf16[16,128,1024]{2,1,0:T(8,128)(2,1)S(1)} convert(f32[16,128,1024]{2,1,0:T(8,128)} %get-tuple-element.11) | non-fusion elementwise | flops 2097152 | bytes 12582912 | tf_op jit(solution)/shard_map/convert_element_type | solution.py:153
  249.1 50.4 %all_to_all.32 = bf16[16,128,1024]{2,1,0:T(8,128)(2,1)S(1)} all-to-all(bf16[16,128,1024]{2,1,0:T(8,128)(2,1)S(1)} %convert_element_type.26), channel_id=1, replica_groups=mesh['fact'=8,'dim'=16] {'dim'}, dimensions={0} | all-to-all | bytes 8388608 | tf_op jit(solution)/shard_map/all_to_all | solution.py:153
  299.5 2.4 fusion
  301.9 4.4 %copy.50 = f32[8,128,1024]{2,1,0:T(8,128)} copy(f32[8,128,1024]{2,0,1:T(8,128)S(1)} %fusion) | data formatting | bytes 8388608 | tf_op jit(solution)/shard_map/ep,ejs->pjs/dot_general | solution.py:161
  306.3 1.8 convert_element_type.25
  308.1 35.4 %reduce-scatter.5.cloned.1.call-done = f32[1024,128]{1,0:T(8,128)} async-done(((f32[1024,1024]{1,0:T(8,128)}), f32[1024,128]{1,0:T(8,128)}) %reduce-scatter.5.cloned.1.call-update) | async-done | bytes 524304 | tf_op jit(solution)/shard_map/reduce_scatter | solution.py:171
  343.5 1.8 convert_element_type.27
  (14 shorter events, 0.2 us)
Async XLA Ops:
  7.2 16.2 %copy-start = (bf16[1024,1024]{1,0:T(8,128)(2,1)S(1)}, bf16[1024,1024]{1,0:T(8,128)(2,1)}, u32[]{:S(2)}) copy-start(bf16[1024,1024]{1,0:T(8,128)(2,1)} %param.8) | copy-start | bytes 6291460
  8.7 20.6 %copy-start.3 = (s32[2,8]{1,0:T(2,128)}, s32[2,8]{1,0:T(2,128)S(1)}, u32[]{:S(2)}) copy-start(s32[2,8]{1,0:T(2,128)S(1)} %get-tuple-element.13.owner_ref) | copy-start | bytes 196
  29.3 5.9 %copy-start.2 = (bf16[1024,1024]{1,0:T(8,128)(2,1)S(1)}, bf16[1024,1024]{1,0:T(8,128)(2,1)}, u32[]{:S(2)}) copy-start(bf16[1024,1024]{1,0:T(8,128)(2,1)} %param.7) | copy-start | bytes 6291460
  29.3 65.0 %all-to-all-start.2 = ((bf16[16,128,1024]{2,1,0:T(8,128)(2,1)}), bf16[16,128,1024]{2,1,0:T(8,128)(2,1)}, u32[]{:S(2)}, u32[]{:S(2)}) async-start(bf16[16,128,1024]{2,1,0:T(8,128)(2,1)} %copy.61), calls=%async_computation.2 | async-start | bytes 8388608 | tf_op jit(solution)/shard_map/all_to_all | solution.py:146
  35.2 271.1 %reduce-scatter.3.cloned.1.call-start = ((), (), s32[]{:S(2)}) async-start(), calls=%async_computation.7 | async-start | bytes 4718592 | tf_op jit(solution)/shard_map/reduce_scatter | solution.py:165
  245.0 98.6 %reduce-scatter.5.cloned.1.call-start = ((), (), s32[]{:S(2)}) async-start(), calls=%async_computation.8 | async-start | bytes 4718592 | tf_op jit(solution)/shard_map/reduce_scatter | solution.py:171
  301.9 43.4 %copy-start.1 = (bf16[1024,1024]{1,0:T(8,128)(2,1)S(1)}, bf16[1024,1024]{1,0:T(8,128)(2,1)}, u32[]{:S(2)}) copy-start(bf16[1024,1024]{1,0:T(8,128)(2,1)} %param.8) | copy-start | bytes 6291460
Sparse Core Ops, SparseCore 0:
  245.1 37.7 reduce-scatter.2
  306.4 37.0 reduce-scatter.4

commit v3 on v2

--- a/solution.py
+++ b/solution.py
@@ -26,7 +26,7 @@
 
 
 def attention_kernel(owner_ref, length_ref, q_ref, g_ref, k_ref, v_ref,
-                     att_ref, qg_ref, dk_ref, dv_ref, kbuf, vbuf):
+                     att_ref, qg_ref, dk_out, dv_out, kbuf, vbuf, dk_ref, dv_ref):
     tiles = q_ref.shape[0] // TILE
     slots = kbuf.shape[0] // TILE
     scale = HEAD_DIM ** (-0.5)
@@ -74,6 +74,8 @@
             owner = owner_ref[t, j]
             dk_ref[owner] = dk_ref[owner] + key_grad[j * TILE:(j + 1) * TILE]
             dv_ref[owner] = dv_ref[owner] + value_grad[j * TILE:(j + 1) * TILE]
+    dk_out[0] = dk_ref[...].astype(dk_out.dtype)
+    dv_out[0] = dv_ref[...].astype(dv_out.dtype)
 
 
 def attend_local(owner_of, tile_lengths, queries, cotangent, fetched_keys, fetched_values):
@@ -95,12 +97,14 @@
         out_specs=[
             pl.BlockSpec((rows, PAIR), col),
             pl.BlockSpec((rows, PAIR), col),
-            pl.BlockSpec((owners, TILE, PAIR), blk),
-            pl.BlockSpec((owners, TILE, PAIR), blk),
+            pl.BlockSpec((1, owners, TILE, PAIR), lambda hp, own, ln: (hp, 0, 0, 0)),
+            pl.BlockSpec((1, owners, TILE, PAIR), lambda hp, own, ln: (hp, 0, 0, 0)),
         ],
         scratch_shapes=[
             pltpu.VMEM((slots * TILE, PAIR), jnp.bfloat16),
             pltpu.VMEM((slots * TILE, PAIR), jnp.bfloat16),
+            pltpu.VMEM((owners, TILE, PAIR), jnp.float32),
+            pltpu.VMEM((owners, TILE, PAIR), jnp.float32),
         ],
     )
     return pl.pallas_call(
@@ -109,8 +113,8 @@
         out_shape=[
             jax.ShapeDtypeStruct((rows, width), jnp.bfloat16),
             jax.ShapeDtypeStruct((rows, width), jnp.bfloat16),
-            jax.ShapeDtypeStruct((owners, TILE, width), jnp.float32),
-            jax.ShapeDtypeStruct((owners, TILE, width), jnp.float32),
+            jax.ShapeDtypeStruct((pairs, owners, TILE, PAIR), jnp.bfloat16),
+            jax.ShapeDtypeStruct((pairs, owners, TILE, PAIR), jnp.bfloat16),
         ],
         compiler_params=pltpu.CompilerParams(dimension_semantics=("arbitrary",)),
     )(owner_of, tile_lengths, queries, cotangent, fetched_keys, fetched_values)
@@ -148,33 +152,26 @@
     attended_out, query_grad_out, partial_keys, partial_values = attend_local(
         owner_of, tile_lengths, queries, cotangent, fetched_keys, fetched_values
     )
-    incoming_key_rows, incoming_value_rows = (
-        lax.all_to_all(partial_keys.astype(jnp.bfloat16), "dim", split_axis=0, concat_axis=0, tiled=True),
-        lax.all_to_all(partial_values.astype(jnp.bfloat16), "dim", split_axis=0, concat_axis=0, tiled=True),
+    fact_count = lax.axis_size("fact")
+    everyone = ("fact", "dim")
+    pieces_keys = lax.all_to_all(
+        partial_keys.reshape(fact_count * owners, TILE, model_width // fact_count),
+        everyone, split_axis=0, concat_axis=0, tiled=True,
     )
-    incoming_key_rows = incoming_key_rows.astype(jnp.float32)
-    incoming_value_rows = incoming_value_rows.astype(jnp.float32)
-    block_selector = (requests == block_ids).astype(jnp.float32)
-    reduced_key_grad = jnp.einsum(
-        "ep,ejs->pjs", block_selector, incoming_key_rows, precision=lax.Precision.HIGHEST
+    pieces_values = lax.all_to_all(
+        partial_values.reshape(fact_count * owners, TILE, model_width // fact_count),
+        everyone, split_axis=0, concat_axis=0, tiled=True,
     )
-    summed_values = jnp.einsum(
-        "ep,ejs->pjs", block_selector, incoming_value_rows, precision=lax.Precision.HIGHEST
-    )
-    key_grad_out, value_grad_out = (
-        lax.psum_scatter(
-            reduced_key_grad.reshape(blocks_here * TILE, model_width),
-            "fact",
-            scatter_dimension=1,
-            tiled=True,
-        ),
-        lax.psum_scatter(
-            summed_values.reshape(blocks_here * TILE, model_width),
-            "fact",
-            scatter_dimension=1,
-            tiled=True,
-        ),
-    )
+    all_requests = lax.all_gather(requests.reshape(owners), "fact", tiled=True)
+    block_selector = (all_requests[:, None] == block_ids).astype(jnp.float32)
+    key_grad_out = jnp.einsum(
+        "ep,ejs->pjs", block_selector, pieces_keys.astype(jnp.float32),
+        precision=lax.Precision.HIGHEST,
+    ).reshape(blocks_here * TILE, model_width // fact_count)
+    value_grad_out = jnp.einsum(
+        "ep,ejs->pjs", block_selector, pieces_values.astype(jnp.float32),
+        precision=lax.Precision.HIGHEST,
+    ).reshape(blocks_here * TILE, model_width // fact_count)
     return (
         attended_out,
         query_grad_out,

time: 353 us -> 304 us (0.86)
  waiting for transfers between devices: 88.6 us -> 51.7 us
  between operations: 14.1 us -> 1.35 us
  other arithmetic: 13.7 us -> 2.03 us
  blocking collectives: 168 us -> 175 us
  local copies, waits for them, and re-layouts: 17.4 us -> 11 us
  matrix products: 8.13 us -> 13.7 us
  starting transfers between devices: 5.95 us -> 11.2 us
    unnamed x0 -> x1, blocking collectives: none -> 49.2 us
    all_to_all x2 -> x1, blocking collectives: 102 us -> 59.6 us  [body(): lax.all_to_all(partial_keys.reshape(fact_count * owners, TILE, model_widt...]
    reduce_scatter x2 -> x0, waiting for transfers between devices: 35.5 us -> none  [the longest x1 35.4 us: body(): lax.psum_scatter(summed_values.reshape(blocks_here * TILE, model_width),...]
    convert_element_type x4 -> x0, other arithmetic: 11.6 us -> none  [the longest x1 4.04 us: body(): partial_values.astype(jnp.bfloat16)]
    dot_general x2 -> x0, local copies, waits for them, and re-layouts: 8.75 us -> none  [the longest x1 4.38 us: body(): jnp.einsum('ep,ejs->pjs', block_selector, incoming_key_rows, precision=la...]
    all_to_all x0 -> x1, starting transfers between devices: none -> 5.5 us  [body(): lax.all_to_all(partial_values.reshape(fact_count * owners, TILE, model_wi...]
    dot_general x2, matrix products: 4.83 us -> 8.97 us  [the longest x1 4.48 us: body(): jnp.einsum('ep,ejs->pjs', block_selector, pieces_values.astype(jnp.float3...]
  transfers between devices with their start and end apart: 3 -> 2, of which waited for: 2 -> 1; matrix products, arithmetic and copies ran while one was open for 5% -> 4% of each run, Pallas kernels for 0% -> 0%
where the time goes in v3:
time: 304 us; the launch traced here: 303 us
  blocking collectives  175 us (58%)
  waiting for transfers between devices  51.7 us (17%)
  Pallas kernels  36.3 us (12%)
  matrix products  13.7 us (5%)
  starting transfers between devices  11.2 us (4%)
  local copies, waits for them, and re-layouts  11 us (4%)
    all_to_all x1, blocking collectives, body(): lax.all_to_all(partial_keys.reshape(fact_count * owners, TILE, model_widt...  59.6 us
    all_to_all x1, blocking collectives, body(): lax.all_to_all(reply_keys, 'dim', split_axis=0, concat_axis=0, tiled=True)  52.4 us
    all_to_all x1, waiting for transfers between devices, body(): lax.all_to_all(reply_values, 'dim', split_axis=0, concat_axis=0, tiled=True)  51.7 us
    unnamed x1, blocking collectives  49.2 us
    pallas_call x1, Pallas kernels, attend_local(): pl.pallas_call(attention_kernel, grid_spec=grid_spec, out_shape=[jax.Shap...  36.3 us
    all_to_all x1, blocking collectives, body(): lax.all_to_all(wanted.reshape(owners, 1), 'dim', split_axis=0, concat_axi...  14 us
  transfers between devices with their start and end apart: 2, of which 1 were waited for; matrix products, arithmetic and copies ran while one was open for 4% of the time, Pallas kernels for 0%

profile of v3, /device:TPU:32, one launch (start us, length us, event | category | flops | bytes accessed | tf_op | source)
XLA Modules:
  0.0 302.5 jit_solution(11106658882643241100)
XLA Ops:
  0.6 0.0 copy-start
  0.6 0.9 iota_compare_fusion.3
  1.5 0.7 and_select_fusion
  2.2 0.1 select_reduce_fusion
  2.3 0.1 copy.42
  2.4 14.0 %all_to_all.29 = s32[16,1,1]{2,1,0:T(1,128)S(1)} all-to-all(s32[16,1,1]{2,1,0:T(1,128)S(1)} %copy.42), channel_id=1, replica_groups=mesh['fact'=8,'dim'=16] {'dim'}, dimensions={0} | all-to-all | bytes 128 | tf_op jit(solution)/shard_map/all_to_all | solution.py:135
  16.4 0.4 reduce
  16.8 1.6 fusion.4
  18.5 4.3 %copy.65 = bf16[16,128,1024]{2,1,0:T(8,128)(2,1)} copy(bf16[16,128,1024]{2,0,1:T(8,128)(2,1)S(1)} %fusion.4) | data formatting | bytes 8388608 | tf_op jit(solution)/shard_map/nh,hcm->ncm/dot_general | solution.py:145
  22.8 5.7 %all-to-all-start.2 = ((bf16[16,128,1024]{2,1,0:T(8,128)(2,1)}), bf16[16,128,1024]{2,1,0:T(8,128)(2,1)}, u32[]{:S(2)}, u32[]{:S(2)}) async-start(bf16[16,128,1024]{2,1,0:T(8,128)(2,1)} %copy.65), calls=%async_computation.2 | async-start | bytes 8388608 | tf_op jit(solution)/shard_map/all_to_all | solution.py:150
  28.5 3.1 %fusion.6 = bf16[16,128,1024]{2,0,1:T(8,128)(2,1)S(1)} fusion(bf16[8,128,1024]{2,1,0:T(8,128)(2,1)} %bitcast.19, s32[16]{0:T(128)S(1)} %reduce), kind=kOutput, calls=%fused_computation.8 | convolution fusion | flops 33554560 | bytes 6291520 | tf_op jit(solution)/shard_map/nh,hcm->ncm/dot_general | solution.py:142
  31.6 4.3 %copy.66 = bf16[16,128,1024]{2,1,0:T(8,128)(2,1)} copy(bf16[16,128,1024]{2,0,1:T(8,128)(2,1)S(1)} %fusion.6) | data formatting | bytes 8388608 | tf_op jit(solution)/shard_map/nh,hcm->ncm/dot_general | solution.py:142
  35.9 51.7 %all-to-all-done.2.v_ref = bf16[16,128,1024]{2,1,0:T(8,128)(2,1)} async-done(((bf16[16,128,1024]{2,1,0:T(8,128)(2,1)}), bf16[16,128,1024]{2,1,0:T(8,128)(2,1)}, u32[]{:S(2)}, u32[]{:S(2)}) %all-to-all-start.2) | async-done | bytes 4194336 | tf_op jit(solution)/shard_map/all_to_all | solution.py:150
  87.6 52.4 %all_to_all.30.k_ref = bf16[16,128,1024]{2,1,0:T(8,128)(2,1)} all-to-all(bf16[16,128,1024]{2,1,0:T(8,128)(2,1)} %copy.66), channel_id=1, replica_groups=mesh['fact'=8,'dim'=16] {'dim'}, dimensions={0} | all-to-all | bytes 8388608 | tf_op jit(solution)/shard_map/all_to_all | solution.py:149
  140.0 36.3 %shard_map.93 = (bf16[256,1024]{1,0:T(8,128)(2,1)}, bf16[256,1024]{1,0:T(8,128)(2,1)}, bf16[8,16,128,128]{3,2,1,0:T(8,128)(2,1)}, bf16[8,16,128,128]{3,2,1,0:T(8,128)(2,1)}) custom-call(s32[2,8]{1,0:T(2,128)} %copy-done.1, s32[2]{0:T(128)} %length_ref.1, bf16[256,1024]{1,0:T(8,128)(2,1)} %q_ref.1, bf16[256,1024]{1,0:T(8,128)(2,1)} %g_ref.1, ...), custom_call_target="tpu_custom_call" | custom-call | tf_op jit(solution)/shard_map/pallas_call | solution.py:110
  176.3 59.6 %all_to_all.31 = bf16[128,128,128]{2,1,0:T(8,128)(2,1)} all-to-all(bf16[128,128,128]{2,1,0:T(8,128)(2,1)} %bitcast.18), channel_id=1, replica_groups=mesh['fact'=8,'dim'=16] {'fact','dim'}, dimensions={0} | all-to-all | bytes 8388608 | tf_op jit(solution)/shard_map/all_to_all | solution.py:157
  235.8 5.5 %all-to-all-start.4 = ((bf16[128,128,128]{2,1,0:T(8,128)(2,1)}), bf16[128,128,128]{2,1,0:T(8,128)(2,1)}, u32[]{:S(2)}, u32[]{:S(2)}) async-start(bf16[128,128,128]{2,1,0:T(8,128)(2,1)} %bitcast.17), calls=%async_computation.4 | async-start | bytes 8388608 | tf_op jit(solution)/shard_map/all_to_all | solution.py:161
  241.4 0.6 dynamic-slice
  242.6 0.2 dynamic-update-slice
  242.8 49.2 %all-reduce = s32[128]{0:T(128)S(1)} all-reduce(s32[128]{0:T(128)S(1)} %dynamic-update-slice), channel_id=2, replica_groups=mesh['fact'=8,'dim'=16] {'fact'}, use_global_device_ids=true, to_apply=%add | all-reduce | flops 128 | bytes 1024
  292.0 4.5 %fusion.8 = bf16[8,128,128]{2,0,1:T(8,128)(2,1)S(1)} fusion(bf16[128,128,128]{2,1,0:T(8,128)(2,1)} %all_to_all.31, s32[128]{0:T(128)S(1)} %all-reduce), kind=kOutput, calls=%fused_computation.10 | convolution fusion | flops 33686528 | bytes 4456960 | tf_op jit(solution)/shard_map/ep,ejs->pjs/dot_general | solution.py:167
  296.5 0.7 copy.48
  297.3 4.5 %fusion.11 = bf16[8,128,128]{2,0,1:T(8,128)(2,1)S(1)} fusion(bf16[128,128,128]{2,1,0:T(8,128)(2,1)} %all-to-all-done.4, s32[128]{0:T(128)S(1)} %all-reduce), kind=kOutput, calls=%fused_computation.11 | convolution fusion | flops 33686528 | bytes 4456960 | tf_op jit(solution)/shard_map/ep,ejs->pjs/dot_general | solution.py:171
  301.8 0.7 copy.50
  (7 shorter events, 0.0 us)
Async XLA Ops:
  0.6 16.2 %copy-start = (bf16[1024,1024]{1,0:T(8,128)(2,1)S(1)}, bf16[1024,1024]{1,0:T(8,128)(2,1)}, u32[]{:S(2)}) copy-start(bf16[1024,1024]{1,0:T(8,128)(2,1)} %param.8) | copy-start | bytes 6291460
  2.2 20.6 %copy-start.1 = (s32[2,8]{1,0:T(2,128)}, s32[2,8]{1,0:T(2,128)S(1)}, u32[]{:S(2)}) copy-start(s32[2,8]{1,0:T(2,128)S(1)} %get-tuple-element.13.owner_ref) | copy-start | bytes 196
  22.8 64.8 %all-to-all-start.2 = ((bf16[16,128,1024]{2,1,0:T(8,128)(2,1)}), bf16[16,128,1024]{2,1,0:T(8,128)(2,1)}, u32[]{:S(2)}, u32[]{:S(2)}) async-start(bf16[16,128,1024]{2,1,0:T(8,128)(2,1)} %copy.65), calls=%async_computation.2 | async-start | bytes 8388608 | tf_op jit(solution)/shard_map/all_to_all | solution.py:150
  235.8 5.5 %copy-start.2 = (u32[128]{0:T(128)S(1)}, u32[128]{0:T(128)}, u32[]{:S(2)}) copy-start(u32[128]{0:T(128)} %constant.35) | copy-start | bytes 1540
  235.8 61.4 %all-to-all-start.4 = ((bf16[128,128,128]{2,1,0:T(8,128)(2,1)}), bf16[128,128,128]{2,1,0:T(8,128)(2,1)}, u32[]{:S(2)}, u32[]{:S(2)}) async-start(bf16[128,128,128]{2,1,0:T(8,128)(2,1)} %bitcast.17), calls=%async_computation.4 | async-start | bytes 8388608 | tf_op jit(solution)/shard_map/all_to_all | solution.py:161

commit v4 on v3

--- a/solution.py
+++ b/solution.py
@@ -26,7 +26,7 @@
 
 
 def attention_kernel(owner_ref, length_ref, q_ref, g_ref, k_ref, v_ref,
-                     att_ref, qg_ref, dk_out, dv_out, kbuf, vbuf, dk_ref, dv_ref):
+                     att_ref, qg_ref, grad_out, kbuf, vbuf, dk_ref, dv_ref):
     tiles = q_ref.shape[0] // TILE
     slots = kbuf.shape[0] // TILE
     scale = HEAD_DIM ** (-0.5)
@@ -74,12 +74,13 @@
             owner = owner_ref[t, j]
             dk_ref[owner] = dk_ref[owner] + key_grad[j * TILE:(j + 1) * TILE]
             dv_ref[owner] = dv_ref[owner] + value_grad[j * TILE:(j + 1) * TILE]
-    dk_out[0] = dk_ref[...].astype(dk_out.dtype)
-    dv_out[0] = dv_ref[...].astype(dv_out.dtype)
-
-
-def attend_local(owner_of, tile_lengths, queries, cotangent, fetched_keys, fetched_values):
-    owners, _, width = fetched_keys.shape
+    grad_out[0, :, :, :PAIR] = dk_ref[...].astype(grad_out.dtype)
+    grad_out[0, :, :, PAIR:] = dv_ref[...].astype(grad_out.dtype)
+
+
+def attend_local(owner_of, tile_lengths, queries, cotangent, fetched):
+    owners, _, both = fetched.shape
+    width = both // 2
     rows = queries.shape[0]
     slots = owner_of.shape[1]
     pairs = width // PAIR
@@ -92,13 +93,12 @@
             pl.BlockSpec((rows, PAIR), col),
             pl.BlockSpec((rows, PAIR), col),
             pl.BlockSpec((owners, TILE, PAIR), blk),
-            pl.BlockSpec((owners, TILE, PAIR), blk),
+            pl.BlockSpec((owners, TILE, PAIR), lambda hp, own, ln: (0, 0, hp + pairs)),
         ],
         out_specs=[
             pl.BlockSpec((rows, PAIR), col),
             pl.BlockSpec((rows, PAIR), col),
-            pl.BlockSpec((1, owners, TILE, PAIR), lambda hp, own, ln: (hp, 0, 0, 0)),
-            pl.BlockSpec((1, owners, TILE, PAIR), lambda hp, own, ln: (hp, 0, 0, 0)),
+            pl.BlockSpec((1, owners, TILE, 2 * PAIR), lambda hp, own, ln: (hp, 0, 0, 0)),
         ],
         scratch_shapes=[
             pltpu.VMEM((slots * TILE, PAIR), jnp.bfloat16),
@@ -113,11 +113,33 @@
         out_shape=[
             jax.ShapeDtypeStruct((rows, width), jnp.bfloat16),
             jax.ShapeDtypeStruct((rows, width), jnp.bfloat16),
-            jax.ShapeDtypeStruct((pairs, owners, TILE, PAIR), jnp.bfloat16),
-            jax.ShapeDtypeStruct((pairs, owners, TILE, PAIR), jnp.bfloat16),
+            jax.ShapeDtypeStruct((pairs, owners, TILE, 2 * PAIR), jnp.bfloat16),
         ],
         compiler_params=pltpu.CompilerParams(dimension_semantics=("arbitrary",)),
-    )(owner_of, tile_lengths, queries, cotangent, fetched_keys, fetched_values)
+    )(owner_of, tile_lengths, queries, cotangent, fetched, fetched)
+
+
+def reply_kernel(pick_ref, k_ref, v_ref, out_ref):
+    width = k_ref.shape[2]
+    out_ref[0, :, :width] = k_ref[0]
+    out_ref[0, :, width:] = v_ref[0]
+
+
+def gather_reply(picks, key_blocks, value_blocks):
+    _, rows, width = key_blocks.shape
+    count = picks.shape[0]
+    src = lambda i, pick: (pick[i], 0, 0)
+    grid_spec = pltpu.PrefetchScalarGridSpec(
+        num_scalar_prefetch=1,
+        grid=(count,),
+        in_specs=[pl.BlockSpec((1, rows, width), src), pl.BlockSpec((1, rows, width), src)],
+        out_specs=pl.BlockSpec((1, rows, 2 * width), lambda i, pick: (i, 0, 0)),
+    )
+    return pl.pallas_call(
+        reply_kernel,
+        grid_spec=grid_spec,
+        out_shape=jax.ShapeDtypeStruct((count, rows, 2 * width), key_blocks.dtype),
+    )(picks, key_blocks, value_blocks)
 
 
 def body(queries, key_rows, value_rows, cotangent, block_lists, tile_lengths):
@@ -136,42 +158,29 @@
         wanted.reshape(owners, 1), "dim", split_axis=0, concat_axis=0, tiled=True
     )
     block_ids = jnp.arange(blocks_here, dtype=jnp.int32)[None, :]
-    slot_selector = (requests == block_ids).astype(jnp.bfloat16)
-    gathered_key_blocks = key_rows.reshape(blocks_here, TILE, model_width)
-    gathered_value_blocks = value_rows.reshape(blocks_here, TILE, model_width)
-    reply_keys = jnp.einsum(
-        "nh,hcm->ncm", slot_selector, gathered_key_blocks, preferred_element_type=jnp.float32
-    ).astype(jnp.bfloat16)
-    reply_values = jnp.einsum(
-        "nh,hcm->ncm", slot_selector, gathered_value_blocks, preferred_element_type=jnp.float32
-    ).astype(jnp.bfloat16)
-    fetched_keys, fetched_values = (
-        lax.all_to_all(reply_keys, "dim", split_axis=0, concat_axis=0, tiled=True),
-        lax.all_to_all(reply_values, "dim", split_axis=0, concat_axis=0, tiled=True),
-    )
-    attended_out, query_grad_out, partial_keys, partial_values = attend_local(
-        owner_of, tile_lengths, queries, cotangent, fetched_keys, fetched_values
+    picks = jnp.clip(requests.reshape(owners), 0, blocks_here - 1)
+    reply = gather_reply(
+        picks,
+        key_rows.reshape(blocks_here, TILE, model_width),
+        value_rows.reshape(blocks_here, TILE, model_width),
+    )
+    fetched = lax.all_to_all(reply, "dim", split_axis=0, concat_axis=0, tiled=True)
+    attended_out, query_grad_out, partial_grads = attend_local(
+        owner_of, tile_lengths, queries, cotangent, fetched
     )
     fact_count = lax.axis_size("fact")
-    everyone = ("fact", "dim")
-    pieces_keys = lax.all_to_all(
-        partial_keys.reshape(fact_count * owners, TILE, model_width // fact_count),
-        everyone, split_axis=0, concat_axis=0, tiled=True,
-    )
-    pieces_values = lax.all_to_all(
-        partial_values.reshape(fact_count * owners, TILE, model_width // fact_count),
-        everyone, split_axis=0, concat_axis=0, tiled=True,
+    span = model_width // fact_count
+    pieces = lax.all_to_all(
+        partial_grads.reshape(fact_count * owners, TILE, 2 * span),
+        ("fact", "dim"), split_axis=0, concat_axis=0, tiled=True,
     )
     all_requests = lax.all_gather(requests.reshape(owners), "fact", tiled=True)
-    block_selector = (all_requests[:, None] == block_ids).astype(jnp.float32)
-    key_grad_out = jnp.einsum(
-        "ep,ejs->pjs", block_selector, pieces_keys.astype(jnp.float32),
-        precision=lax.Precision.HIGHEST,
-    ).reshape(blocks_here * TILE, model_width // fact_count)
-    value_grad_out = jnp.einsum(
-        "ep,ejs->pjs", block_selector, pieces_values.astype(jnp.float32),
-        precision=lax.Precision.HIGHEST,
-    ).reshape(blocks_here * TILE, model_width // fact_count)
+    block_selector = (all_requests[:, None] == block_ids).astype(jnp.bfloat16)
+    summed = jnp.einsum(
+        "ep,ejs->pjs", block_selector, pieces, preferred_element_type=jnp.float32
+    )
+    key_grad_out = summed[:, :, :span].reshape(blocks_here * TILE, span)
+    value_grad_out = summed[:, :, span:].reshape(blocks_here * TILE, span)
     return (
         attended_out,
         query_grad_out,

time: 304 us -> 290 us (0.954)
  waiting for transfers between devices: 51.7 us -> 4.7 us
  blocking collectives: 175 us -> 214 us
  Pallas kernels: 36.3 us -> 47.7 us
  local copies, waits for them, and re-layouts: 11 us -> 2.45 us
  matrix products: 13.7 us -> 7.86 us
  starting transfers between devices: 11.2 us -> 7.5 us
    unnamed x1, blocking collectives: 49.2 us -> 99.8 us
    all_to_all x2 -> x1, waiting for transfers between devices: 51.7 us -> 4.7 us  [body(): lax.all_to_all(partial_grads.reshape(fact_count * owners, TILE, 2 * span)...]
    all_to_all x2 -> x1, blocking collectives: 112 us -> 100 us  [body(): lax.all_to_all(reply, 'dim', split_axis=0, concat_axis=0, tiled=True)]
    pallas_call x0 -> x1, Pallas kernels: none -> 11 us  [gather_reply(): pl.pallas_call(reply_kernel, grid_spec=grid_spec, out_shape=jax.ShapeDtyp...]
    dot_general x2 -> x0, local copies, waits for them, and re-layouts: 8.59 us -> none  [the longest x1 4.3 us: body(): jnp.einsum('nh,hcm->ncm', slot_selector, gathered_value_blocks, preferred...]
    dot_general x4 -> x1, matrix products: 13.7 us -> 7.86 us  [body(): jnp.einsum('ep,ejs->pjs', block_selector, pieces, preferred_element_type=...]
    all_to_all x2 -> x1, starting transfers between devices: 11.2 us -> 7.5 us  [body(): lax.all_to_all(partial_grads.reshape(fact_count * owners, TILE, 2 * span)...]
  transfers between devices with their start and end apart: 2 -> 1, of which waited for: 1 -> 1; matrix products, arithmetic and copies ran while one was open for 4% -> 0% of each run, Pallas kernels for 0% -> 0%
where the time goes in v4:
time: 290 us; the launch traced here: 288 us
  blocking collectives  214 us (74%)
  Pallas kernels  47.7 us (16%)
  matrix products  7.86 us (3%)
  starting transfers between devices  7.5 us (3%)
  waiting for transfers between devices  4.7 us (2%)
    all_to_all x1, blocking collectives, body(): lax.all_to_all(reply, 'dim', split_axis=0, concat_axis=0, tiled=True)  100 us
    unnamed x1, blocking collectives  99.8 us
    pallas_call x1, Pallas kernels, attend_local(): pl.pallas_call(attention_kernel, grid_spec=grid_spec, out_shape=[jax.Shap...  36.7 us
    all_to_all x1, blocking collectives, body(): lax.all_to_all(wanted.reshape(owners, 1), 'dim', split_axis=0, concat_axi...  14 us
    pallas_call x1, Pallas kernels, gather_reply(): pl.pallas_call(reply_kernel, grid_spec=grid_spec, out_shape=jax.ShapeDtyp...  11 us
    dot_general x1, matrix products, body(): jnp.einsum('ep,ejs->pjs', block_selector, pieces, preferred_element_type=...  7.86 us
    all_to_all x1, starting transfers between devices, body(): lax.all_to_all(partial_grads.reshape(fact_count * owners, TILE, 2 * span)...  7.5 us
  transfers between devices with their start and end apart: 1, of which 1 were waited for; matrix products, arithmetic and copies ran while one was open for 0% of the time, Pallas kernels for 0%

profile of v4, /device:TPU:32, one launch (start us, length us, event | category | flops | bytes accessed | tf_op | source)
XLA Modules:
  0.0 288.2 jit_solution(4602267182166646376)
XLA Ops:
  0.6 0.7 iota_compare_fusion.2
  1.4 0.7 and_select_fusion
  2.0 0.0 copy-start
  2.1 0.1 select_reduce_fusion
  2.1 0.1 copy.22
  2.2 14.0 %all_to_all.19 = s32[16,1,1]{2,1,0:T(1,128)S(1)} all-to-all(s32[16,1,1]{2,1,0:T(1,128)S(1)} %copy.22), channel_id=1, replica_groups=mesh['fact'=8,'dim'=16] {'dim'}, dimensions={0} | all-to-all | bytes 128 | tf_op jit(solution)/shard_map/all_to_all | solution.py:157
  16.3 1.2 fusion.9
  17.5 11.0 %shard_map.93 = bf16[16,128,2048]{2,1,0:T(8,128)(2,1)} custom-call(s32[16]{0:T(128)} %get-tuple-element.11.pick_ref, bf16[8,128,1024]{2,1,0:T(8,128)(2,1)} %bitcast.11, bf16[8,128,1024]{2,1,0:T(8,128)(2,1)} %bitcast.12), custom_call_target="tpu_custom_call" | custom-call | tf_op jit(solution)/shard_map/pallas_call | solution.py:138
  28.4 100.2 %all_to_all.20.k_ref.v_ref = bf16[16,128,2048]{2,1,0:T(8,128)(2,1)} all-to-all(bf16[16,128,2048]{2,1,0:T(8,128)(2,1)} %shard_map.93), channel_id=1, replica_groups=mesh['fact'=8,'dim'=16] {'dim'}, dimensions={0} | all-to-all | bytes 16777216 | tf_op jit(solution)/shard_map/all_to_all | solution.py:167
  128.6 0.0 copy-done
  128.6 36.7 %shard_map.94 = (bf16[256,1024]{1,0:T(8,128)(2,1)}, bf16[256,1024]{1,0:T(8,128)(2,1)}, bf16[8,16,128,256]{3,2,1,0:T(8,128)(2,1)}) custom-call(s32[2,8]{1,0:T(2,128)} %copy-done, s32[2]{0:T(128)} %length_ref.1, bf16[256,1024]{1,0:T(8,128)(2,1)} %q_ref.1, bf16[256,1024]{1,0:T(8,128)(2,1)} %g_ref.1, bf16[16,128,2048]{2,1,0:T(8,128)(2,1)} %all_to_all.20.k_ref.v_ref, ...), custom_call_target="tpu_custom_call" | custom-call | tf_op jit(solution)/shard_map/pallas_call | solution.py:110
  165.3 0.0 copy-start.1
  165.3 7.5 %all-to-all-start.2 = ((bf16[128,128,256]{2,1,0:T(8,128)(2,1)}), bf16[128,128,256]{2,1,0:T(8,128)(2,1)}, u32[]{:S(2)}, u32[]{:S(2)}) async-start(bf16[128,128,256]{2,1,0:T(8,128)(2,1)} %bitcast.10), calls=%async_computation.2 | async-start | bytes 16777216 | tf_op jit(solution)/shard_map/all_to_all | solution.py:173
  172.8 0.0 copy-done.1
  172.8 0.6 dynamic-slice
  174.1 0.2 dynamic-update-slice
  174.3 99.8 %all-reduce = s32[128]{0:T(128)S(1)} all-reduce(s32[128]{0:T(128)S(1)} %dynamic-update-slice), channel_id=2, replica_groups=mesh['fact'=8,'dim'=16] {'fact'}, use_global_device_ids=true, to_apply=%add | all-reduce | flops 128 | bytes 1024
  274.1 4.7 %all-to-all-done.2 = bf16[128,128,256]{2,1,0:T(8,128)(2,1)} async-done(((bf16[128,128,256]{2,1,0:T(8,128)(2,1)}), bf16[128,128,256]{2,1,0:T(8,128)(2,1)}, u32[]{:S(2)}, u32[]{:S(2)}) %all-to-all-start.2) | async-done | bytes 8388640 | tf_op jit(solution)/shard_map/all_to_all | solution.py:173
  278.8 7.9 %fusion.2 = bf16[8,128,256]{2,0,1:T(8,128)(2,1)S(1)} fusion(bf16[128,128,256]{2,1,0:T(8,128)(2,1)} %all-to-all-done.2, s32[128]{0:T(128)S(1)} %all-reduce), kind=kOutput, calls=%fused_computation.2 | convolution fusion | flops 67372032 | bytes 8913408 | tf_op jit(solution)/shard_map/ep,ejs->pjs/dot_general | solution.py:179
  286.7 0.7 copy.25
  287.5 0.7 copy.24
  (2 shorter events, 0.0 us)
Async XLA Ops:
  2.0 126.6 %copy-start = (s32[2,8]{1,0:T(2,128)}, s32[2,8]{1,0:T(2,128)S(1)}, u32[]{:S(2)}) copy-start(s32[2,8]{1,0:T(2,128)S(1)} %get-tuple-element.15.owner_ref) | copy-start | bytes 196
  165.3 7.5 %copy-start.1 = (u32[128]{0:T(128)S(1)}, u32[128]{0:T(128)}, u32[]{:S(2)}) copy-start(u32[128]{0:T(128)} %constant.37) | copy-start | bytes 1540
  165.3 113.5 %all-to-all-start.2 = ((bf16[128,128,256]{2,1,0:T(8,128)(2,1)}), bf16[128,128,256]{2,1,0:T(8,128)(2,1)}, u32[]{:S(2)}, u32[]{:S(2)}) async-start(bf16[128,128,256]{2,1,0:T(8,128)(2,1)} %bitcast.10), calls=%async_computation.2 | async-start | bytes 16777216 | tf_op jit(solution)/shard_map/all_to_all | solution.py:173

commit v5 on v4

--- a/solution.py
+++ b/solution.py
@@ -79,8 +79,7 @@
 
 
 def attend_local(owner_of, tile_lengths, queries, cotangent, fetched):
-    owners, _, both = fetched.shape
-    width = both // 2
+    owners, _, _, width = fetched.shape
     rows = queries.shape[0]
     slots = owner_of.shape[1]
     pairs = width // PAIR
@@ -92,8 +91,8 @@
         in_specs=[
             pl.BlockSpec((rows, PAIR), col),
             pl.BlockSpec((rows, PAIR), col),
-            pl.BlockSpec((owners, TILE, PAIR), blk),
-            pl.BlockSpec((owners, TILE, PAIR), lambda hp, own, ln: (0, 0, hp + pairs)),
+            pl.BlockSpec((owners, None, TILE, PAIR), lambda hp, own, ln: (0, 0, 0, hp)),
+            pl.BlockSpec((owners, None, TILE, PAIR), lambda hp, own, ln: (0, 1, 0, hp)),
         ],
         out_specs=[
             pl.BlockSpec((rows, PAIR), col),
@@ -119,27 +118,81 @@
     )(owner_of, tile_lengths, queries, cotangent, fetched, fetched)
 
 
-def reply_kernel(pick_ref, k_ref, v_ref, out_ref):
-    width = k_ref.shape[2]
-    out_ref[0, :, :width] = k_ref[0]
-    out_ref[0, :, width:] = v_ref[0]
+def reply_kernel(pick_ref, k_hbm, v_hbm, out_hbm, sems):
+    copies = []
+    for i in range(out_hbm.shape[0]):
+        for plane, src in enumerate((k_hbm, v_hbm)):
+            copy = pltpu.make_async_copy(src.at[pick_ref[i]], out_hbm.at[i, plane], sems.at[i, plane])
+            copy.start()
+            copies.append(copy)
+    for copy in copies:
+        copy.wait()
 
 
 def gather_reply(picks, key_blocks, value_blocks):
     _, rows, width = key_blocks.shape
     count = picks.shape[0]
-    src = lambda i, pick: (pick[i], 0, 0)
     grid_spec = pltpu.PrefetchScalarGridSpec(
         num_scalar_prefetch=1,
-        grid=(count,),
-        in_specs=[pl.BlockSpec((1, rows, width), src), pl.BlockSpec((1, rows, width), src)],
-        out_specs=pl.BlockSpec((1, rows, 2 * width), lambda i, pick: (i, 0, 0)),
+        grid=(1,),
+        in_specs=[pl.BlockSpec(memory_space=pl.ANY), pl.BlockSpec(memory_space=pl.ANY)],
+        out_specs=pl.BlockSpec(memory_space=pl.ANY),
+        scratch_shapes=[pltpu.SemaphoreType.DMA((count, 2))],
     )
     return pl.pallas_call(
         reply_kernel,
         grid_spec=grid_spec,
-        out_shape=jax.ShapeDtypeStruct((count, rows, 2 * width), key_blocks.dtype),
+        out_shape=jax.ShapeDtypeStruct((count, 2, rows, width), key_blocks.dtype),
     )(picks, key_blocks, value_blocks)
+
+
+def sum_kernel(req_ref, piece_ref, key_out, value_out, acc):
+    step = pl.program_id(0)
+    chunk = piece_ref.shape[0]
+    span = key_out.shape[1]
+    rows = piece_ref.shape[1]
+
+    @pl.when(step == 0)
+    def _():
+        acc[...] = jnp.zeros_like(acc)
+
+    for i in range(chunk):
+        target = req_ref[step * chunk + i]
+
+        @pl.when(target >= 0)
+        def _():
+            acc[target] = acc[target] + piece_ref[i].astype(jnp.float32)
+
+    @pl.when(step == pl.num_programs(0) - 1)
+    def _():
+        for l in range(acc.shape[0]):
+            key_out[pl.ds(l * rows, rows), :] = acc[l, :, :span].astype(key_out.dtype)
+            value_out[pl.ds(l * rows, rows), :] = acc[l, :, span:].astype(value_out.dtype)
+
+
+def sum_pieces(all_requests, pieces, blocks):
+    sources, rows, both = pieces.shape
+    span = both // 2
+    chunk = 16
+    grid_spec = pltpu.PrefetchScalarGridSpec(
+        num_scalar_prefetch=1,
+        grid=(sources // chunk,),
+        in_specs=[pl.BlockSpec((chunk, rows, both), lambda i, req: (i, 0, 0))],
+        out_specs=[
+            pl.BlockSpec((blocks * rows, span), lambda i, req: (0, 0)),
+            pl.BlockSpec((blocks * rows, span), lambda i, req: (0, 0)),
+        ],
+        scratch_shapes=[pltpu.VMEM((blocks, rows, both), jnp.float32)],
+    )
+    return pl.pallas_call(
+        sum_kernel,
+        grid_spec=grid_spec,
+        out_shape=[
+            jax.ShapeDtypeStruct((blocks * rows, span), jnp.bfloat16),
+            jax.ShapeDtypeStruct((blocks * rows, span), jnp.bfloat16),
+        ],
+        compiler_params=pltpu.CompilerParams(dimension_semantics=("arbitrary",)),
+    )(all_requests, pieces)
 
 
 def body(queries, key_rows, value_rows, cotangent, block_lists, tile_lengths):
@@ -175,17 +228,12 @@
         ("fact", "dim"), split_axis=0, concat_axis=0, tiled=True,
     )
     all_requests = lax.all_gather(requests.reshape(owners), "fact", tiled=True)
-    block_selector = (all_requests[:, None] == block_ids).astype(jnp.bfloat16)
-    summed = jnp.einsum(
-        "ep,ejs->pjs", block_selector, pieces, preferred_element_type=jnp.float32
-    )
-    key_grad_out = summed[:, :, :span].reshape(blocks_here * TILE, span)
-    value_grad_out = summed[:, :, span:].reshape(blocks_here * TILE, span)
+    key_grad_out, value_grad_out = sum_pieces(all_requests, pieces, blocks_here)
     return (
         attended_out,
         query_grad_out,
-        key_grad_out.astype(jnp.bfloat16),
-        value_grad_out.astype(jnp.bfloat16),
+        key_grad_out,
+        value_grad_out,
     )
 
 

time: 290 us -> 533 us (1.84)
  Pallas kernels: 47.7 us -> 301 us
  matrix products: 7.86 us -> 0 us
    pallas_call x1, Pallas kernels: 11 us -> 256 us  [gather_reply(): pl.pallas_call(reply_kernel, grid_spec=grid_spec, out_shape=jax.ShapeDtyp...]
    all_gather x0 -> x1, blocking collectives: none -> 100 us  [body(): all_requests = lax.all_gather(requests.reshape(owners), 'fact', tiled=True)]
    unnamed x1 -> x0, blocking collectives: 99.8 us -> none
    dot_general x1 -> x0, matrix products: 7.86 us -> none  [body(): jnp.einsum('ep,ejs->pjs', block_selector, pieces, preferred_element_type=...]
    pallas_call x0 -> x1, Pallas kernels: none -> 7.82 us  [sum_pieces(): pl.pallas_call(sum_kernel, grid_spec=grid_spec, out_shape=[jax.ShapeDtype...]
where the time goes in v5:
time: 533 us
  Pallas kernels  301 us (56%)
  blocking collectives  214 us (40%)
  starting transfers between devices  9.29 us (2%)
    pallas_call x1, Pallas kernels, gather_reply(): pl.pallas_call(reply_kernel, grid_spec=grid_spec, out_shape=jax.ShapeDtyp...  256 us
    all_gather x1, blocking collectives, body(): all_requests = lax.all_gather(requests.reshape(owners), 'fact', tiled=True)  100 us
    all_to_all x1, blocking collectives, body(): lax.all_to_all(reply, 'dim', split_axis=0, concat_axis=0, tiled=True)  99 us
    pallas_call x1, Pallas kernels, attend_local(): pl.pallas_call(attention_kernel, grid_spec=grid_spec, out_shape=[jax.Shap...  36.7 us
    all_to_all x1, blocking collectives, body(): lax.all_to_all(wanted.reshape(owners, 1), 'dim', split_axis=0, concat_axi...  14 us
  transfers between devices with their start and end apart: 1, of which 1 were waited for; matrix products, arithmetic and copies ran while one was open for 0% of the time, Pallas kernels for 0%

profile of v5, /device:TPU:32, one launch (start us, length us, event | category | flops | bytes accessed | tf_op | source)
XLA Modules:
  0.0 532.5 jit_solution(15183024472013949911)
XLA Ops:
  0.6 0.7 iota_compare_fusion.1
  1.4 0.7 and_select_fusion
  2.0 0.0 copy-start
  2.1 0.1 select_reduce_fusion
  2.1 0.1 copy.12
  2.2 14.0 %all_to_all.19 = s32[16,1,1]{2,1,0:T(1,128)S(1)} all-to-all(s32[16,1,1]{2,1,0:T(1,128)S(1)} %copy.12), channel_id=1, replica_groups=mesh['fact'=8,'dim'=16] {'dim'}, dimensions={0} | all-to-all | bytes 128 | tf_op jit(solution)/shard_map/all_to_all | solution.py:210
  16.3 1.2 fusion.1
  17.5 256.2 %shard_map.93 = bf16[16,2,128,1024]{3,2,1,0:T(8,128)(2,1)} custom-call(s32[16]{0:T(128)} %get-tuple-element.15.pick_ref, bf16[8,128,1024]{2,1,0:T(8,128)(2,1)} %bitcast.6, bf16[8,128,1024]{2,1,0:T(8,128)(2,1)} %bitcast.7), custom_call_target="tpu_custom_call" | custom-call | tf_op jit(solution)/shard_map/pallas_call | solution.py:142
  273.6 99.0 %all_to_all.20.k_ref.v_ref = bf16[16,2,128,1024]{3,2,1,0:T(8,128)(2,1)} all-to-all(bf16[16,2,128,1024]{3,2,1,0:T(8,128)(2,1)} %shard_map.93), channel_id=1, replica_groups=mesh['fact'=8,'dim'=16] {'dim'}, dimensions={0} | all-to-all | bytes 16777216 | tf_op jit(solution)/shard_map/all_to_all | solution.py:220
  372.7 0.0 copy-done
  372.7 36.7 %shard_map.94 = (bf16[256,1024]{1,0:T(8,128)(2,1)}, bf16[256,1024]{1,0:T(8,128)(2,1)}, bf16[8,16,128,256]{3,2,1,0:T(8,128)(2,1)}) custom-call(s32[2,8]{1,0:T(2,128)} %copy-done, s32[2]{0:T(128)} %length_ref.1, bf16[256,1024]{1,0:T(8,128)(2,1)} %q_ref.1, bf16[256,1024]{1,0:T(8,128)(2,1)} %g_ref.1, bf16[16,2,128,1024]{3,2,1,0:T(8,128)(2,1)} %all_to_all.20.k_ref.v_ref, ...), custom_call_target="tpu_custom_call" | custom-call | tf_op jit(solution)/shard_map/pallas_call | solution.py:109
  409.4 0.0 copy-start.1
  409.4 9.3 %all-to-all-start.2 = ((bf16[128,128,256]{2,1,0:T(8,128)(2,1)}), bf16[128,128,256]{2,1,0:T(8,128)(2,1)}, u32[]{:S(2)}, u32[]{:S(2)}) async-start(bf16[128,128,256]{2,1,0:T(8,128)(2,1)} %bitcast.5), calls=%async_computation.2 | async-start | bytes 16777216 | tf_op jit(solution)/shard_map/all_to_all | solution.py:226
  418.7 0.0 copy-done.1
  418.7 0.6 dynamic-slice
  420.0 0.2 dynamic-update-slice
  420.2 100.5 %all-reduce.req_ref = s32[128]{0:T(128)} all-reduce(s32[128]{0:T(128)S(1)} %dynamic-update-slice), channel_id=2, replica_groups=mesh['fact'=8,'dim'=16] {'fact'}, use_global_device_ids=true, to_apply=%add | all-reduce | flops 128 | bytes 1024 | tf_op jit(solution)/shard_map/all_gather | solution.py:230
  520.6 4.0 all-to-all-done.2.piece_ref
  524.7 7.8 %shard_map.95 = (bf16[1024,128]{1,0:T(8,128)(2,1)}, bf16[1024,128]{1,0:T(8,128)(2,1)}) custom-call(s32[128]{0:T(128)} %all-reduce.req_ref, bf16[128,128,256]{2,1,0:T(8,128)(2,1)} %all-to-all-done.2.piece_ref), custom_call_target="tpu_custom_call" | custom-call | tf_op jit(solution)/shard_map/pallas_call | solution.py:187
  (1 shorter events, 0.0 us)
Async XLA Ops:
  2.0 370.6 %copy-start = (s32[2,8]{1,0:T(2,128)}, s32[2,8]{1,0:T(2,128)S(1)}, u32[]{:S(2)}) copy-start(s32[2,8]{1,0:T(2,128)S(1)} %get-tuple-element.17.owner_ref) | copy-start | bytes 196
  409.4 9.3 %copy-start.1 = (u32[128]{0:T(128)S(1)}, u32[128]{0:T(128)}, u32[]{:S(2)}) copy-start(u32[128]{0:T(128)} %constant.37) | copy-start | bytes 1540
  409.4 115.3 %all-to-all-start.2 = ((bf16[128,128,256]{2,1,0:T(8,128)(2,1)}), bf16[128,128,256]{2,1,0:T(8,128)(2,1)}, u32[]{:S(2)}, u32[]{:S(2)}) async-start(bf16[128,128,256]{2,1,0:T(8,128)(2,1)} %bitcast.5), calls=%async_computation.2 | async-start | bytes 16777216 | tf_op jit(solution)/shard_map/all_to_all | solution.py:226

commit v6 on v5

v6 whole, which is shorter than its diff:
```python
import functools
import jax
import jax.numpy as jnp
from jax import lax
from jax.experimental import pallas as pl
from jax.experimental.pallas import tpu as pltpu
from jax.sharding import PartitionSpec as P

HEADS = 16
HEAD_DIM = 64
TILE = 128
NEG_FILL = -1e30
PAIR = 2 * HEAD_DIM


def _nt(a, b):
    return lax.dot_general(a, b, (((1,), (1,)), ((), ())), preferred_element_type=jnp.float32)


def _tn(a, b):
    return lax.dot_general(a, b, (((0,), (0,)), ((), ())), preferred_element_type=jnp.float32)


def _nn(a, b):
    return jnp.dot(a, b, preferred_element_type=jnp.float32)


def pair_attention(q, g, keys, values, alive, first):
    scale = HEAD_DIM ** (-0.5)
    outs = []
    for h in range(2):
        mine = first if h == 0 else jnp.logical_not(first)
        qh = jnp.where(mine, q, jnp.zeros_like(q))
        gh = jnp.where(mine, g, jnp.zeros_like(g))
        scores = _nt(qh, keys) * scale
        scores = jnp.where(alive, scores, NEG_FILL)
        row_max = jnp.max(scores, axis=-1, keepdims=True)
        expo = jnp.exp(scores - row_max)
        weights = expo / jnp.sum(expo, axis=-1, keepdims=True)
        weights_low = weights.astype(jnp.bfloat16)
        attended = _nn(weights_low, values)
        dweights = _nt(gh, values)
        row_delta = jnp.sum(weights * dweights, axis=-1, keepdims=True)
        dscores = (weights * (dweights - row_delta)).astype(jnp.bfloat16)
        query_grad = _nn(dscores, keys)
        key_grad = _tn(dscores, q)
        value_grad = _tn(weights_low, g)
        outs.append((attended, query_grad, key_grad, value_grad))
    pick = lambda i: jnp.where(first, outs[0][i], outs[1][i])
    return pick(0), pick(1) * scale, pick(2) * scale, pick(3)


def fetch_attend_kernel(pick_ref, owner_ref, length_ref, slot_ref, k_ref, v_ref, q_ref, g_ref,
                        att_ref, qg_ref, grad_ref,
                        stage, kbuf, vbuf, gbuf, send_sem, recv_sem, *recv):
    owners = stage.shape[1]
    pairs = stage.shape[0]
    tiles = q_ref.shape[0] // TILE
    slots = kbuf.shape[0] // TILE
    me = lax.axis_index("dim")
    fact = lax.axis_index("fact")
    mesh = pl.DeviceIdType.MESH
    for hp in range(pairs):
        cols = pl.ds(hp * PAIR, PAIR)
        for peer in range(owners):
            chosen = pick_ref[peer]
            stage[hp, peer, 0] = k_ref[chosen, :, cols]
            stage[hp, peer, 1] = v_ref[chosen, :, cols]
    for hp in range(pairs):
        recv[hp][me] = stage[hp, me]
    barrier = pltpu.get_barrier_semaphore()
    for k in range(1, owners):
        pl.semaphore_signal(barrier, inc=1, device_id=(fact, lax.rem(me + k, owners)), device_id_type=mesh)
    pl.semaphore_wait(barrier, owners - 1)

    def remote(hp, k, src):
        dest = lax.rem(me + k, owners)
        return pltpu.make_async_remote_copy(
            src_ref=stage.at[hp, dest],
            dst_ref=recv[hp].at[src],
            send_sem=send_sem.at[hp, dest],
            recv_sem=recv_sem.at[hp, src],
            device_id=(fact, dest),
            device_id_type=mesh,
        )

    for hp in range(pairs):
        for k in range(1, owners):
            remote(hp, k, me).start()

    gbuf[:, slots] = jnp.zeros(gbuf.shape[:1] + gbuf.shape[2:], gbuf.dtype)
    lane = lax.broadcasted_iota(jnp.int32, (1, PAIR), 1)
    first = lane < HEAD_DIM
    key_pos = lax.broadcasted_iota(jnp.int32, (1, slots * TILE), 1)
    for hp in range(pairs):
        cols = pl.ds(hp * PAIR, PAIR)
        for k in range(1, owners):
            remote(hp, owners - k, lax.rem(me + k, owners)).wait_recv()
        for t in range(tiles):
            rows = pl.ds(t * TILE, TILE)
            for j in range(slots):
                owner = owner_ref[t, j]
                kbuf[pl.ds(j * TILE, TILE), :] = recv[hp][owner, 0]
                vbuf[pl.ds(j * TILE, TILE), :] = recv[hp][owner, 1]
            alive = key_pos < length_ref[t] * TILE
            attended, query_grad, key_grad, value_grad = pair_attention(
                q_ref[rows, cols], g_ref[rows, cols], kbuf[...], vbuf[...], alive, first
            )
            att_ref[rows, cols] = attended.astype(att_ref.dtype)
            qg_ref[rows, cols] = query_grad.astype(qg_ref.dtype)
            for j in range(slots):
                gbuf[t, j, :, :PAIR] = key_grad[j * TILE:(j + 1) * TILE]
                gbuf[t, j, :, PAIR:] = value_grad[j * TILE:(j + 1) * TILE]
        for owner in range(owners):
            total = gbuf[0, slot_ref[0, owner]]
            for t in range(1, tiles):
                total = total + gbuf[t, slot_ref[t, owner]]
            grad_ref[hp, owner] = total.astype(grad_ref.dtype)
    for hp in range(pairs):
        for k in range(1, owners):
            remote(hp, k, me).wait_send()


def fetch_attend(picks, owner_of, tile_lengths, slot_of, key_blocks, value_blocks, queries, cotangent):
    _, _, width = key_blocks.shape
    owners = picks.shape[0]
    rows = queries.shape[0]
    slots = owner_of.shape[1]
    pairs = width // PAIR
    whole = pl.BlockSpec(memory_space=pltpu.VMEM)
    grid_spec = pltpu.PrefetchScalarGridSpec(
        num_scalar_prefetch=4,
        grid=(1,),
        in_specs=[whole] * 4,
        out_specs=[whole] * 3,
        scratch_shapes=[
            pltpu.VMEM((pairs, owners, 2, TILE, PAIR), jnp.bfloat16),
            pltpu.VMEM((slots * TILE, PAIR), jnp.bfloat16),
            pltpu.VMEM((slots * TILE, PAIR), jnp.bfloat16),
            pltpu.VMEM((rows // TILE, slots + 1, TILE, 2 * PAIR), jnp.float32),
            pltpu.SemaphoreType.DMA((pairs, owners)),
            pltpu.SemaphoreType.DMA((pairs, owners)),
        ] + [pltpu.VMEM((owners, 2, TILE, PAIR), jnp.bfloat16) for _ in range(pairs)],
    )
    return pl.pallas_call(
        fetch_attend_kernel,
        grid_spec=grid_spec,
        out_shape=[
            jax.ShapeDtypeStruct((rows, width), jnp.bfloat16),
            jax.ShapeDtypeStruct((rows, width), jnp.bfloat16),
            jax.ShapeDtypeStruct((pairs, owners, TILE, 2 * PAIR), jnp.bfloat16),
        ],
        compiler_params=pltpu.CompilerParams(
            collective_id=0, has_side_effects=True, vmem_limit_bytes=60 * 1024 * 1024
        ),
    )(picks, owner_of, tile_lengths, slot_of, key_blocks, value_blocks, queries, cotangent)


def sum_kernel(req_ref, piece_ref, key_out, value_out, acc):
    step = pl.program_id(0)
    chunk = piece_ref.shape[0]
    span = key_out.shape[1]
    rows = piece_ref.shape[1]

    @pl.when(step == 0)
    def _():
        acc[...] = jnp.zeros_like(acc)

    for i in range(chunk):
        target = req_ref[step * chunk + i]

        @pl.when(target >= 0)
        def _():
            acc[target] = acc[target] + piece_ref[i].astype(jnp.float32)

    @pl.when(step == pl.num_programs(0) - 1)
    def _():
        for l in range(acc.shape[0]):
            key_out[pl.ds(l * rows, rows), :] = acc[l, :, :span].astype(key_out.dtype)
            value_out[pl.ds(l * rows, rows), :] = acc[l, :, span:].astype(value_out.dtype)


def sum_pieces(all_requests, pieces, blocks):
    sources, rows, both = pieces.shape
    span = both // 2
    chunk = 16
    grid_spec = pltpu.PrefetchScalarGridSpec(
        num_scalar_prefetch=1,
        grid=(sources // chunk,),
        in_specs=[pl.BlockSpec((chunk, rows, both), lambda i, req: (i, 0, 0))],
        out_specs=[
            pl.BlockSpec((blocks * rows, span), lambda i, req: (0, 0)),
            pl.BlockSpec((blocks * rows, span), lambda i, req: (0, 0)),
        ],
        scratch_shapes=[pltpu.VMEM((blocks, rows, both), jnp.float32)],
    )
    return pl.pallas_call(
        sum_kernel,
        grid_spec=grid_spec,
        out_shape=[
            jax.ShapeDtypeStruct((blocks * rows, span), jnp.bfloat16),
            jax.ShapeDtypeStruct((blocks * rows, span), jnp.bfloat16),
        ],
        compiler_params=pltpu.CompilerParams(dimension_semantics=("arbitrary",)),
    )(all_requests, pieces)


def body(queries, key_rows, value_rows, cotangent, block_lists, tile_lengths):
    owners = lax.axis_size("dim")
    tile_count = block_lists.shape[0]
    slot_count = block_lists.shape[1]
    blocks_here = key_rows.shape[0] // TILE
    model_width = key_rows.shape[1]
    alive_slots = jnp.arange(slot_count, dtype=jnp.int32)[None, :] < tile_lengths[:, None]
    owner_of = jnp.clip(block_lists // blocks_here, 0, owners - 1)
    local_of = block_lists % blocks_here
    owner_ids = jnp.arange(owners, dtype=jnp.int32)
    matched = (owner_of[:, :, None] == owner_ids[None, None, :]) & alive_slots[:, :, None]
    wanted = jnp.max(jnp.where(matched, local_of[:, :, None], -1), axis=(0, 1))
    requests = lax.all_to_all(
        wanted.reshape(owners, 1), "dim", split_axis=0, concat_axis=0, tiled=True
    )
    block_ids = jnp.arange(blocks_here, dtype=jnp.int32)[None, :]
    picks = jnp.clip(requests.reshape(owners), 0, blocks_here - 1)
    slot_ids = jnp.arange(slot_count, dtype=jnp.int32)[None, :, None]
    live_match = (owner_of[:, :, None] == owner_ids[None, None, :]) & alive_slots[:, :, None]
    slot_of = jnp.min(jnp.where(live_match, slot_ids, slot_count), axis=1)
    attended_out, query_grad_out, partial_grads = fetch_attend(
        picks,
        owner_of,
        tile_lengths,
        slot_of,
        key_rows.reshape(blocks_here, TILE, model_width),
        value_rows.reshape(blocks_here, TILE, model_width),
        queries,
        cotangent,
    )
    fact_count = lax.axis_size("fact")
    span = model_width // fact_count
    pieces = lax.all_to_all(
        partial_grads.reshape(fact_count * owners, TILE, 2 * span),
        ("fact", "dim"), split_axis=0, concat_axis=0, tiled=True,
    )
    all_requests = lax.all_gather(requests.reshape(owners), "fact", tiled=True)
    key_grad_out, value_grad_out = sum_pieces(all_requests, pieces, blocks_here)
    return (
        attended_out,
        query_grad_out,
        key_grad_out,
        value_grad_out,
    )


def solution(mesh):
    in_specs = (
        P(("fact", "dim"), None),
        P("dim", None),
        P("dim", None),
        P(("fact", "dim"), None),
        P(("fact", "dim"), None),
        P(("fact", "dim")),
    )
    out_specs = (
        P(("fact", "dim"), None),
        P(("fact", "dim"), None),
        P("dim", "fact"),
        P("dim", "fact"),
    )
    return jax.shard_map(body, mesh=mesh, in_specs=in_specs, out_specs=out_specs, check_vma=False)
```

time: 533 us -> 252 us (0.47)
  Pallas kernels: 301 us -> 118 us
  blocking collectives: 214 us -> 114 us
    pallas_call x2 -> x1, Pallas kernels: 293 us -> 110 us  [fetch_attend(): pl.pallas_call(fetch_attend_kernel, grid_spec=grid_spec, out_shape=[jax.S...]
    all_to_all x1 -> x0, blocking collectives: 99 us -> none  [body(): lax.all_to_all(reply, 'dim', split_axis=0, concat_axis=0, tiled=True)]
where the time goes in v6:
time: 252 us
  Pallas kernels  118 us (47%)
  blocking collectives  114 us (45%)
  starting transfers between devices  8.66 us (3%)
  waiting for transfers between devices  4.04 us (2%)
  other arithmetic  3.26 us (1%)
  local copies, waits for them, and re-layouts  2.52 us (1%)
    pallas_call x1, Pallas kernels, fetch_attend(): pl.pallas_call(fetch_attend_kernel, grid_spec=grid_spec, out_shape=[jax.S...  110 us
    all_gather x1, blocking collectives, body(): all_requests = lax.all_gather(requests.reshape(owners), 'fact', tiled=True)  100 us
    all_to_all x1, blocking collectives, body(): lax.all_to_all(wanted.reshape(owners, 1), 'dim', split_axis=0, concat_axi...  14 us
    all_to_all x1, starting transfers between devices, body(): lax.all_to_all(partial_grads.reshape(fact_count * owners, TILE, 2 * span)...  8.66 us
    pallas_call x1, Pallas kernels, sum_pieces(): pl.pallas_call(sum_kernel, grid_spec=grid_spec, out_shape=[jax.ShapeDtype...  7.62 us
  transfers between devices with their start and end apart: 1, of which 1 were waited for; matrix products, arithmetic and copies ran while one was open for 0% of the time, Pallas kernels for 0%

profile of v6, /device:TPU:32, one launch (start us, length us, event | category | flops | bytes accessed | tf_op | source)
XLA Modules:
  0.0 252.0 jit_solution(10461732864171790430)
XLA Ops:
  0.6 0.7 iota_compare_fusion.1
  1.4 0.7 and_select_fusion
  2.1 0.0 copy-start.2
  2.1 0.7 select_reduce_fusion
  2.7 0.1 copy.12
  2.8 14.0 %all_to_all.14 = s32[16,1,1]{2,1,0:T(1,128)S(1)} all-to-all(s32[16,1,1]{2,1,0:T(1,128)S(1)} %copy.12), channel_id=1, replica_groups=mesh['fact'=8,'dim'=16] {'dim'}, dimensions={0} | all-to-all | bytes 128 | tf_op jit(solution)/shard_map/all_to_all | solution.py:220
  16.8 1.2 fusion.2
  18.0 0.0 copy-done.2
  18.0 110.0 %shard_map.93 = (bf16[256,1024]{1,0:T(8,128)(2,1)}, bf16[256,1024]{1,0:T(8,128)(2,1)}, bf16[8,16,128,256]{3,2,1,0:T(8,128)(2,1)}) custom-call(s32[16]{0:T(128)} %get-tuple-element.15.pick_ref, s32[2,8]{1,0:T(2,128)} %copy-done.2, s32[2]{0:T(128)} %length_ref.1, s32[2,16]{1,0:T(2,128)} %get-tuple-element.16.slot_ref, bf16[8,128,1024]{2,1,0:T(8,128)(2,1)} %bitcast.6, ...), custom_call_target="tpu_custom_call" | custom-call | tf_op jit(solution)/shard_map/pallas_call | solution.py:145
  128.1 0.0 copy-start.3
  128.1 8.7 %all-to-all-start.1 = ((bf16[128,128,256]{2,1,0:T(8,128)(2,1)}), bf16[128,128,256]{2,1,0:T(8,128)(2,1)}, u32[]{:S(2)}, u32[]{:S(2)}) async-start(bf16[128,128,256]{2,1,0:T(8,128)(2,1)} %bitcast.5), calls=%async_computation.1 | async-start | bytes 16777216 | tf_op jit(solution)/shard_map/all_to_all | solution.py:240
  136.8 0.0 copy-start.1
  136.8 0.0 copy-start
  136.8 0.0 copy-done.3
  136.8 0.6 dynamic-slice
  138.0 0.2 dynamic-update-slice
  138.3 100.4 %all-reduce.req_ref = s32[128]{0:T(128)} all-reduce(s32[128]{0:T(128)S(1)} %dynamic-update-slice), channel_id=2, replica_groups=mesh['fact'=8,'dim'=16] {'fact'}, use_global_device_ids=true, to_apply=%add | all-reduce | flops 128 | bytes 1024 | tf_op jit(solution)/shard_map/all_gather | solution.py:244
  238.7 4.0 %all-to-all-done.1.piece_ref = bf16[128,128,256]{2,1,0:T(8,128)(2,1)} async-done(((bf16[128,128,256]{2,1,0:T(8,128)(2,1)}), bf16[128,128,256]{2,1,0:T(8,128)(2,1)}, u32[]{:S(2)}, u32[]{:S(2)}) %all-to-all-start.1) | async-done | bytes 8388640 | tf_op jit(solution)/shard_map/all_to_all | solution.py:240
  242.8 7.6 %shard_map.94 = (bf16[1024,128]{1,0:T(8,128)(2,1)}, bf16[1024,128]{1,0:T(8,128)(2,1)}) custom-call(s32[128]{0:T(128)} %all-reduce.req_ref, bf16[128,128,256]{2,1,0:T(8,128)(2,1)} %all-to-all-done.1.piece_ref), custom_call_target="tpu_custom_call" | custom-call | tf_op jit(solution)/shard_map/pallas_call | solution.py:197
  250.4 0.0 copy-done.1
  250.4 0.8 copy.16
  251.2 0.0 copy-done
  251.2 0.8 copy.17
  (1 shorter events, 0.0 us)
Async XLA Ops:
  2.1 16.0 %copy-start.2 = (s32[2,8]{1,0:T(2,128)}, s32[2,8]{1,0:T(2,128)S(1)}, u32[]{:S(2)}) copy-start(s32[2,8]{1,0:T(2,128)S(1)} %get-tuple-element.19.owner_ref) | copy-start | bytes 196
  128.1 8.7 %copy-start.3 = (u32[128]{0:T(128)S(1)}, u32[128]{0:T(128)}, u32[]{:S(2)}) copy-start(u32[128]{0:T(128)} %constant.41) | copy-start | bytes 1540
  128.1 114.7 %all-to-all-start.1 = ((bf16[128,128,256]{2,1,0:T(8,128)(2,1)}), bf16[128,128,256]{2,1,0:T(8,128)(2,1)}, u32[]{:S(2)}, u32[]{:S(2)}) async-start(bf16[128,128,256]{2,1,0:T(8,128)(2,1)} %bitcast.5), calls=%async_computation.1 | async-start | bytes 16777216 | tf_op jit(solution)/shard_map/all_to_all | solution.py:240
  136.8 113.6 %copy-start.1 = (bf16[256,1024]{1,0:T(8,128)(2,1)S(1)}, bf16[256,1024]{1,0:T(8,128)(2,1)}, u32[]{:S(2)}) copy-start(bf16[256,1024]{1,0:T(8,128)(2,1)} %get-tuple-element.24) | copy-start | bytes 1572868
  136.8 114.4 %copy-start = (bf16[256,1024]{1,0:T(8,128)(2,1)S(1)}, bf16[256,1024]{1,0:T(8,128)(2,1)}, u32[]{:S(2)}) copy-start(bf16[256,1024]{1,0:T(8,128)(2,1)} %get-tuple-element.25) | copy-start | bytes 1572868

commit v7 on v6

--- a/solution.py
+++ b/solution.py
@@ -52,7 +52,8 @@
 
 def fetch_attend_kernel(pick_ref, owner_ref, length_ref, slot_ref, k_ref, v_ref, q_ref, g_ref,
                         att_ref, qg_ref, grad_ref,
-                        stage, kbuf, vbuf, gbuf, send_sem, recv_sem, *recv):
+                        stage, kbuf, vbuf, gbuf, gsend, send_sem, recv_sem, gsend_sem, grecv_sem,
+                        *recv):
     owners = stage.shape[1]
     pairs = stage.shape[0]
     tiles = q_ref.shape[0] // TILE
@@ -68,10 +69,29 @@
             stage[hp, peer, 1] = v_ref[chosen, :, cols]
     for hp in range(pairs):
         recv[hp][me] = stage[hp, me]
+    facts = pairs
+    others = [(fo, k) for fo in range(facts) for k in range(owners) if (fo, k) != (0, 0)]
     barrier = pltpu.get_barrier_semaphore()
-    for k in range(1, owners):
-        pl.semaphore_signal(barrier, inc=1, device_id=(fact, lax.rem(me + k, owners)), device_id_type=mesh)
-    pl.semaphore_wait(barrier, owners - 1)
+    for fo, k in others:
+        pl.semaphore_signal(
+            barrier, inc=1,
+            device_id=(lax.rem(fact + fo, facts), lax.rem(me + k, owners)), device_id_type=mesh,
+        )
+    pl.semaphore_wait(barrier, len(others))
+    own_slot = fact * owners + me
+
+    def grad_remote(hp, dest, slot):
+        return pltpu.make_async_remote_copy(
+            src_ref=gsend.at[hp, dest],
+            dst_ref=grad_ref.at[slot],
+            send_sem=gsend_sem.at[hp, dest],
+            recv_sem=grecv_sem.at[slot],
+            device_id=(hp, dest),
+            device_id_type=mesh,
+        )
+
+    def grad_local(hp):
+        return pltpu.make_async_copy(gsend.at[hp, me], grad_ref.at[own_slot], grecv_sem.at[own_slot])
 
     def remote(hp, k, src):
         dest = lax.rem(me + k, owners)
@@ -115,10 +135,35 @@
             total = gbuf[0, slot_ref[0, owner]]
             for t in range(1, tiles):
                 total = total + gbuf[t, slot_ref[t, owner]]
-            grad_ref[hp, owner] = total.astype(grad_ref.dtype)
+            gsend[hp, owner] = total.astype(gsend.dtype)
+        for k in range(1, owners):
+            grad_remote(hp, lax.rem(me + k, owners), own_slot).start()
+
+        @pl.when(fact != hp)
+        def _():
+            grad_remote(hp, me, own_slot).start()
+
+        @pl.when(fact == hp)
+        def _():
+            grad_local(hp).start()
+
     for hp in range(pairs):
         for k in range(1, owners):
             remote(hp, k, me).wait_send()
+    for fo, k in others:
+        slot = lax.rem(fact + fo, facts) * owners + lax.rem(me + k, owners)
+        grad_remote(0, me, slot).wait_recv()
+    for hp in range(pairs):
+        for k in range(1, owners):
+            grad_remote(hp, lax.rem(me + k, owners), own_slot).wait_send()
+
+        @pl.when(fact != hp)
+        def _():
+            grad_remote(hp, me, own_slot).wait_send()
+
+        @pl.when(fact == hp)
+        def _():
+            grad_local(hp).wait()
 
 
 def fetch_attend(picks, owner_of, tile_lengths, slot_of, key_blocks, value_blocks, queries, cotangent):
@@ -132,14 +177,17 @@
         num_scalar_prefetch=4,
         grid=(1,),
         in_specs=[whole] * 4,
-        out_specs=[whole] * 3,
+        out_specs=[whole, whole, pl.BlockSpec(memory_space=pl.ANY)],
         scratch_shapes=[
             pltpu.VMEM((pairs, owners, 2, TILE, PAIR), jnp.bfloat16),
             pltpu.VMEM((slots * TILE, PAIR), jnp.bfloat16),
             pltpu.VMEM((slots * TILE, PAIR), jnp.bfloat16),
             pltpu.VMEM((rows // TILE, slots + 1, TILE, 2 * PAIR), jnp.float32),
+            pltpu.VMEM((pairs, owners, TILE, 2 * PAIR), jnp.bfloat16),
             pltpu.SemaphoreType.DMA((pairs, owners)),
             pltpu.SemaphoreType.DMA((pairs, owners)),
+            pltpu.SemaphoreType.DMA((pairs, owners)),
+            pltpu.SemaphoreType.DMA((pairs * owners,)),
         ] + [pltpu.VMEM((owners, 2, TILE, PAIR), jnp.bfloat16) for _ in range(pairs)],
     )
     return pl.pallas_call(
@@ -148,7 +196,7 @@
         out_shape=[
             jax.ShapeDtypeStruct((rows, width), jnp.bfloat16),
             jax.ShapeDtypeStruct((rows, width), jnp.bfloat16),
-            jax.ShapeDtypeStruct((pairs, owners, TILE, 2 * PAIR), jnp.bfloat16),
+            jax.ShapeDtypeStruct((pairs * owners, TILE, 2 * PAIR), jnp.bfloat16),
         ],
         compiler_params=pltpu.CompilerParams(
             collective_id=0, has_side_effects=True, vmem_limit_bytes=60 * 1024 * 1024
@@ -235,12 +283,7 @@
         queries,
         cotangent,
     )
-    fact_count = lax.axis_size("fact")
-    span = model_width // fact_count
-    pieces = lax.all_to_all(
-        partial_grads.reshape(fact_count * owners, TILE, 2 * span),
-        ("fact", "dim"), split_axis=0, concat_axis=0, tiled=True,
-    )
+    pieces = partial_grads
     all_requests = lax.all_gather(requests.reshape(owners), "fact", tiled=True)
     key_grad_out, value_grad_out = sum_pieces(all_requests, pieces, blocks_here)
     return (

time: 252 us -> 299 us (1.19)
  Pallas kernels: 118 us -> 267 us
  blocking collectives: 114 us -> 9.73 us
    pallas_call x1, Pallas kernels: 110 us -> 259 us  [fetch_attend(): pl.pallas_call(fetch_attend_kernel, grid_spec=grid_spec, out_shape=[jax.S...]
    all_gather x1, blocking collectives: 100 us -> 9.73 us  [body(): all_requests = lax.all_gather(requests.reshape(owners), 'fact', tiled=True)]
    all_to_all x1 -> x0, blocking collectives: 14 us -> none  [body(): lax.all_to_all(wanted.reshape(owners, 1), 'dim', split_axis=0, concat_axi...]
where the time goes in v7:
time: 299 us; the launch traced here: 297 us
  Pallas kernels  267 us (89%)
  blocking collectives  9.73 us (3%)
  starting transfers between devices  8.07 us (3%)
  waiting for transfers between devices  4.23 us (1%)
  local copies, waits for them, and re-layouts  3.71 us (1%)
  other arithmetic  3.26 us (1%)
    pallas_call x1, Pallas kernels, fetch_attend(): pl.pallas_call(fetch_attend_kernel, grid_spec=grid_spec, out_shape=[jax.S...  259 us
    all_gather x1, blocking collectives, body(): all_requests = lax.all_gather(requests.reshape(owners), 'fact', tiled=True)  9.73 us
    all_to_all x1, starting transfers between devices, body(): lax.all_to_all(wanted.reshape(owners, 1), 'dim', split_axis=0, concat_axi...  8.07 us
    pallas_call x1, Pallas kernels, sum_pieces(): pl.pallas_call(sum_kernel, grid_spec=grid_spec, out_shape=[jax.ShapeDtype...  7.74 us
  transfers between devices with their start and end apart: 1, of which 1 were waited for; matrix products, arithmetic and copies ran while one was open for 0% of the time, Pallas kernels for 0%

profile of v7, /device:TPU:32, one launch (start us, length us, event | category | flops | bytes accessed | tf_op | source)
XLA Modules:
  0.0 297.3 jit_solution(16416589039099167483)
XLA Ops:
  0.6 0.7 iota_compare_fusion.1
  1.4 0.7 and_select_fusion
  2.1 0.0 copy-start.2
  2.1 0.7 select_reduce_fusion
  2.7 0.7 copy.12
  3.4 8.1 %all-to-all-start = ((s32[16,1,1]{2,1,0:T(1,128)}), s32[16,1,1]{2,1,0:T(1,128)S(1)}, u32[]{:S(2)}, u32[]{:S(2)}) async-start(s32[16,1,1]{2,1,0:T(1,128)} %copy.12), calls=%async_computation | async-start | bytes 16384 | tf_op jit(solution)/shard_map/all_to_all | solution.py:268
  11.5 1.2 dynamic-slice
  13.4 4.2 %all-to-all-done = s32[16,1,1]{2,1,0:T(1,128)S(1)} async-done(((s32[16,1,1]{2,1,0:T(1,128)}), s32[16,1,1]{2,1,0:T(1,128)S(1)}, u32[]{:S(2)}, u32[]{:S(2)}) %all-to-all-start) | async-done | bytes 96 | tf_op jit(solution)/shard_map/all_to_all | solution.py:268
  17.6 1.2 fusion.2
  18.8 0.2 dynamic-update-slice
  19.0 9.7 %all-reduce.req_ref = s32[128]{0:T(128)} all-reduce(s32[128]{0:T(128)S(1)} %dynamic-update-slice), channel_id=2, replica_groups=mesh['fact'=8,'dim'=16] {'fact'}, use_global_device_ids=true, to_apply=%add | all-reduce | flops 128 | bytes 1024 | tf_op jit(solution)/shard_map/all_gather | solution.py:287
  28.7 0.0 copy-done.2
  28.7 259.3 %shard_map.93 = (bf16[256,1024]{1,0:T(8,128)(2,1)}, bf16[256,1024]{1,0:T(8,128)(2,1)}, bf16[128,128,256]{2,1,0:T(8,128)(2,1)}) custom-call(s32[16]{0:T(128)} %get-tuple-element.15.pick_ref, s32[2,8]{1,0:T(2,128)} %copy-done.2, s32[2]{0:T(128)} %length_ref.1, s32[2,16]{1,0:T(2,128)} %get-tuple-element.16.slot_ref, bf16[8,128,1024]{2,1,0:T(8,128)(2,1)} %bitcast.4, ...), custom_call_target="tpu_custom_call" | custom-call | tf_op jit(solution)/shard_map/pallas_call | solution.py:193
  288.0 0.0 copy-start.1
  288.0 0.0 copy-start
  288.0 7.7 %shard_map.94 = (bf16[1024,128]{1,0:T(8,128)(2,1)}, bf16[1024,128]{1,0:T(8,128)(2,1)}) custom-call(s32[128]{0:T(128)} %all-reduce.req_ref, bf16[128,128,256]{2,1,0:T(8,128)(2,1)} %get-tuple-element.11.piece_ref), custom_call_target="tpu_custom_call" | custom-call | tf_op jit(solution)/shard_map/pallas_call | solution.py:245
  295.7 0.0 copy-done.1
  295.7 0.8 copy.16
  296.5 0.0 copy-done
  296.5 0.8 copy.17
  (1 shorter events, 0.0 us)
Async XLA Ops:
  2.1 26.6 %copy-start.2 = (s32[2,8]{1,0:T(2,128)}, s32[2,8]{1,0:T(2,128)S(1)}, u32[]{:S(2)}) copy-start(s32[2,8]{1,0:T(2,128)S(1)} %get-tuple-element.19.owner_ref) | copy-start | bytes 196
  3.4 14.2 %all-to-all-start = ((s32[16,1,1]{2,1,0:T(1,128)}), s32[16,1,1]{2,1,0:T(1,128)S(1)}, u32[]{:S(2)}, u32[]{:S(2)}) async-start(s32[16,1,1]{2,1,0:T(1,128)} %copy.12), calls=%async_computation | async-start | bytes 16384 | tf_op jit(solution)/shard_map/all_to_all | solution.py:268
  288.0 7.8 %copy-start.1 = (bf16[256,1024]{1,0:T(8,128)(2,1)S(1)}, bf16[256,1024]{1,0:T(8,128)(2,1)}, u32[]{:S(2)}) copy-start(bf16[256,1024]{1,0:T(8,128)(2,1)} %get-tuple-element.24) | copy-start | bytes 1572868
  288.0 8.6 %copy-start = (bf16[256,1024]{1,0:T(8,128)(2,1)S(1)}, bf16[256,1024]{1,0:T(8,128)(2,1)}, u32[]{:S(2)}) copy-start(bf16[256,1024]{1,0:T(8,128)(2,1)} %get-tuple-element.25) | copy-start | bytes 1572868

commit v8 on v6

--- a/solution.py
+++ b/solution.py
@@ -217,11 +217,13 @@
     owner_ids = jnp.arange(owners, dtype=jnp.int32)
     matched = (owner_of[:, :, None] == owner_ids[None, None, :]) & alive_slots[:, :, None]
     wanted = jnp.max(jnp.where(matched, local_of[:, :, None], -1), axis=(0, 1))
-    requests = lax.all_to_all(
-        wanted.reshape(owners, 1), "dim", split_axis=0, concat_axis=0, tiled=True
-    )
+    everyone = lax.all_gather(wanted, ("fact", "dim"), tiled=False)
+    me = lax.axis_index("dim")
+    fact = lax.axis_index("fact")
+    column = lax.dynamic_slice_in_dim(everyone, me, 1, axis=1).reshape(everyone.shape[0])
+    requests = lax.dynamic_slice_in_dim(column, fact * owners, owners)
     block_ids = jnp.arange(blocks_here, dtype=jnp.int32)[None, :]
-    picks = jnp.clip(requests.reshape(owners), 0, blocks_here - 1)
+    picks = jnp.clip(requests, 0, blocks_here - 1)
     slot_ids = jnp.arange(slot_count, dtype=jnp.int32)[None, :, None]
     live_match = (owner_of[:, :, None] == owner_ids[None, None, :]) & alive_slots[:, :, None]
     slot_of = jnp.min(jnp.where(live_match, slot_ids, slot_count), axis=1)
@@ -241,7 +243,7 @@
         partial_grads.reshape(fact_count * owners, TILE, 2 * span),
         ("fact", "dim"), split_axis=0, concat_axis=0, tiled=True,
     )
-    all_requests = lax.all_gather(requests.reshape(owners), "fact", tiled=True)
+    all_requests = column
     key_grad_out, value_grad_out = sum_pieces(all_requests, pieces, blocks_here)
     return (
         attended_out,

time: 252 us -> 307 us (1.22)
  waiting for transfers between devices: 4.04 us -> 105 us
  blocking collectives: 114 us -> 65.8 us
    all_to_all x1, waiting for transfers between devices: 4.04 us -> 105 us  [body(): lax.all_to_all(partial_grads.reshape(fact_count * owners, TILE, 2 * span)...]
    all_gather x1 -> x0, blocking collectives: 100 us -> none  [body(): all_requests = lax.all_gather(requests.reshape(owners), 'fact', tiled=True)]
    unnamed x0 -> x1, blocking collectives: none -> 65.8 us
    all_to_all x1 -> x0, blocking collectives: 14 us -> none  [body(): lax.all_to_all(wanted.reshape(owners, 1), 'dim', split_axis=0, concat_axi...]
where the time goes in v8:
time: 307 us
  Pallas kernels  120 us (39%)
  waiting for transfers between devices  105 us (34%)
  blocking collectives  65.8 us (21%)
  starting transfers between devices  9.48 us (3%)
    pallas_call x1, Pallas kernels, fetch_attend(): pl.pallas_call(fetch_attend_kernel, grid_spec=grid_spec, out_shape=[jax.S...  112 us
    all_to_all x1, waiting for transfers between devices, body(): lax.all_to_all(partial_grads.reshape(fact_count * owners, TILE, 2 * span)...  105 us
    unnamed x1, blocking collectives  65.8 us
    all_to_all x1, starting transfers between devices, body(): lax.all_to_all(partial_grads.reshape(fact_count * owners, TILE, 2 * span)...  9.48 us
    pallas_call x1, Pallas kernels, sum_pieces(): pl.pallas_call(sum_kernel, grid_spec=grid_spec, out_shape=[jax.ShapeDtype...  7.82 us
  transfers between devices with their start and end apart: 1, of which 1 were waited for; matrix products, arithmetic and copies ran while one was open for 0% of the time, Pallas kernels for 0%

profile of v8, /device:TPU:32, one launch (start us, length us, event | category | flops | bytes accessed | tf_op | source)
XLA Modules:
  0.0 306.9 jit_solution(2602691136146246234)
XLA Ops:
  0.6 0.7 iota_compare_fusion.1
  1.4 0.7 and_select_fusion
  2.1 0.0 copy-start.2
  2.1 0.7 select_reduce_fusion
  2.7 0.2 dynamic-update-slice
  2.9 65.8 %all-reduce = s32[2048]{0:T(1024)S(1)} all-reduce(s32[2048]{0:T(1024)S(1)} %dynamic-update-slice), channel_id=2, replica_groups=mesh['fact'=8,'dim'=16] {'fact','dim'}, use_global_device_ids=true, to_apply=%add | all-reduce | flops 2048 | bytes 16384
  68.7 0.1 reshape.51
  68.8 0.7 clamp_reduce_fusion.pick_ref
  69.5 0.0 copy-done.2
  69.5 112.4 %shard_map.93 = (bf16[256,1024]{1,0:T(8,128)(2,1)}, bf16[256,1024]{1,0:T(8,128)(2,1)}, bf16[8,16,128,256]{3,2,1,0:T(8,128)(2,1)}) custom-call(s32[16]{0:T(128)} %clamp_reduce_fusion.pick_ref, s32[2,8]{1,0:T(2,128)} %copy-done.2, s32[2]{0:T(128)} %length_ref.1, s32[2,16]{1,0:T(2,128)} %get-tuple-element.14.slot_ref, bf16[8,128,1024]{2,1,0:T(8,128)(2,1)} %bitcast.4, ...), custom_call_target="tpu_custom_call" | custom-call | tf_op jit(solution)/shard_map/pallas_call | solution.py:145
  182.0 9.5 %all-to-all-start = ((bf16[128,128,256]{2,1,0:T(8,128)(2,1)}), bf16[128,128,256]{2,1,0:T(8,128)(2,1)}, u32[]{:S(2)}, u32[]{:S(2)}) async-start(bf16[128,128,256]{2,1,0:T(8,128)(2,1)} %bitcast.3), calls=%async_computation | async-start | bytes 16777216 | tf_op jit(solution)/shard_map/all_to_all | solution.py:242
  191.4 0.0 copy-start.1
  191.5 0.0 copy-start
  191.5 0.7 dynamic-slice_reduce_fusion.req_ref
  192.2 105.3 %all-to-all-done.piece_ref = bf16[128,128,256]{2,1,0:T(8,128)(2,1)} async-done(((bf16[128,128,256]{2,1,0:T(8,128)(2,1)}), bf16[128,128,256]{2,1,0:T(8,128)(2,1)}, u32[]{:S(2)}, u32[]{:S(2)}) %all-to-all-start) | async-done | bytes 8388640 | tf_op jit(solution)/shard_map/all_to_all | solution.py:242
  297.4 7.8 %shard_map.94 = (bf16[1024,128]{1,0:T(8,128)(2,1)}, bf16[1024,128]{1,0:T(8,128)(2,1)}) custom-call(s32[128]{0:T(128)} %dynamic-slice_reduce_fusion.req_ref, bf16[128,128,256]{2,1,0:T(8,128)(2,1)} %all-to-all-done.piece_ref), custom_call_target="tpu_custom_call" | custom-call | tf_op jit(solution)/shard_map/pallas_call | solution.py:197
  305.3 0.0 copy-done.1
  305.3 0.8 copy.13
  306.1 0.0 copy-done
  306.1 0.8 copy.14
  (1 shorter events, 0.0 us)
Async XLA Ops:
  2.1 67.5 %copy-start.2 = (s32[2,8]{1,0:T(2,128)}, s32[2,8]{1,0:T(2,128)S(1)}, u32[]{:S(2)}) copy-start(s32[2,8]{1,0:T(2,128)S(1)} %get-tuple-element.17.owner_ref) | copy-start | bytes 196
  182.0 115.5 %all-to-all-start = ((bf16[128,128,256]{2,1,0:T(8,128)(2,1)}), bf16[128,128,256]{2,1,0:T(8,128)(2,1)}, u32[]{:S(2)}, u32[]{:S(2)}) async-start(bf16[128,128,256]{2,1,0:T(8,128)(2,1)} %bitcast.3), calls=%async_computation | async-start | bytes 16777216 | tf_op jit(solution)/shard_map/all_to_all | solution.py:242
  191.4 113.8 %copy-start.1 = (bf16[256,1024]{1,0:T(8,128)(2,1)S(1)}, bf16[256,1024]{1,0:T(8,128)(2,1)}, u32[]{:S(2)}) copy-start(bf16[256,1024]{1,0:T(8,128)(2,1)} %get-tuple-element.22) | copy-start | bytes 1572868
  191.5 114.6 %copy-start = (bf16[256,1024]{1,0:T(8,128)(2,1)S(1)}, bf16[256,1024]{1,0:T(8,128)(2,1)}, u32[]{:S(2)}) copy-start(bf16[256,1024]{1,0:T(8,128)(2,1)} %get-tuple-element.23) | copy-start | bytes 1572868

commit v9 on v6

--- a/solution.py
+++ b/solution.py
@@ -51,8 +51,8 @@
 
 
 def fetch_attend_kernel(pick_ref, owner_ref, length_ref, slot_ref, k_ref, v_ref, q_ref, g_ref,
-                        att_ref, qg_ref, grad_ref,
-                        stage, kbuf, vbuf, gbuf, send_sem, recv_sem, *recv):
+                        att_ref, qg_ref, kgrad_ref, vgrad_ref,
+                        stage, kbuf, vbuf, gbuf, gsend, send_sem, recv_sem, out_sem, *recv):
     owners = stage.shape[1]
     pairs = stage.shape[0]
     tiles = q_ref.shape[0] // TILE
@@ -115,10 +115,15 @@
             total = gbuf[0, slot_ref[0, owner]]
             for t in range(1, tiles):
                 total = total + gbuf[t, slot_ref[t, owner]]
-            grad_ref[hp, owner] = total.astype(grad_ref.dtype)
+            gsend[hp, owner, 0] = total[:, :PAIR].astype(gsend.dtype)
+            gsend[hp, owner, 1] = total[:, PAIR:].astype(gsend.dtype)
+        for plane, dst in enumerate((kgrad_ref, vgrad_ref)):
+            pltpu.make_async_copy(gsend.at[hp, :, plane], dst.at[hp], out_sem.at[hp, plane]).start()
     for hp in range(pairs):
         for k in range(1, owners):
             remote(hp, k, me).wait_send()
+        for plane, dst in enumerate((kgrad_ref, vgrad_ref)):
+            pltpu.make_async_copy(gsend.at[hp, :, plane], dst.at[hp], out_sem.at[hp, plane]).wait()
 
 
 def fetch_attend(picks, owner_of, tile_lengths, slot_of, key_blocks, value_blocks, queries, cotangent):
@@ -132,14 +137,16 @@
         num_scalar_prefetch=4,
         grid=(1,),
         in_specs=[whole] * 4,
-        out_specs=[whole] * 3,
+        out_specs=[whole, whole, pl.BlockSpec(memory_space=pl.ANY), pl.BlockSpec(memory_space=pl.ANY)],
         scratch_shapes=[
             pltpu.VMEM((pairs, owners, 2, TILE, PAIR), jnp.bfloat16),
             pltpu.VMEM((slots * TILE, PAIR), jnp.bfloat16),
             pltpu.VMEM((slots * TILE, PAIR), jnp.bfloat16),
             pltpu.VMEM((rows // TILE, slots + 1, TILE, 2 * PAIR), jnp.float32),
+            pltpu.VMEM((pairs, owners, 2, TILE, PAIR), jnp.bfloat16),
             pltpu.SemaphoreType.DMA((pairs, owners)),
             pltpu.SemaphoreType.DMA((pairs, owners)),
+            pltpu.SemaphoreType.DMA((pairs, 2)),
         ] + [pltpu.VMEM((owners, 2, TILE, PAIR), jnp.bfloat16) for _ in range(pairs)],
     )
     return pl.pallas_call(
@@ -148,7 +155,8 @@
         out_shape=[
             jax.ShapeDtypeStruct((rows, width), jnp.bfloat16),
             jax.ShapeDtypeStruct((rows, width), jnp.bfloat16),
-            jax.ShapeDtypeStruct((pairs, owners, TILE, 2 * PAIR), jnp.bfloat16),
+            jax.ShapeDtypeStruct((pairs, owners, TILE, PAIR), jnp.bfloat16),
+            jax.ShapeDtypeStruct((pairs, owners, TILE, PAIR), jnp.bfloat16),
         ],
         compiler_params=pltpu.CompilerParams(
             collective_id=0, has_side_effects=True, vmem_limit_bytes=60 * 1024 * 1024
@@ -156,10 +164,9 @@
     )(picks, owner_of, tile_lengths, slot_of, key_blocks, value_blocks, queries, cotangent)
 
 
-def sum_kernel(req_ref, piece_ref, key_out, value_out, acc):
+def sum_kernel(req_ref, piece_ref, out_ref, acc):
     step = pl.program_id(0)
     chunk = piece_ref.shape[0]
-    span = key_out.shape[1]
     rows = piece_ref.shape[1]
 
     @pl.when(step == 0)
@@ -176,31 +183,23 @@
     @pl.when(step == pl.num_programs(0) - 1)
     def _():
         for l in range(acc.shape[0]):
-            key_out[pl.ds(l * rows, rows), :] = acc[l, :, :span].astype(key_out.dtype)
-            value_out[pl.ds(l * rows, rows), :] = acc[l, :, span:].astype(value_out.dtype)
+            out_ref[pl.ds(l * rows, rows), :] = acc[l].astype(out_ref.dtype)
 
 
 def sum_pieces(all_requests, pieces, blocks):
-    sources, rows, both = pieces.shape
-    span = both // 2
+    sources, rows, span = pieces.shape
     chunk = 16
     grid_spec = pltpu.PrefetchScalarGridSpec(
         num_scalar_prefetch=1,
         grid=(sources // chunk,),
-        in_specs=[pl.BlockSpec((chunk, rows, both), lambda i, req: (i, 0, 0))],
-        out_specs=[
-            pl.BlockSpec((blocks * rows, span), lambda i, req: (0, 0)),
-            pl.BlockSpec((blocks * rows, span), lambda i, req: (0, 0)),
-        ],
-        scratch_shapes=[pltpu.VMEM((blocks, rows, both), jnp.float32)],
+        in_specs=[pl.BlockSpec((chunk, rows, span), lambda i, req: (i, 0, 0))],
+        out_specs=pl.BlockSpec((blocks * rows, span), lambda i, req: (0, 0)),
+        scratch_shapes=[pltpu.VMEM((blocks, rows, span), jnp.float32)],
     )
     return pl.pallas_call(
         sum_kernel,
         grid_spec=grid_spec,
-        out_shape=[
-            jax.ShapeDtypeStruct((blocks * rows, span), jnp.bfloat16),
-            jax.ShapeDtypeStruct((blocks * rows, span), jnp.bfloat16),
-        ],
+        out_shape=jax.ShapeDtypeStruct((blocks * rows, span), jnp.bfloat16),
         compiler_params=pltpu.CompilerParams(dimension_semantics=("arbitrary",)),
     )(all_requests, pieces)
 
@@ -225,7 +224,7 @@
     slot_ids = jnp.arange(slot_count, dtype=jnp.int32)[None, :, None]
     live_match = (owner_of[:, :, None] == owner_ids[None, None, :]) & alive_slots[:, :, None]
     slot_of = jnp.min(jnp.where(live_match, slot_ids, slot_count), axis=1)
-    attended_out, query_grad_out, partial_grads = fetch_attend(
+    attended_out, query_grad_out, key_parts, value_parts = fetch_attend(
         picks,
         owner_of,
         tile_lengths,
@@ -237,12 +236,17 @@
     )
     fact_count = lax.axis_size("fact")
     span = model_width // fact_count
-    pieces = lax.all_to_all(
-        partial_grads.reshape(fact_count * owners, TILE, 2 * span),
+    all_requests = lax.all_gather(requests.reshape(owners), "fact", tiled=True)
+    key_pieces = lax.all_to_all(
+        key_parts.reshape(fact_count * owners, TILE, span),
         ("fact", "dim"), split_axis=0, concat_axis=0, tiled=True,
     )
-    all_requests = lax.all_gather(requests.reshape(owners), "fact", tiled=True)
-    key_grad_out, value_grad_out = sum_pieces(all_requests, pieces, blocks_here)
+    key_grad_out = sum_pieces(all_requests, key_pieces, blocks_here)
+    value_pieces = lax.all_to_all(
+        value_parts.reshape(fact_count * owners, TILE, span),
+        ("fact", "dim"), split_axis=0, concat_axis=0, tiled=True,
+    )
+    value_grad_out = sum_pieces(all_requests, value_pieces, blocks_here)
     return (
         attended_out,
         query_grad_out,

time: 252 us -> 259 us (1.028)
  blocking collectives: 114 us -> 124 us
  waiting for transfers between devices: 4.04 us -> 0.01 us
  starting transfers between devices: 8.66 us -> 5.49 us
  Pallas kernels: 118 us -> 121 us
    all_to_all x0 -> x1, blocking collectives: none -> 60.3 us  [body(): lax.all_to_all(key_parts.reshape(fact_count * owners, TILE, span), ('fact...]
    all_gather x1, blocking collectives: 100 us -> 49.7 us  [body(): all_requests = lax.all_gather(requests.reshape(owners), 'fact', tiled=True)]
    pallas_call x1 -> x2, Pallas kernels: 7.62 us -> 12.9 us  [sum_pieces(): pl.pallas_call(sum_kernel, grid_spec=grid_spec, out_shape=jax.ShapeDtypeS...]
    all_to_all x1, waiting for transfers between devices: 4.04 us -> 0.01 us  [body(): lax.all_to_all(value_parts.reshape(fact_count * owners, TILE, span), ('fa...]
    all_to_all x1, starting transfers between devices: 8.66 us -> 5.49 us  [body(): lax.all_to_all(value_parts.reshape(fact_count * owners, TILE, span), ('fa...]
  transfers between devices with their start and end apart: 1 -> 1, of which waited for: 1 -> 0; matrix products, arithmetic and copies ran while one was open for 0% -> 0% of each run, Pallas kernels for 0% -> 3%
where the time goes in v9:
time: 259 us; the launch traced here: 258 us
  blocking collectives  124 us (48%)
  Pallas kernels  121 us (47%)
  starting transfers between devices  5.49 us (2%)
  other arithmetic  3.26 us (1%)
    pallas_call x1, Pallas kernels, fetch_attend(): pl.pallas_call(fetch_attend_kernel, grid_spec=grid_spec, out_shape=[jax.S...  108 us
    all_to_all x1, blocking collectives, body(): lax.all_to_all(key_parts.reshape(fact_count * owners, TILE, span), ('fact...  60.3 us
    all_gather x1, blocking collectives, body(): all_requests = lax.all_gather(requests.reshape(owners), 'fact', tiled=True)  49.7 us
    all_to_all x1, blocking collectives, body(): lax.all_to_all(wanted.reshape(owners, 1), 'dim', split_axis=0, concat_axi...  14 us
    pallas_call x2, Pallas kernels, sum_pieces(): pl.pallas_call(sum_kernel, grid_spec=grid_spec, out_shape=jax.ShapeDtypeS...  12.9 us
    all_to_all x1, starting transfers between devices, body(): lax.all_to_all(value_parts.reshape(fact_count * owners, TILE, span), ('fa...  5.49 us
  transfers between devices with their start and end apart: 1, of which 0 were waited for; matrix products, arithmetic and copies ran while one was open for 0% of the time, Pallas kernels for 3%

profile of v9, /device:TPU:32, one launch (start us, length us, event | category | flops | bytes accessed | tf_op | source)
XLA Modules:
  0.0 258.0 jit_solution(5738183775257537412)
XLA Ops:
  0.6 0.7 iota_compare_fusion.1
  1.4 0.7 and_select_fusion
  2.1 0.0 copy-start.2
  2.1 0.7 select_reduce_fusion
  2.7 0.1 copy.12
  2.8 14.0 %all_to_all.19 = s32[16,1,1]{2,1,0:T(1,128)S(1)} all-to-all(s32[16,1,1]{2,1,0:T(1,128)S(1)} %copy.12), channel_id=1, replica_groups=mesh['fact'=8,'dim'=16] {'dim'}, dimensions={0} | all-to-all | bytes 128 | tf_op jit(solution)/shard_map/all_to_all | solution.py:219
  16.8 1.2 fusion.2
  18.0 0.0 copy-done.2
  18.0 108.5 %shard_map.93 = (bf16[256,1024]{1,0:T(8,128)(2,1)}, bf16[256,1024]{1,0:T(8,128)(2,1)}, bf16[8,16,128,128]{3,2,1,0:T(8,128)(2,1)}, bf16[8,16,128,128]{3,2,1,0:T(8,128)(2,1)}) custom-call(s32[16]{0:T(128)} %get-tuple-element.13.pick_ref, s32[2,8]{1,0:T(2,128)} %copy-done.2, s32[2]{0:T(128)} %length_ref.1, s32[2,16]{1,0:T(2,128)} %get-tuple-element.14.slot_ref, ...), custom_call_target="tpu_custom_call" | custom-call | tf_op jit(solution)/shard_map/pallas_call | solution.py:152
  126.5 60.3 %all_to_all.20.piece_ref = bf16[128,128,128]{2,1,0:T(8,128)(2,1)} all-to-all(bf16[128,128,128]{2,1,0:T(8,128)(2,1)} %bitcast.7), channel_id=1, replica_groups=mesh['fact'=8,'dim'=16] {'fact','dim'}, dimensions={0} | all-to-all | bytes 8388608 | tf_op jit(solution)/shard_map/all_to_all | solution.py:240
  186.8 0.0 copy-start.3
  186.8 5.5 %all-to-all-start.2 = ((bf16[128,128,128]{2,1,0:T(8,128)(2,1)}), bf16[128,128,128]{2,1,0:T(8,128)(2,1)}, u32[]{:S(2)}, u32[]{:S(2)}) async-start(bf16[128,128,128]{2,1,0:T(8,128)(2,1)} %bitcast.6), calls=%async_computation.2 | async-start | bytes 8388608 | tf_op jit(solution)/shard_map/all_to_all | solution.py:245
  192.3 0.0 copy-done.3
  192.3 0.6 dynamic-slice
  193.6 0.2 dynamic-update-slice
  193.8 49.7 %all-reduce.req_ref = s32[128]{0:T(128)} all-reduce(s32[128]{0:T(128)S(1)} %dynamic-update-slice), channel_id=2, replica_groups=mesh['fact'=8,'dim'=16] {'fact'}, use_global_device_ids=true, to_apply=%add | all-reduce | flops 128 | bytes 1024 | tf_op jit(solution)/shard_map/all_gather | solution.py:239
  243.5 0.0 copy-start.1
  243.5 6.5 %shard_map.94 = bf16[1024,128]{1,0:T(8,128)(2,1)} custom-call(s32[128]{0:T(128)} %all-reduce.req_ref, bf16[128,128,128]{2,1,0:T(8,128)(2,1)} %all_to_all.20.piece_ref), custom_call_target="tpu_custom_call" | custom-call | tf_op jit(solution)/shard_map/pallas_call | solution.py:199
  250.0 0.0 all-to-all-done.2.piece_ref
  250.0 6.4 %shard_map.95 = bf16[1024,128]{1,0:T(8,128)(2,1)} custom-call(s32[128]{0:T(128)} %all-reduce.req_ref, bf16[128,128,128]{2,1,0:T(8,128)(2,1)} %all-to-all-done.2.piece_ref), custom_call_target="tpu_custom_call" | custom-call | tf_op jit(solution)/shard_map/pallas_call | solution.py:199
  256.4 0.0 copy-done.1
  256.4 0.8 copy.16
  257.2 0.0 copy-done
  257.2 0.8 copy.17
  (2 shorter events, 0.0 us)
Async XLA Ops:
  2.1 16.0 %copy-start.2 = (s32[2,8]{1,0:T(2,128)}, s32[2,8]{1,0:T(2,128)S(1)}, u32[]{:S(2)}) copy-start(s32[2,8]{1,0:T(2,128)S(1)} %get-tuple-element.17.owner_ref) | copy-start | bytes 196
  186.8 5.5 %copy-start.3 = (u32[128]{0:T(128)S(1)}, u32[128]{0:T(128)}, u32[]{:S(2)}) copy-start(u32[128]{0:T(128)} %constant.41) | copy-start | bytes 1540
  186.8 63.2 %all-to-all-start.2 = ((bf16[128,128,128]{2,1,0:T(8,128)(2,1)}), bf16[128,128,128]{2,1,0:T(8,128)(2,1)}, u32[]{:S(2)}, u32[]{:S(2)}) async-start(bf16[128,128,128]{2,1,0:T(8,128)(2,1)} %bitcast.6), calls=%async_computation.2 | async-start | bytes 8388608 | tf_op jit(solution)/shard_map/all_to_all | solution.py:245
  243.5 12.9 %copy-start.1 = (bf16[256,1024]{1,0:T(8,128)(2,1)S(1)}, bf16[256,1024]{1,0:T(8,128)(2,1)}, u32[]{:S(2)}) copy-start(bf16[256,1024]{1,0:T(8,128)(2,1)} %get-tuple-element.22) | copy-start | bytes 1572868
  243.5 13.7 %copy-start = (bf16[256,1024]{1,0:T(8,128)(2,1)S(1)}, bf16[256,1024]{1,0:T(8,128)(2,1)}, u32[]{:S(2)}) copy-start(bf16[256,1024]{1,0:T(8,128)(2,1)} %get-tuple-element.23) | copy-start | bytes 1572868

commit v10 on v6

--- a/solution.py
+++ b/solution.py
@@ -166,16 +166,15 @@
     def _():
         acc[...] = jnp.zeros_like(acc)
 
+    spare = acc.shape[0] - 1
     for i in range(chunk):
         target = req_ref[step * chunk + i]
-
-        @pl.when(target >= 0)
-        def _():
-            acc[target] = acc[target] + piece_ref[i].astype(jnp.float32)
+        target = jnp.where(target < 0, spare, jnp.minimum(target, spare))
+        acc[target] = acc[target] + piece_ref[i].astype(jnp.float32)
 
     @pl.when(step == pl.num_programs(0) - 1)
     def _():
-        for l in range(acc.shape[0]):
+        for l in range(acc.shape[0] - 1):
             key_out[pl.ds(l * rows, rows), :] = acc[l, :, :span].astype(key_out.dtype)
             value_out[pl.ds(l * rows, rows), :] = acc[l, :, span:].astype(value_out.dtype)
 
@@ -183,7 +182,7 @@
 def sum_pieces(all_requests, pieces, blocks):
     sources, rows, both = pieces.shape
     span = both // 2
-    chunk = 16
+    chunk = 32
     grid_spec = pltpu.PrefetchScalarGridSpec(
         num_scalar_prefetch=1,
         grid=(sources // chunk,),
@@ -192,7 +191,7 @@
             pl.BlockSpec((blocks * rows, span), lambda i, req: (0, 0)),
             pl.BlockSpec((blocks * rows, span), lambda i, req: (0, 0)),
         ],
-        scratch_shapes=[pltpu.VMEM((blocks, rows, both), jnp.float32)],
+        scratch_shapes=[pltpu.VMEM((blocks + 1, rows, both), jnp.float32)],
     )
     return pl.pallas_call(
         sum_kernel,

time: 252 us -> 251 us (level)
  no operation moved by 1% of the time
where the time goes in v10:
time: 251 us
  Pallas kernels  116 us (46%)
  blocking collectives  114 us (45%)
  starting transfers between devices  8.66 us (3%)
  waiting for transfers between devices  4.04 us (2%)
  other arithmetic  3.26 us (1%)
  local copies, waits for them, and re-layouts  2.52 us (1%)
    pallas_call x1, Pallas kernels, fetch_attend(): pl.pallas_call(fetch_attend_kernel, grid_spec=grid_spec, out_shape=[jax.S...  110 us
    all_gather x1, blocking collectives, body(): all_requests = lax.all_gather(requests.reshape(owners), 'fact', tiled=True)  100 us
    all_to_all x1, blocking collectives, body(): lax.all_to_all(wanted.reshape(owners, 1), 'dim', split_axis=0, concat_axi...  14 us
    all_to_all x1, starting transfers between devices, body(): lax.all_to_all(partial_grads.reshape(fact_count * owners, TILE, 2 * span)...  8.66 us
    pallas_call x1, Pallas kernels, sum_pieces(): pl.pallas_call(sum_kernel, grid_spec=grid_spec, out_shape=[jax.ShapeDtype...  6.4 us
  transfers between devices with their start and end apart: 1, of which 1 were waited for; matrix products, arithmetic and copies ran while one was open for 0% of the time, Pallas kernels for 0%

profile of v10, /device:TPU:32, one launch (start us, length us, event | category | flops | bytes accessed | tf_op | source)
XLA Modules:
  0.0 250.7 jit_solution(3773230405765546541)
XLA Ops:
  0.6 0.7 iota_compare_fusion.1
  1.4 0.7 and_select_fusion
  2.1 0.0 copy-start.2
  2.1 0.7 select_reduce_fusion
  2.7 0.1 copy.12
  2.8 14.0 %all_to_all.14 = s32[16,1,1]{2,1,0:T(1,128)S(1)} all-to-all(s32[16,1,1]{2,1,0:T(1,128)S(1)} %copy.12), channel_id=1, replica_groups=mesh['fact'=8,'dim'=16] {'dim'}, dimensions={0} | all-to-all | bytes 128 | tf_op jit(solution)/shard_map/all_to_all | solution.py:219
  16.8 1.2 fusion.2
  18.0 0.0 copy-done.2
  18.0 110.0 %shard_map.93 = (bf16[256,1024]{1,0:T(8,128)(2,1)}, bf16[256,1024]{1,0:T(8,128)(2,1)}, bf16[8,16,128,256]{3,2,1,0:T(8,128)(2,1)}) custom-call(s32[16]{0:T(128)} %get-tuple-element.15.pick_ref, s32[2,8]{1,0:T(2,128)} %copy-done.2, s32[2]{0:T(128)} %length_ref.1, s32[2,16]{1,0:T(2,128)} %get-tuple-element.16.slot_ref, bf16[8,128,1024]{2,1,0:T(8,128)(2,1)} %bitcast.6, ...), custom_call_target="tpu_custom_call" | custom-call | tf_op jit(solution)/shard_map/pallas_call | solution.py:145
  128.1 0.0 copy-start.3
  128.1 8.7 %all-to-all-start.1 = ((bf16[128,128,256]{2,1,0:T(8,128)(2,1)}), bf16[128,128,256]{2,1,0:T(8,128)(2,1)}, u32[]{:S(2)}, u32[]{:S(2)}) async-start(bf16[128,128,256]{2,1,0:T(8,128)(2,1)} %bitcast.5), calls=%async_computation.1 | async-start | bytes 16777216 | tf_op jit(solution)/shard_map/all_to_all | solution.py:239
  136.8 0.0 copy-start.1
  136.8 0.0 copy-start
  136.8 0.0 copy-done.3
  136.8 0.6 dynamic-slice
  138.0 0.2 dynamic-update-slice
  138.3 100.4 %all-reduce.req_ref = s32[128]{0:T(128)} all-reduce(s32[128]{0:T(128)S(1)} %dynamic-update-slice), channel_id=2, replica_groups=mesh['fact'=8,'dim'=16] {'fact'}, use_global_device_ids=true, to_apply=%add | all-reduce | flops 128 | bytes 1024 | tf_op jit(solution)/shard_map/all_gather | solution.py:243
  238.7 4.0 %all-to-all-done.1.piece_ref = bf16[128,128,256]{2,1,0:T(8,128)(2,1)} async-done(((bf16[128,128,256]{2,1,0:T(8,128)(2,1)}), bf16[128,128,256]{2,1,0:T(8,128)(2,1)}, u32[]{:S(2)}, u32[]{:S(2)}) %all-to-all-start.1) | async-done | bytes 8388640 | tf_op jit(solution)/shard_map/all_to_all | solution.py:239
  242.8 6.4 %shard_map.94 = (bf16[1024,128]{1,0:T(8,128)(2,1)}, bf16[1024,128]{1,0:T(8,128)(2,1)}) custom-call(s32[128]{0:T(128)} %all-reduce.req_ref, bf16[128,128,256]{2,1,0:T(8,128)(2,1)} %all-to-all-done.1.piece_ref), custom_call_target="tpu_custom_call" | custom-call | tf_op jit(solution)/shard_map/pallas_call | solution.py:196
  249.2 0.0 copy-done.1
  249.2 0.8 copy.16
  249.9 0.0 copy-done
  250.0 0.8 copy.17
  (1 shorter events, 0.0 us)
Async XLA Ops:
  2.1 16.0 %copy-start.2 = (s32[2,8]{1,0:T(2,128)}, s32[2,8]{1,0:T(2,128)S(1)}, u32[]{:S(2)}) copy-start(s32[2,8]{1,0:T(2,128)S(1)} %get-tuple-element.19.owner_ref) | copy-start | bytes 196
  128.1 8.7 %copy-start.3 = (u32[128]{0:T(128)S(1)}, u32[128]{0:T(128)}, u32[]{:S(2)}) copy-start(u32[128]{0:T(128)} %constant.41) | copy-start | bytes 1540
  128.1 114.7 %all-to-all-start.1 = ((bf16[128,128,256]{2,1,0:T(8,128)(2,1)}), bf16[128,128,256]{2,1,0:T(8,128)(2,1)}, u32[]{:S(2)}, u32[]{:S(2)}) async-start(bf16[128,128,256]{2,1,0:T(8,128)(2,1)} %bitcast.5), calls=%async_computation.1 | async-start | bytes 16777216 | tf_op jit(solution)/shard_map/all_to_all | solution.py:239
  136.8 112.4 %copy-start.1 = (bf16[256,1024]{1,0:T(8,128)(2,1)S(1)}, bf16[256,1024]{1,0:T(8,128)(2,1)}, u32[]{:S(2)}) copy-start(bf16[256,1024]{1,0:T(8,128)(2,1)} %get-tuple-element.24) | copy-start | bytes 1572868
  136.8 113.2 %copy-start = (bf16[256,1024]{1,0:T(8,128)(2,1)S(1)}, bf16[256,1024]{1,0:T(8,128)(2,1)}, u32[]{:S(2)}) copy-start(bf16[256,1024]{1,0:T(8,128)(2,1)} %get-tuple-element.25) | copy-start | bytes 1572868

commit v11 on v10

--- a/solution.py
+++ b/solution.py
@@ -52,7 +52,7 @@
 
 def fetch_attend_kernel(pick_ref, owner_ref, length_ref, slot_ref, k_ref, v_ref, q_ref, g_ref,
                         att_ref, qg_ref, grad_ref,
-                        stage, kbuf, vbuf, gbuf, send_sem, recv_sem, *recv):
+                        stage, kbuf, vbuf, gbuf, gsend, send_sem, recv_sem, out_sem, *recv):
     owners = stage.shape[1]
     pairs = stage.shape[0]
     tiles = q_ref.shape[0] // TILE
@@ -115,10 +115,12 @@
             total = gbuf[0, slot_ref[0, owner]]
             for t in range(1, tiles):
                 total = total + gbuf[t, slot_ref[t, owner]]
-            grad_ref[hp, owner] = total.astype(grad_ref.dtype)
+            gsend[hp, owner] = total.astype(gsend.dtype)
+        pltpu.make_async_copy(gsend.at[hp], grad_ref.at[hp], out_sem.at[hp]).start()
     for hp in range(pairs):
         for k in range(1, owners):
             remote(hp, k, me).wait_send()
+        pltpu.make_async_copy(gsend.at[hp], grad_ref.at[hp], out_sem.at[hp]).wait()
 
 
 def fetch_attend(picks, owner_of, tile_lengths, slot_of, key_blocks, value_blocks, queries, cotangent):
@@ -132,14 +134,16 @@
         num_scalar_prefetch=4,
         grid=(1,),
         in_specs=[whole] * 4,
-        out_specs=[whole] * 3,
+        out_specs=[whole, whole, pl.BlockSpec(memory_space=pl.ANY)],
         scratch_shapes=[
             pltpu.VMEM((pairs, owners, 2, TILE, PAIR), jnp.bfloat16),
             pltpu.VMEM((slots * TILE, PAIR), jnp.bfloat16),
             pltpu.VMEM((slots * TILE, PAIR), jnp.bfloat16),
             pltpu.VMEM((rows // TILE, slots + 1, TILE, 2 * PAIR), jnp.float32),
+            pltpu.VMEM((pairs, owners, TILE, 2 * PAIR), jnp.bfloat16),
             pltpu.SemaphoreType.DMA((pairs, owners)),
             pltpu.SemaphoreType.DMA((pairs, owners)),
+            pltpu.SemaphoreType.DMA((pairs,)),
         ] + [pltpu.VMEM((owners, 2, TILE, PAIR), jnp.bfloat16) for _ in range(pairs)],
     )
     return pl.pallas_call(

time: 251 us -> 249 us (level)
  no operation moved by 1% of the time
where the time goes in v11:
time: 249 us
  Pallas kernels  115 us (46%)
  blocking collectives  114 us (46%)
  starting transfers between devices  8.68 us (3%)
  waiting for transfers between devices  4.04 us (2%)
  other arithmetic  3.26 us (1%)
  local copies, waits for them, and re-layouts  2.52 us (1%)
    pallas_call x1, Pallas kernels, fetch_attend(): pl.pallas_call(fetch_attend_kernel, grid_spec=grid_spec, out_shape=[jax.S...  108 us
    all_gather x1, blocking collectives, body(): all_requests = lax.all_gather(requests.reshape(owners), 'fact', tiled=True)  100 us
    all_to_all x1, blocking collectives, body(): lax.all_to_all(wanted.reshape(owners, 1), 'dim', split_axis=0, concat_axi...  14 us
    all_to_all x1, starting transfers between devices, body(): lax.all_to_all(partial_grads.reshape(fact_count * owners, TILE, 2 * span)...  8.68 us
    pallas_call x1, Pallas kernels, sum_pieces(): pl.pallas_call(sum_kernel, grid_spec=grid_spec, out_shape=[jax.ShapeDtype...  6.4 us
  transfers between devices with their start and end apart: 1, of which 1 were waited for; matrix products, arithmetic and copies ran while one was open for 0% of the time, Pallas kernels for 0%

profile of v11, /device:TPU:32, one launch (start us, length us, event | category | flops | bytes accessed | tf_op | source)
XLA Modules:
  0.0 249.1 jit_solution(9579689824757769367)
XLA Ops:
  0.6 0.7 iota_compare_fusion.1
  1.4 0.7 and_select_fusion
  2.1 0.0 copy-start.2
  2.1 0.7 select_reduce_fusion
  2.7 0.1 copy.12
  2.8 14.0 %all_to_all.14 = s32[16,1,1]{2,1,0:T(1,128)S(1)} all-to-all(s32[16,1,1]{2,1,0:T(1,128)S(1)} %copy.12), channel_id=1, replica_groups=mesh['fact'=8,'dim'=16] {'dim'}, dimensions={0} | all-to-all | bytes 128 | tf_op jit(solution)/shard_map/all_to_all | solution.py:223
  16.8 1.2 fusion.2
  18.0 0.0 copy-done.2
  18.0 108.3 %shard_map.93 = (bf16[256,1024]{1,0:T(8,128)(2,1)}, bf16[256,1024]{1,0:T(8,128)(2,1)}, bf16[8,16,128,256]{3,2,1,0:T(8,128)(2,1)}) custom-call(s32[16]{0:T(128)} %get-tuple-element.15.pick_ref, s32[2,8]{1,0:T(2,128)} %copy-done.2, s32[2]{0:T(128)} %length_ref.1, s32[2,16]{1,0:T(2,128)} %get-tuple-element.16.slot_ref, bf16[8,128,1024]{2,1,0:T(8,128)(2,1)} %bitcast.6, ...), custom_call_target="tpu_custom_call" | custom-call | tf_op jit(solution)/shard_map/pallas_call | solution.py:149
  126.4 0.0 copy-start.3
  126.4 8.7 %all-to-all-start.1 = ((bf16[128,128,256]{2,1,0:T(8,128)(2,1)}), bf16[128,128,256]{2,1,0:T(8,128)(2,1)}, u32[]{:S(2)}, u32[]{:S(2)}) async-start(bf16[128,128,256]{2,1,0:T(8,128)(2,1)} %bitcast.5), calls=%async_computation.1 | async-start | bytes 16777216 | tf_op jit(solution)/shard_map/all_to_all | solution.py:243
  135.1 0.0 copy-start.1
  135.1 0.0 copy-start
  135.1 0.0 copy-done.3
  135.1 0.6 dynamic-slice
  136.3 0.2 dynamic-update-slice
  136.6 100.4 %all-reduce.req_ref = s32[128]{0:T(128)} all-reduce(s32[128]{0:T(128)S(1)} %dynamic-update-slice), channel_id=2, replica_groups=mesh['fact'=8,'dim'=16] {'fact'}, use_global_device_ids=true, to_apply=%add | all-reduce | flops 128 | bytes 1024 | tf_op jit(solution)/shard_map/all_gather | solution.py:247
  237.0 4.0 %all-to-all-done.1.piece_ref = bf16[128,128,256]{2,1,0:T(8,128)(2,1)} async-done(((bf16[128,128,256]{2,1,0:T(8,128)(2,1)}), bf16[128,128,256]{2,1,0:T(8,128)(2,1)}, u32[]{:S(2)}, u32[]{:S(2)}) %all-to-all-start.1) | async-done | bytes 8388640 | tf_op jit(solution)/shard_map/all_to_all | solution.py:243
  241.1 6.4 %shard_map.94 = (bf16[1024,128]{1,0:T(8,128)(2,1)}, bf16[1024,128]{1,0:T(8,128)(2,1)}) custom-call(s32[128]{0:T(128)} %all-reduce.req_ref, bf16[128,128,256]{2,1,0:T(8,128)(2,1)} %all-to-all-done.1.piece_ref), custom_call_target="tpu_custom_call" | custom-call | tf_op jit(solution)/shard_map/pallas_call | solution.py:200
  247.5 0.0 copy-done.1
  247.5 0.8 copy.16
  248.3 0.0 copy-done
  248.3 0.8 copy.17
  (1 shorter events, 0.0 us)
Async XLA Ops:
  2.1 16.0 %copy-start.2 = (s32[2,8]{1,0:T(2,128)}, s32[2,8]{1,0:T(2,128)S(1)}, u32[]{:S(2)}) copy-start(s32[2,8]{1,0:T(2,128)S(1)} %get-tuple-element.19.owner_ref) | copy-start | bytes 196
  126.4 8.7 %copy-start.3 = (u32[128]{0:T(128)S(1)}, u32[128]{0:T(128)}, u32[]{:S(2)}) copy-start(u32[128]{0:T(128)} %constant.41) | copy-start | bytes 1540
  126.4 114.7 %all-to-all-start.1 = ((bf16[128,128,256]{2,1,0:T(8,128)(2,1)}), bf16[128,128,256]{2,1,0:T(8,128)(2,1)}, u32[]{:S(2)}, u32[]{:S(2)}) async-start(bf16[128,128,256]{2,1,0:T(8,128)(2,1)} %bitcast.5), calls=%async_computation.1 | async-start | bytes 16777216 | tf_op jit(solution)/shard_map/all_to_all | solution.py:243
  135.1 112.4 %copy-start.1 = (bf16[256,1024]{1,0:T(8,128)(2,1)S(1)}, bf16[256,1024]{1,0:T(8,128)(2,1)}, u32[]{:S(2)}) copy-start(bf16[256,1024]{1,0:T(8,128)(2,1)} %get-tuple-element.24) | copy-start | bytes 1572868
  135.1 113.2 %copy-start = (bf16[256,1024]{1,0:T(8,128)(2,1)S(1)}, bf16[256,1024]{1,0:T(8,128)(2,1)}, u32[]{:S(2)}) copy-start(bf16[256,1024]{1,0:T(8,128)(2,1)} %get-tuple-element.25) | copy-start | bytes 1572868

commit v12 on v11

--- a/solution.py
+++ b/solution.py
@@ -60,17 +60,20 @@
     me = lax.axis_index("dim")
     fact = lax.axis_index("fact")
     mesh = pl.DeviceIdType.MESH
+    mine = pick_ref[me]
+    for hp in range(pairs):
+        cols = pl.ds(hp * PAIR, PAIR)
+        recv[hp][me, 0] = k_ref[mine, :, cols]
+        recv[hp][me, 1] = v_ref[mine, :, cols]
+    barrier = pltpu.get_barrier_semaphore()
+    for k in range(1, owners):
+        pl.semaphore_signal(barrier, inc=1, device_id=(fact, lax.rem(me + k, owners)), device_id_type=mesh)
     for hp in range(pairs):
         cols = pl.ds(hp * PAIR, PAIR)
         for peer in range(owners):
             chosen = pick_ref[peer]
             stage[hp, peer, 0] = k_ref[chosen, :, cols]
             stage[hp, peer, 1] = v_ref[chosen, :, cols]
-    for hp in range(pairs):
-        recv[hp][me] = stage[hp, me]
-    barrier = pltpu.get_barrier_semaphore()
-    for k in range(1, owners):
-        pl.semaphore_signal(barrier, inc=1, device_id=(fact, lax.rem(me + k, owners)), device_id_type=mesh)
     pl.semaphore_wait(barrier, owners - 1)
 
     def remote(hp, k, src):

time: 249 us -> 248 us (level)
  no operation moved by 1% of the time
where the time goes in v12:
time: 248 us; the launch traced here: 247 us
  blocking collectives  114 us (46%)
  Pallas kernels  113 us (46%)
  starting transfers between devices  8.92 us (4%)
  waiting for transfers between devices  4.04 us (2%)
  other arithmetic  3.26 us (1%)
  local copies, waits for them, and re-layouts  2.52 us (1%)
    pallas_call x1, Pallas kernels, fetch_attend(): pl.pallas_call(fetch_attend_kernel, grid_spec=grid_spec, out_shape=[jax.S...  106 us
    all_gather x1, blocking collectives, body(): all_requests = lax.all_gather(requests.reshape(owners), 'fact', tiled=True)  100 us
    all_to_all x1, blocking collectives, body(): lax.all_to_all(wanted.reshape(owners, 1), 'dim', split_axis=0, concat_axi...  14 us
    all_to_all x1, starting transfers between devices, body(): lax.all_to_all(partial_grads.reshape(fact_count * owners, TILE, 2 * span)...  8.92 us
    pallas_call x1, Pallas kernels, sum_pieces(): pl.pallas_call(sum_kernel, grid_spec=grid_spec, out_shape=[jax.ShapeDtype...  6.4 us
  transfers between devices with their start and end apart: 1, of which 1 were waited for; matrix products, arithmetic and copies ran while one was open for 0% of the time, Pallas kernels for 0%

profile of v12, /device:TPU:32, one launch (start us, length us, event | category | flops | bytes accessed | tf_op | source)
XLA Modules:
  0.0 247.3 jit_solution(9916752633268645955)
XLA Ops:
  0.6 0.7 iota_compare_fusion.1
  1.4 0.7 and_select_fusion
  2.1 0.0 copy-start.2
  2.1 0.7 select_reduce_fusion
  2.7 0.1 copy.12
  2.8 14.0 %all_to_all.14 = s32[16,1,1]{2,1,0:T(1,128)S(1)} all-to-all(s32[16,1,1]{2,1,0:T(1,128)S(1)} %copy.12), channel_id=1, replica_groups=mesh['fact'=8,'dim'=16] {'dim'}, dimensions={0} | all-to-all | bytes 128 | tf_op jit(solution)/shard_map/all_to_all | solution.py:226
  16.8 1.2 fusion.2
  18.0 0.0 copy-done.2
  18.0 106.4 %shard_map.93 = (bf16[256,1024]{1,0:T(8,128)(2,1)}, bf16[256,1024]{1,0:T(8,128)(2,1)}, bf16[8,16,128,256]{3,2,1,0:T(8,128)(2,1)}) custom-call(s32[16]{0:T(128)} %get-tuple-element.15.pick_ref, s32[2,8]{1,0:T(2,128)} %copy-done.2, s32[2]{0:T(128)} %length_ref.1, s32[2,16]{1,0:T(2,128)} %get-tuple-element.16.slot_ref, bf16[8,128,1024]{2,1,0:T(8,128)(2,1)} %bitcast.6, ...), custom_call_target="tpu_custom_call" | custom-call | tf_op jit(solution)/shard_map/pallas_call | solution.py:152
  124.4 0.0 copy-start.3
  124.4 8.9 %all-to-all-start.1 = ((bf16[128,128,256]{2,1,0:T(8,128)(2,1)}), bf16[128,128,256]{2,1,0:T(8,128)(2,1)}, u32[]{:S(2)}, u32[]{:S(2)}) async-start(bf16[128,128,256]{2,1,0:T(8,128)(2,1)} %bitcast.5), calls=%async_computation.1 | async-start | bytes 16777216 | tf_op jit(solution)/shard_map/all_to_all | solution.py:246
  133.3 0.0 copy-start.1
  133.3 0.0 copy-start
  133.4 0.0 copy-done.3
  133.4 0.6 dynamic-slice
  134.6 0.2 dynamic-update-slice
  134.9 100.4 %all-reduce.req_ref = s32[128]{0:T(128)} all-reduce(s32[128]{0:T(128)S(1)} %dynamic-update-slice), channel_id=2, replica_groups=mesh['fact'=8,'dim'=16] {'fact'}, use_global_device_ids=true, to_apply=%add | all-reduce | flops 128 | bytes 1024 | tf_op jit(solution)/shard_map/all_gather | solution.py:250
  235.3 4.0 %all-to-all-done.1.piece_ref = bf16[128,128,256]{2,1,0:T(8,128)(2,1)} async-done(((bf16[128,128,256]{2,1,0:T(8,128)(2,1)}), bf16[128,128,256]{2,1,0:T(8,128)(2,1)}, u32[]{:S(2)}, u32[]{:S(2)}) %all-to-all-start.1) | async-done | bytes 8388640 | tf_op jit(solution)/shard_map/all_to_all | solution.py:246
  239.3 6.4 %shard_map.94 = (bf16[1024,128]{1,0:T(8,128)(2,1)}, bf16[1024,128]{1,0:T(8,128)(2,1)}) custom-call(s32[128]{0:T(128)} %all-reduce.req_ref, bf16[128,128,256]{2,1,0:T(8,128)(2,1)} %all-to-all-done.1.piece_ref), custom_call_target="tpu_custom_call" | custom-call | tf_op jit(solution)/shard_map/pallas_call | solution.py:203
  245.7 0.0 copy-done.1
  245.7 0.8 copy.16
  246.5 0.0 copy-done
  246.5 0.8 copy.17
  (1 shorter events, 0.0 us)
Async XLA Ops:
  2.1 16.0 %copy-start.2 = (s32[2,8]{1,0:T(2,128)}, s32[2,8]{1,0:T(2,128)S(1)}, u32[]{:S(2)}) copy-start(s32[2,8]{1,0:T(2,128)S(1)} %get-tuple-element.19.owner_ref) | copy-start | bytes 196
  124.4 9.0 %copy-start.3 = (u32[128]{0:T(128)S(1)}, u32[128]{0:T(128)}, u32[]{:S(2)}) copy-start(u32[128]{0:T(128)} %constant.41) | copy-start | bytes 1540
  124.4 114.9 %all-to-all-start.1 = ((bf16[128,128,256]{2,1,0:T(8,128)(2,1)}), bf16[128,128,256]{2,1,0:T(8,128)(2,1)}, u32[]{:S(2)}, u32[]{:S(2)}) async-start(bf16[128,128,256]{2,1,0:T(8,128)(2,1)} %bitcast.5), calls=%async_computation.1 | async-start | bytes 16777216 | tf_op jit(solution)/shard_map/all_to_all | solution.py:246
  133.3 112.4 %copy-start.1 = (bf16[256,1024]{1,0:T(8,128)(2,1)S(1)}, bf16[256,1024]{1,0:T(8,128)(2,1)}, u32[]{:S(2)}) copy-start(bf16[256,1024]{1,0:T(8,128)(2,1)} %get-tuple-element.24) | copy-start | bytes 1572868
  133.3 113.2 %copy-start = (bf16[256,1024]{1,0:T(8,128)(2,1)S(1)}, bf16[256,1024]{1,0:T(8,128)(2,1)}, u32[]{:S(2)}) copy-start(bf16[256,1024]{1,0:T(8,128)(2,1)} %get-tuple-element.25) | copy-start | bytes 1572868

commit v13 on v12

--- a/solution.py
+++ b/solution.py
@@ -189,7 +189,7 @@
 def sum_pieces(all_requests, pieces, blocks):
     sources, rows, both = pieces.shape
     span = both // 2
-    chunk = 32
+    chunk = 64
     grid_spec = pltpu.PrefetchScalarGridSpec(
         num_scalar_prefetch=1,
         grid=(sources // chunk,),

time: 248 us -> 247 us (level)
  no operation moved by 1% of the time
where the time goes in v13:
time: 247 us
  blocking collectives  114 us (46%)
  Pallas kernels  112 us (45%)
  starting transfers between devices  8.92 us (4%)
  waiting for transfers between devices  4.04 us (2%)
  other arithmetic  3.26 us (1%)
  local copies, waits for them, and re-layouts  2.52 us (1%)
    pallas_call x1, Pallas kernels, fetch_attend(): pl.pallas_call(fetch_attend_kernel, grid_spec=grid_spec, out_shape=[jax.S...  106 us
    all_gather x1, blocking collectives, body(): all_requests = lax.all_gather(requests.reshape(owners), 'fact', tiled=True)  100 us
    all_to_all x1, blocking collectives, body(): lax.all_to_all(wanted.reshape(owners, 1), 'dim', split_axis=0, concat_axi...  14 us
    all_to_all x1, starting transfers between devices, body(): lax.all_to_all(partial_grads.reshape(fact_count * owners, TILE, 2 * span)...  8.92 us
    pallas_call x1, Pallas kernels, sum_pieces(): pl.pallas_call(sum_kernel, grid_spec=grid_spec, out_shape=[jax.ShapeDtype...  5.84 us
  transfers between devices with their start and end apart: 1, of which 1 were waited for; matrix products, arithmetic and copies ran while one was open for 0% of the time, Pallas kernels for 0%

profile of v13, /device:TPU:32, one launch (start us, length us, event | category | flops | bytes accessed | tf_op | source)
XLA Modules:
  0.0 246.8 jit_solution(7616714819269860996)
XLA Ops:
  0.6 0.7 iota_compare_fusion.1
  1.4 0.7 and_select_fusion
  2.1 0.0 copy-start.2
  2.1 0.7 select_reduce_fusion
  2.7 0.1 copy.12
  2.8 14.0 %all_to_all.14 = s32[16,1,1]{2,1,0:T(1,128)S(1)} all-to-all(s32[16,1,1]{2,1,0:T(1,128)S(1)} %copy.12), channel_id=1, replica_groups=mesh['fact'=8,'dim'=16] {'dim'}, dimensions={0} | all-to-all | bytes 128 | tf_op jit(solution)/shard_map/all_to_all | solution.py:226
  16.8 1.2 fusion.2
  18.0 0.0 copy-done.2
  18.0 106.4 %shard_map.93 = (bf16[256,1024]{1,0:T(8,128)(2,1)}, bf16[256,1024]{1,0:T(8,128)(2,1)}, bf16[8,16,128,256]{3,2,1,0:T(8,128)(2,1)}) custom-call(s32[16]{0:T(128)} %get-tuple-element.15.pick_ref, s32[2,8]{1,0:T(2,128)} %copy-done.2, s32[2]{0:T(128)} %length_ref.1, s32[2,16]{1,0:T(2,128)} %get-tuple-element.16.slot_ref, bf16[8,128,1024]{2,1,0:T(8,128)(2,1)} %bitcast.6, ...), custom_call_target="tpu_custom_call" | custom-call | tf_op jit(solution)/shard_map/pallas_call | solution.py:152
  124.4 0.0 copy-start.3
  124.4 8.9 %all-to-all-start.1 = ((bf16[128,128,256]{2,1,0:T(8,128)(2,1)}), bf16[128,128,256]{2,1,0:T(8,128)(2,1)}, u32[]{:S(2)}, u32[]{:S(2)}) async-start(bf16[128,128,256]{2,1,0:T(8,128)(2,1)} %bitcast.5), calls=%async_computation.1 | async-start | bytes 16777216 | tf_op jit(solution)/shard_map/all_to_all | solution.py:246
  133.3 0.0 copy-start.1
  133.3 0.0 copy-start
  133.4 0.0 copy-done.3
  133.4 0.6 dynamic-slice
  134.6 0.2 dynamic-update-slice
  134.9 100.4 %all-reduce.req_ref = s32[128]{0:T(128)} all-reduce(s32[128]{0:T(128)S(1)} %dynamic-update-slice), channel_id=2, replica_groups=mesh['fact'=8,'dim'=16] {'fact'}, use_global_device_ids=true, to_apply=%add | all-reduce | flops 128 | bytes 1024 | tf_op jit(solution)/shard_map/all_gather | solution.py:250
  235.3 4.0 %all-to-all-done.1.piece_ref = bf16[128,128,256]{2,1,0:T(8,128)(2,1)} async-done(((bf16[128,128,256]{2,1,0:T(8,128)(2,1)}), bf16[128,128,256]{2,1,0:T(8,128)(2,1)}, u32[]{:S(2)}, u32[]{:S(2)}) %all-to-all-start.1) | async-done | bytes 8388640 | tf_op jit(solution)/shard_map/all_to_all | solution.py:246
  239.3 5.8 %shard_map.94 = (bf16[1024,128]{1,0:T(8,128)(2,1)}, bf16[1024,128]{1,0:T(8,128)(2,1)}) custom-call(s32[128]{0:T(128)} %all-reduce.req_ref, bf16[128,128,256]{2,1,0:T(8,128)(2,1)} %all-to-all-done.1.piece_ref), custom_call_target="tpu_custom_call" | custom-call | tf_op jit(solution)/shard_map/pallas_call | solution.py:203
  245.2 0.0 copy-done.1
  245.2 0.8 copy.16
  246.0 0.0 copy-done
  246.0 0.8 copy.17
  (1 shorter events, 0.0 us)
Async XLA Ops:
  2.1 16.0 %copy-start.2 = (s32[2,8]{1,0:T(2,128)}, s32[2,8]{1,0:T(2,128)S(1)}, u32[]{:S(2)}) copy-start(s32[2,8]{1,0:T(2,128)S(1)} %get-tuple-element.19.owner_ref) | copy-start | bytes 196
  124.4 9.0 %copy-start.3 = (u32[128]{0:T(128)S(1)}, u32[128]{0:T(128)}, u32[]{:S(2)}) copy-start(u32[128]{0:T(128)} %constant.41) | copy-start | bytes 1540
  124.4 114.9 %all-to-all-start.1 = ((bf16[128,128,256]{2,1,0:T(8,128)(2,1)}), bf16[128,128,256]{2,1,0:T(8,128)(2,1)}, u32[]{:S(2)}, u32[]{:S(2)}) async-start(bf16[128,128,256]{2,1,0:T(8,128)(2,1)} %bitcast.5), calls=%async_computation.1 | async-start | bytes 16777216 | tf_op jit(solution)/shard_map/all_to_all | solution.py:246
  133.3 111.8 %copy-start.1 = (bf16[256,1024]{1,0:T(8,128)(2,1)S(1)}, bf16[256,1024]{1,0:T(8,128)(2,1)}, u32[]{:S(2)}) copy-start(bf16[256,1024]{1,0:T(8,128)(2,1)} %get-tuple-element.24) | copy-start | bytes 1572868
  133.3 112.6 %copy-start = (bf16[256,1024]{1,0:T(8,128)(2,1)S(1)}, bf16[256,1024]{1,0:T(8,128)(2,1)}, u32[]{:S(2)}) copy-start(bf16[256,1024]{1,0:T(8,128)(2,1)} %get-tuple-element.25) | copy-start | bytes 1572868
